TPU v7x, 32 devices: a whole 2x2x4 slice. The times are simulated.
32 devices in a mesh: seq: 8 (over y, x, core), dp: 4 (over z).
Axes of the slice: x: 2, y: 2, z: 4, core: 2. Of those that a mesh axis runs over, the one named last changes fastest.
Arguments:
- history: bfloat16 [9, 1024, 4096], P(None, 'seq', 'dp'), may hold values from -6 to 6
- cotangent: bfloat16 [1024, 4096], P('seq', 'dp'), may hold values from -6 to 6
- bucket_len: int32 [4, 8, 2], P('dp', 'seq'), may hold values from 32 to 96, as said below
- valid_len: int32 [4, 8, 2], P('dp', 'seq'), may hold values from 1 to 96, as said below
- gen_gain: float32 [1024], replicated, may hold values from 0.25 to 1.75
- gen_in: bfloat16 [1024, 40], replicated, may hold values from -0.1875 to 0.1875
- gen_out: float32 [40, 4, 9], replicated, may hold values from -1 to 1
- gen_bias: float32 [4, 9], replicated, may hold values from -3 to 3
- norm_gain: float32 [2, 1024], replicated, may hold values from 0.25 to 1.75
- norm_bias: float32 [2, 1024], replicated, may hold values from -2 to 2
- w_in: bfloat16 [1024, 7, 1024], P('seq'), may hold values from -0.1875 to 0.1875
- in_bias: float32 [7, 1024], replicated, may hold values from -2 to 2
- w_out: bfloat16 [1024, 1024], P('seq'), may hold values from -0.75 to 0.75
- w_down: bfloat16 [1024, 4096], P('seq'), may hold values from -0.09375 to 0.09375
- out_bias: float32 [1024], replicated, may hold values from -2 to 2
Outputs:
- new_state: bfloat16 [1024, 4096], P('seq', 'dp')
- history_grad: bfloat16 [9, 1024, 4096], P(None, 'seq', 'dp')
- mix_mean: float32 [4, 9], replicated
- mix_var: float32 [4, 9], replicated
- gen_gain_grad: float32 [1024], replicated
- gen_in_grad: float32 [1024, 40], replicated
- gen_out_grad: float32 [40, 4, 9], replicated
- gen_bias_grad: float32 [4, 9], replicated
- norm_gain_grad: float32 [2, 1024], replicated
- norm_bias_grad: float32 [2, 1024], replicated
- w_in_grad: float32 [1024, 7, 1024], P('seq')
- in_bias_grad: float32 [7, 1024], replicated
- w_out_grad: float32 [1024, 1024], P('seq')
- w_down_grad: float32 [1024, 4096], P('seq')
- out_bias_grad: float32 [1024], replicated
Inputs may be any that keep to these rules, and one draw needn't show every extreme that they name: `bucket_len`: the two buckets of one token block together hold 128 tokens. Each bucket's valid tokens are its first valid_len tokens, at least one and at most the bucket's length.
All inputs are finite; a program needn't handle non-finite values.
Results may differ from a plain program's by a relative error of at most 0.015.
Values may be sent and summed in bfloat16 or wider, within the bound.
A program may use at most 256 MiB of HBM per device.

v0:
```python
import math

import jax
import jax.numpy as jnp
from jax import lax
from jax.sharding import PartitionSpec as P

HEADS = 16
HEAD_DIM = 64
ROT = 16


ln_eps = 1e-05
rms_eps = 1e-06
masked_score = -1e30
highest = lax.Precision.HIGHEST


def gelu_exact(values):
    return jax.nn.gelu(values, approximate=False)


def rotary_tables(position):
    freq_index = jnp.arange(ROT // 2, dtype=jnp.float32)
    inverse_freq = jnp.exp(freq_index * (-2.0 * math.log(10000.0) / ROT))
    angles = position.astype(jnp.float32)[:, None] * inverse_freq[None, :]
    return (jnp.cos(angles), jnp.sin(angles))


def rotate(values, cosine, sine):
    half = ROT // 2
    former = values[..., :half]
    latter = values[..., half:ROT]
    cos_heads = cosine[:, None, :]
    sin_heads = sine[:, None, :]
    return jnp.concatenate(
        [
            former * cos_heads - latter * sin_heads,
            latter * cos_heads + former * sin_heads,
            values[..., ROT:],
        ],
        axis=-1,
    )


def token_layout(lengths, counts, tokens):
    index = jnp.arange(tokens, dtype=jnp.int32)
    second = index >= lengths[0]
    position = index - jnp.where(second, lengths[0], 0)
    valid = position < jnp.where(second, counts[1], counts[0])
    return (second, position, valid)


def normalize(streams):
    centre = jnp.mean(streams, axis=-1, keepdims=True)
    centred = streams - centre
    inverse = lax.rsqrt(jnp.mean(centred * centred, axis=-1, keepdims=True) + ln_eps)
    return (centred * inverse, inverse)


def normalize_back(grad_scaled, scaled, inverse):
    mean_grad = jnp.mean(grad_scaled, axis=-1, keepdims=True)
    mean_along = jnp.mean(grad_scaled * scaled, axis=-1, keepdims=True)
    return inverse * (grad_scaled - mean_grad - scaled * mean_along)


def per_device(
    history,
    cotangent,
    bucket_len,
    valid_len,
    gen_gain,
    gen_in,
    gen_out,
    gen_bias,
    norm_gain,
    norm_bias,
    w_in,
    in_bias,
    w_out,
    w_down,
    out_bias,
):
    states = history.shape[0]
    stacked = jnp.concatenate([history, cotangent[None]], axis=0)
    arrived = lax.all_to_all(stacked, "seq", split_axis=2, concat_axis=1, tiled=True)
    arrived_rows = jnp.swapaxes(arrived, 1, 2)
    hist_local = arrived_rows[:states]
    cot_local = arrived_rows[states]
    tokens = hist_local.shape[1]
    width = hist_local.shape[2]
    second, position, valid = token_layout(bucket_len.reshape(2), valid_len.reshape(2), tokens)
    valid_float = valid.astype(jnp.float32)
    last = hist_local[states - 1].astype(jnp.float32)
    rms = lax.rsqrt(jnp.mean(last * last, axis=-1, keepdims=True) + rms_eps)
    gen_normed = (last * rms * gen_gain).astype(jnp.bfloat16)
    gen_pre = jnp.dot(gen_normed, gen_in, preferred_element_type=jnp.float32)
    gen_hidden, gen_pull = jax.vjp(gelu_exact, gen_pre)
    mixing = jnp.einsum("th,hsj->tsj", gen_hidden, gen_out, precision=highest) + gen_bias
    weighted = mixing * valid_float[:, None, None]
    stat_sums = jnp.sum(weighted, axis=0)
    stat_squares = jnp.sum(weighted * mixing, axis=0)
    stat_count = jnp.sum(valid_float)
    streams = mixing[:, :, 0].T[:, :, None] * hist_local[0]
    for state in range(1, states):
        streams = streams + mixing[:, :, state].T[:, :, None] * hist_local[state]
    scaled, inverse = normalize(streams)
    normed_attn = (scaled[:3] * norm_gain[0] + norm_bias[0]).astype(jnp.bfloat16)
    normed_mlp = (scaled[3] * norm_gain[1] + norm_bias[1]).astype(jnp.bfloat16)
    piece = lax.all_gather(w_in, "seq", axis=0, tiled=True)
    attn_part = jnp.einsum(
        "stk,nsk->stn", normed_attn, piece[:, :3], preferred_element_type=jnp.float32
    )
    mlp_part = jnp.einsum(
        "tk,njk->jtn", normed_mlp, piece[:, 3:], preferred_element_type=jnp.float32
    )
    projected = jnp.concatenate([attn_part, mlp_part], axis=0) + in_bias[:, None, :]
    cosine, sine = rotary_tables(position)
    heads_shape = (tokens, HEADS, HEAD_DIM)
    queries = (rotate(projected[0].reshape(heads_shape), cosine, sine) * HEAD_DIM ** (-0.5)).astype(
        jnp.bfloat16
    )
    keys = rotate(projected[1].reshape(heads_shape), cosine, sine).astype(jnp.bfloat16)
    values = projected[2].reshape(heads_shape).astype(jnp.bfloat16)
    index = jnp.arange(tokens, dtype=jnp.int32)
    allowed = (
        (second[:, None] == second[None, :]) & (index[None, :] <= index[:, None]) & valid[None, :]
    )
    scores = jnp.einsum("qhd,khd->hqk", queries, keys, preferred_element_type=jnp.float32)
    scores = jnp.where(allowed[None], scores, masked_score)
    top = jnp.max(scores, axis=-1, keepdims=True)
    weights = jnp.exp(scores - top)
    weight_total = jnp.sum(weights, axis=-1, keepdims=True)
    log_total = top + jnp.log(weight_total)
    probs_low = (weights / weight_total).astype(jnp.bfloat16)
    attended = jnp.einsum("hqk,khd->qhd", probs_low, values, preferred_element_type=jnp.float32)
    attn_low = attended.reshape(tokens, width).astype(jnp.bfloat16)
    gelu_up, up_pull = jax.vjp(gelu_exact, projected[3:])
    gelu_low = gelu_up.astype(jnp.bfloat16)
    grad_out_low = jnp.where(valid[:, None], cot_local, jnp.zeros_like(cot_local))
    piece_out, piece_down = lax.all_gather((w_out, w_down), "seq", axis=0, tiled=True)
    down_part = piece_down.reshape(piece_down.shape[0], 4, width)
    result = jnp.einsum("tk,nk->tn", attn_low, piece_out, preferred_element_type=jnp.float32)
    branch = result + jnp.einsum(
        "jtk,njk->tn", gelu_low, down_part, preferred_element_type=jnp.float32
    )
    new_local = (streams[3] + branch + out_bias).astype(jnp.bfloat16)
    piece_out = lax.all_gather(w_out, "seq", axis=0, tiled=True)
    piece_down = lax.all_gather(w_down, "seq", axis=0, tiled=True)
    count = piece_out.shape[0]
    part = grad_out_low
    attn_add = jnp.einsum("tn,nk->tk", part, piece_out, preferred_element_type=jnp.float32)
    gelu_add = jnp.einsum(
        "tn,njk->jtk", part, piece_down.reshape(count, 4, width), preferred_element_type=jnp.float32
    )
    grad_attn = attn_add
    part = grad_out_low
    term_out = jnp.einsum("tn,tk->nk", part, attn_low, preferred_element_type=jnp.float32)
    term_down = jnp.einsum(
        "tn,jtk->njk", part, gelu_low, preferred_element_type=jnp.float32
    ).reshape(lax.axis_size("seq") * w_out.shape[0], 4 * width)
    out_grads = lax.psum_scatter(
        jnp.concatenate([term_out, term_down], axis=1).astype(jnp.bfloat16),
        "seq",
        scatter_dimension=0,
        tiled=True,
    )
    out_bias_grad = jnp.sum(grad_out_low.astype(jnp.float32), axis=0)
    grad_attended = grad_attn.astype(jnp.bfloat16).reshape(heads_shape)
    rescored = jnp.einsum("qhd,khd->hqk", queries, keys, preferred_element_type=jnp.float32)
    probs = jnp.where(allowed[None], jnp.exp(rescored - log_total), 0.0)
    grad_values = jnp.einsum(
        "hqk,qhd->khd",
        probs.astype(jnp.bfloat16),
        grad_attended,
        preferred_element_type=jnp.float32,
    )
    grad_probs = jnp.einsum(
        "qhd,khd->hqk", grad_attended, values, preferred_element_type=jnp.float32
    )
    grad_scores = (
        probs * (grad_probs - jnp.sum(probs * grad_probs, axis=-1, keepdims=True))
    ).astype(jnp.bfloat16)
    grad_queries = jnp.einsum(
        "hqk,khd->qhd", grad_scores, keys, preferred_element_type=jnp.float32
    ) * HEAD_DIM ** (-0.5)
    grad_keys = jnp.einsum("hqk,qhd->khd", grad_scores, queries, preferred_element_type=jnp.float32)
    grad_up = up_pull(gelu_add)[0]
    grad_proj = jnp.concatenate(
        [
            rotate(grad_queries, cosine, -sine).reshape(1, tokens, width),
            rotate(grad_keys, cosine, -sine).reshape(1, tokens, width),
            grad_values.reshape(1, tokens, width),
            grad_up,
        ],
        axis=0,
    )
    in_bias_grad = jnp.sum(grad_proj, axis=1)
    grad_proj_low = grad_proj.astype(jnp.bfloat16)
    piece = lax.all_gather(w_in, "seq", axis=0, tiled=True)
    part = grad_proj_low
    attn_add = jnp.einsum(
        "stn,nsk->stk", part[:3], piece[:, :3], preferred_element_type=jnp.float32
    )
    mlp_add = jnp.einsum("jtn,njk->tk", part[3:], piece[:, 3:], preferred_element_type=jnp.float32)
    part = grad_proj_low
    attn_term = jnp.einsum(
        "stn,stk->nsk", part[:3], normed_attn, preferred_element_type=jnp.float32
    )
    mlp_term = jnp.einsum("jtn,tk->njk", part[3:], normed_mlp, preferred_element_type=jnp.float32)
    in_grads = lax.psum_scatter(
        jnp.concatenate([attn_term, mlp_term], axis=1).astype(jnp.bfloat16),
        "seq",
        scatter_dimension=0,
        tiled=True,
    )
    norm_gain_grad = jnp.stack(
        [jnp.sum(attn_add * scaled[:3], axis=(0, 1)), jnp.sum(mlp_add * scaled[3], axis=0)]
    )
    norm_bias_grad = jnp.stack([jnp.sum(attn_add, axis=(0, 1)), jnp.sum(mlp_add, axis=0)])
    grad_attn_streams = normalize_back(attn_add * norm_gain[0], scaled[:3], inverse[:3])
    grad_mlp_stream = normalize_back(
        mlp_add * norm_gain[1], scaled[3], inverse[3]
    ) + grad_out_low.astype(jnp.float32)
    grad_streams = jnp.concatenate([grad_attn_streams, grad_mlp_stream[None]], axis=0)
    grad_mixing = jnp.stack(
        [
            jnp.einsum(
                "std,td->ts", grad_streams, hist_local[state].astype(jnp.float32), precision=highest
            )
            for state in range(states)
        ],
        axis=-1,
    )
    hist_terms = [
        jnp.einsum("ts,std->td", mixing[:, :, state], grad_streams, precision=highest)
        for state in range(states)
    ]
    gen_bias_grad = jnp.sum(grad_mixing, axis=0)
    gen_out_grad = jnp.einsum("th,tsj->hsj", gen_hidden, grad_mixing, precision=highest)
    grad_hidden = jnp.einsum("tsj,hsj->th", grad_mixing, gen_out, precision=highest)
    grad_pre_low = gen_pull(grad_hidden)[0].astype(jnp.bfloat16)
    gen_in_grad = jnp.einsum(
        "tk,th->kh", gen_normed, grad_pre_low, preferred_element_type=jnp.float32
    )
    grad_gen = jnp.einsum("th,kh->tk", grad_pre_low, gen_in, preferred_element_type=jnp.float32)
    gen_gain_grad = jnp.sum(grad_gen * last * rms, axis=0)
    gained = grad_gen * gen_gain
    grad_last = rms * gained - last * (rms * rms * rms) * jnp.mean(
        gained * last, axis=-1, keepdims=True
    )
    hist_stack = jnp.stack(hist_terms[: states - 1] + [hist_terms[states - 1] + grad_last]).astype(
        jnp.bfloat16
    )
    departing = jnp.swapaxes(jnp.concatenate([new_local[None], hist_stack], axis=0), 1, 2)
    returned = lax.all_to_all(departing, "seq", split_axis=1, concat_axis=2, tiled=True)
    w_in_grad, out_total = (
        lax.psum(in_grads, "dp").astype(jnp.float32),
        lax.psum(out_grads, "dp").astype(jnp.float32),
    )
    w_out_grad = out_total[:, :width]
    w_down_grad = out_total[:, width:]
    joined = lax.psum(
        (
            gen_gain_grad,
            gen_in_grad,
            gen_out_grad,
            gen_bias_grad,
            norm_gain_grad,
            norm_bias_grad,
            in_bias_grad,
            out_bias_grad,
            stat_sums,
            stat_squares,
            stat_count,
        ),
        ("seq", "dp"),
    )
    small_totals = joined[:8]
    stat_totals = joined[8:]
    mix_mean = stat_totals[0] / stat_totals[2]
    mix_var = stat_totals[1] / stat_totals[2] - mix_mean * mix_mean
    return (
        returned[0],
        returned[1:],
        mix_mean,
        mix_var,
        small_totals[0],
        small_totals[1],
        small_totals[2],
        small_totals[3],
        small_totals[4],
        small_totals[5],
        w_in_grad,
        small_totals[6],
        w_out_grad,
        w_down_grad,
        small_totals[7],
    )


def solution(mesh):
    in_specs = (
        P(None, "seq", "dp"),
        P("seq", "dp"),
        P("dp", "seq", None),
        P("dp", "seq", None),
        P(),
        P(),
        P(),
        P(),
        P(),
        P(),
        P("seq", None, None),
        P(),
        P("seq", None),
        P("seq", None),
        P(),
    )
    out_specs = (
        P("seq", "dp"),
        P(None, "seq", "dp"),
        P(),
        P(),
        P(),
        P(),
        P(),
        P(),
        P(),
        P(),
        P("seq", None, None),
        P(),
        P("seq", None),
        P("seq", None),
        P(),
    )
    return jax.shard_map(
        per_device, mesh=mesh, in_specs=in_specs, out_specs=out_specs, check_vma=False
    )
```

profile of v0, /device:TPU:0, one launch (start us, length us, event | category | flops | bytes accessed | tf_op | source)
XLA Modules:
  0.0 703.6 jit_solution(17909491425658481265)
XLA Ops:
  11.4 7.4 %copy.110 = bf16[9,128,1024]{1,0,2:T(8,128)(2,1)} copy(bf16[9,128,1024]{2,1,0:T(8,128)(2,1)S(1)} %copy-done.17) | data formatting | bytes 4718592 | tf_op args[0]
  18.8 6.1 pad_maximum_fusion.2
  25.0 5.3 all-to-all-start
  33.8 65.4 %all-to-all-done = bf16[10,128,1024]{1,0,2:T(8,128)(2,1)} async-done(((bf16[10,128,1024]{1,0,2:T(8,128)(2,1)}), bf16[10,128,1024]{1,0,2:T(8,128)(2,1)}, u32[]{:S(2)}, u32[]{:S(2)}) %all-to-all-start) | async-done | bytes 2621472 | tf_op jit(solution)/shard_map/all_to_all | solution.py:86
  99.1 5.4 copy.298
  119.4 33.5 %all-gather.4.cloned.1.call-done = bf16[1024,7,1024]{2,0,1:T(8,128)(2,1)} async-done(((bf16[128,7,1024]{2,0,1:T(8,128)(2,1)}), bf16[1024,7,1024]{2,0,1:T(8,128)(2,1)}) %all-gather.4.cloned.1.call-update) | async-done | bytes 14680080 | tf_op jit(solution)/shard_map/all_gather | solution.py:110
  152.9 5.0 fusion.6
  157.9 6.3 fusion.22
  186.5 7.3 %multiply_convert_fusion = (bf16[4,128,1024]{2,1,0:T(8,128)(2,1)}, f32[4,128,1024]{2,1,0:T(8,128)}) fusion(f32[7,128,1024]{2,1,0:T(8,128)} %copy-done.3), kind=kLoop, calls=%fused_computation.30 | loop fusion | flops 34078720 | bytes 5242880 | tf_op jit(solution)/shard_map/convert_element_type | solution.py:139
  193.8 16.9 %all-gather.8.cloned.1.call-done = bf16[1024,4096]{0,1:T(8,128)(2,1)} async-done(((bf16[128,4096]{0,1:T(8,128)(2,1)}), bf16[1024,4096]{0,1:T(8,128)(2,1)}) %all-gather.8.cloned.1.call-update) | async-done | bytes 8388624 | tf_op jit(solution)/shard_map/all_gather | solution.py:141
  210.7 8.0 %fusion.15 = f32[4,128,1024]{2,1,0:T(8,128)S(1)} fusion(f32[4,128,1024]{2,1,0:T(8,128)} %get-tuple-element.106, f32[7,128,1024]{2,1,0:T(8,128)} %copy-done.3, bf16[1024,4,1024]{0,2,1:T(8,128)(2,1)} %bitcast.374, pred[128]{0:T(512)(128)(4,1)S(1)} %copy-done.57, bf16[10,128,1024]{2,1,0:T(8,128)(2,1)} %bitcast.365), kind=kOutput, calls=%fused_computation.28 | convolution fusion | flops 1080688640 | bytes 14942336 | tf_op jit(solution)/shard_map/tn,njk->jtk/dot_general | solution.py:153
  224.9 8.3 %pad_maximum_fusion = bf16[1024,7,1024]{0,2,1:T(8,128)(2,1)} fusion(bf16[1024,4,1024]{0,2,1:T(8,128)(2,1)S(1)} %convert_bitcast_fusion, bf16[1024,3,1024]{0,2,1:T(8,128)(2,1)S(1)} %convert_bitcast_fusion.1), kind=kLoop, calls=%fused_computation | loop fusion | flops 7340032 | bytes 29360128 | tf_op jit(solution)/shard_map/concatenate | solution.py:212
  233.2 18.5 %copy.186 = bf16[1024,7168]{1,0:T(8,128)(2,1)} copy(bf16[1024,7168]{0,1:T(8,128)(2,1)} %bitcast.360) | data formatting | bytes 29360128
  266.1 5.9 pad_maximum_fusion.1
  279.3 5.9 multiply_reduce_fusion.5
  285.2 5.0 multiply_reduce_fusion.1
  292.7 4.8 fusion.68
  297.5 4.8 fusion.66
  302.4 5.0 fusion.64
  307.5 4.8 fusion.62
  312.9 4.8 fusion.60
  318.4 5.2 fusion.58
  324.2 4.8 fusion.56
  329.7 4.8 fusion.54
  335.1 5.6 fusion.52
  344.7 5.2 fusion.154
  350.0 4.9 convolution_bitcast_fusion.1
  389.7 52.1 %reduce-scatter.5.cloned.1.call-done = bf16[128,5120]{1,0:T(8,128)(2,1)} async-done(((bf16[1024,5120]{1,0:T(8,128)(2,1)}), bf16[128,5120]{1,0:T(8,128)(2,1)}) %reduce-scatter.5.cloned.1.call-update) | async-done | bytes 1310736 | tf_op jit(solution)/shard_map/reduce_scatter | solution.py:162
  458.8 6.8 copy.129
  465.7 4.8 all-to-all-start.1
  474.3 82.3 %all-reduce = (f32[4,9]{1,0:T(4,128)S(1)}, f32[]{:T(128)}, f32[4,9]{1,0:T(4,128)S(1)}, f32[1024]{0:T(1024)}, f32[40,4,9]{0,2,1:T(8,128)S(1)}, /*index=5*/f32[4,9...) all-reduce(f32[4,9]{1,0:T(4,128)S(1)} %copy-done.85, ...), channel_id=1, replica_groups=mesh['seq'=8,'dp'=4] {'seq','dp'}, use_global_device_ids=true, to_apply=%region_12.13 | all-reduce | flops 14861 | bytes 118888 | tf_op jit(solution)/shard_map/psum | solution.py:263
  577.2 117.6 %all-reduce.5.cloned.1.call-done = f32[1024,40]{0,1:T(8,128)} async-done(((f32[1024,40]{0,1:T(8,128)}), f32[1024,40]{0,1:T(8,128)}) %all-reduce.5.cloned.1.call-update) | async-done | bytes 163856 | tf_op jit(solution)/shard_map/psum | solution.py:263
  (345 shorter events, 159.7 us)
Async XLA Ops:
  7.2 102.8 %copy-start = (bf16[1024,40]{0,1:T(8,128)(2,1)S(1)}, bf16[1024,40]{0,1:T(8,128)(2,1)}, u32[]{:S(2)}) copy-start(bf16[1024,40]{0,1:T(8,128)(2,1)} %param.20) | copy-start | bytes 245764
  7.2 109.8 %all-gather.6.cloned.1.call-start = ((), (), s32[]{:S(2)}) async-start(), calls=%async_computation.5 | async-start | bytes 2359296 | tf_op jit(solution)/shard_map/all_gather | solution.py:141
  7.9 144.9 %all-gather.4.cloned.1.call-start = ((), (), s32[]{:S(2)}) async-start(), calls=%async_computation.4 | async-start | bytes 16515072 | tf_op jit(solution)/shard_map/all_gather | solution.py:110
  8.7 202.0 %all-gather.8.cloned.1.call-start = ((), (), s32[]{:S(2)}) async-start(), calls=%async_computation.6 | async-start | bytes 9437184 | tf_op jit(solution)/shard_map/all_gather | solution.py:141
  25.0 8.7 %copy-start.86 = (f32[2,1024]{1,0:T(2,128)S(1)}, f32[2,1024]{1,0:T(2,128)}, u32[]{:S(2)}) copy-start(f32[2,1024]{1,0:T(2,128)} %param.24) | copy-start | bytes 24580
  25.0 8.7 %copy-start.87 = (f32[2,1024]{1,0:T(2,128)S(1)}, f32[2,1024]{1,0:T(2,128)}, u32[]{:S(2)}) copy-start(f32[2,1024]{1,0:T(2,128)} %param.23) | copy-start | bytes 24580
  25.0 74.2 %all-to-all-start = ((bf16[10,128,1024]{1,0,2:T(8,128)(2,1)}), bf16[10,128,1024]{1,0,2:T(8,128)(2,1)}, u32[]{:S(2)}, u32[]{:S(2)}) async-start(bf16[10,128,1024]{1,0,2:T(8,128)(2,1)} %pad_maximum_fusion.2), calls=%async_computation | async-start | bytes 8388608 | tf_op jit(solution)/shard_map/all_to_all | solution.py:86
  30.2 355.6 %reduce-scatter.7.cloned.1.call-start = ((), (), s32[]{:S(2)}) async-start(), calls=%async_computation.9 | async-start | bytes 16515072
  32.8 84.2 %copy-start.56 = (pred[128]{0:T(512)(128)(4,1)}, pred[128]{0:T(512)(128)(4,1)S(1)}, u32[]{:S(2)}) copy-start(pred[128]{0:T(512)(128)(4,1)S(1)} %get-tuple-element.104) | copy-start | bytes 388
  33.6 119.2 %copy-start.78 = (f32[1,1024]{1,0:T(1,128)}, f32[1,1024]{1,0:T(1,128)S(1)}, u32[]{:S(2)}) copy-start(f32[1,1024]{1,0:T(1,128)S(1)} %get-tuple-element.152) | copy-start | bytes 12292
  33.7 124.2 %copy-start.82 = (f32[1,1024]{1,0:T(1,128)}, f32[1,1024]{1,0:T(1,128)S(1)}, u32[]{:S(2)}) copy-start(f32[1,1024]{1,0:T(1,128)S(1)} %get-tuple-element.153) | copy-start | bytes 12292
  157.9 6.3 copy-start.53
  186.5 24.2 %copy-start.57 = (pred[128]{0:T(512)(128)(4,1)S(1)}, pred[128]{0:T(512)(128)(4,1)}, u32[]{:S(2)}) copy-start(pred[128]{0:T(512)(128)(4,1)} %copy-done.56) | copy-start | bytes 388
  210.7 9.3 %copy-start.11 = (f32[1,128,1024]{2,1,0:T(8,128)S(1)}, f32[1,128,1024]{2,1,0:T(8,128)}, u32[]{:S(2)}) copy-start(f32[1,128,1024]{2,1,0:T(8,128)} %copy.127) | copy-start | bytes 1572868
  210.7 9.3 %copy-start.13 = (f32[1,128,1024]{2,1,0:T(8,128)S(1)}, f32[1,128,1024]{2,1,0:T(8,128)}, u32[]{:S(2)}) copy-start(f32[1,128,1024]{2,1,0:T(8,128)} %copy.126) | copy-start | bytes 1572868
  210.7 9.3 %copy-start.15 = (f32[1,128,1024]{2,1,0:T(8,128)S(1)}, f32[1,128,1024]{2,1,0:T(8,128)}, u32[]{:S(2)}) copy-start(f32[1,128,1024]{2,1,0:T(8,128)} %copy.125) | copy-start | bytes 1572868
  251.7 190.1 %reduce-scatter.5.cloned.1.call-start = ((), (), s32[]{:S(2)}) async-start(), calls=%async_computation.8 | async-start | bytes 11796480 | tf_op jit(solution)/shard_map/reduce_scatter | solution.py:162
  272.0 6.5 copy-start.61
  272.0 7.3 %copy-start.59 = (f32[4,128]{1,0:T(4,128)S(1)}, f32[4,128]{1,0:T(4,128)}, u32[]{:S(2)}) copy-start(f32[4,128]{1,0:T(4,128)} %copy-done.58) | copy-start | bytes 6148
  272.1 297.5 %all-reduce.7.cloned.1.call-start = ((), (), s32[]{:S(2)}) async-start(), calls=%async_computation.10 | async-start | bytes 6291456 | tf_op jit(solution)/shard_map/psum | solution.py:258
  340.7 9.3 %copy-start.4 = (bf16[4,128,1024]{2,1,0:T(8,128)(2,1)S(1)}, bf16[4,128,1024]{2,1,0:T(8,128)(2,1)}, u32[]{:S(2)}) copy-start(bf16[4,128,1024]{2,1,0:T(8,128)(2,1)} %get-tuple-element.105) | copy-start | bytes 3145732
  373.1 6.2 copy-start.39
  389.7 52.1 %copy-start.38 = (f32[128,4,1]{1,2,0:T(1,128)S(1)}, f32[128,4,1]{1,2,0:T(1,128)}, u32[]{:S(2)}) copy-start(f32[128,4,1]{1,2,0:T(1,128)} %copy.157) | copy-start | bytes 6148
  465.6 7.0 copy-start.91
  465.6 7.0 copy-start.93
  465.6 7.0 copy-start.90
  465.6 7.0 copy-start.92
  465.6 7.0 copy-start.7
  465.6 7.0 copy-start.12
  465.7 7.0 copy-start.14
  465.7 92.8 %all-to-all-start.1 = ((bf16[10,1024,128]{2,0,1:T(8,128)(2,1)}), bf16[10,1024,128]{2,0,1:T(8,128)(2,1)}, u32[]{:S(2)}, u32[]{:S(2)}) async-start(bf16[10,1024,128]{2,0,1:T(8,128)(2,1)} %copy.129), calls=%async_computation.1 | async-start | bytes 8388608 | tf_op jit(solution)/shard_map/all_to_all | solution.py:256
  470.5 224.3 %all-reduce.5.cloned.1.call-start = ((), (), s32[]{:S(2)}) async-start(), calls=%async_computation.7 | async-start | bytes 327680 | tf_op jit(solution)/shard_map/psum | solution.py:263
  (78 other events, 257.3 us)
Sparse Core Ops, SparseCore 0:
  9.9 35.9 all-gather.5
  47.8 104.9 all-gather.3
  154.8 55.8 all-gather.7
  251.8 104.6 reduce-scatter.6
  359.8 81.9 reduce-scatter.4
  444.1 122.0 all-reduce.6
  572.3 122.4 all-reduce.4
where the time goes:
time: 712 us; the launch traced here: 704 us
  waiting for transfers between devices  287 us (40%)
  matrix products  147 us (21%)
  local copies, waits for them, and re-layouts  115 us (16%)
  blocking collectives  82.3 us (12%)
  other arithmetic  45.8 us (6%)
  between operations  15.9 us (2%)
  starting transfers between devices  10.6 us (1%)
    psum x1, waiting for transfers between devices, per_device(): lax.psum((gen_gain_grad, gen_in_grad, gen_out_grad, gen_bias_grad, norm_g...  118 us
    psum x1, blocking collectives, per_device(): lax.psum((gen_gain_grad, gen_in_grad, gen_out_grad, gen_bias_grad, norm_g...  82.3 us
    all_to_all x1, waiting for transfers between devices, per_device(): lax.all_to_all(stacked, 'seq', split_axis=2, concat_axis=1, tiled=True)  65.4 us
    reduce_scatter x1, waiting for transfers between devices, per_device(): lax.psum_scatter(jnp.concatenate([term_out, term_down], axis=1).astype(jn...  52.1 us
    unnamed x218, local copies, waits for them, and re-layouts  50.6 us
    dot_general x9, matrix products, per_device(): jnp.einsum('std,td->ts', grad_streams, hist_local[state].astype(jnp.float...  44.5 us
    dot_general x9, matrix products, per_device(): jnp.einsum('ts,std->td', mixing[:, :, state], grad_streams, precision=hig...  40.6 us
    all_gather x1, waiting for transfers between devices, per_device(): piece = lax.all_gather(w_in, 'seq', axis=0, tiled=True)  33.5 us
  transfers between devices with their start and end apart: 9, of which 5 were waited for; matrix products, arithmetic and copies ran while one was open for 36% of the time, Pallas kernels for 0%

commit v1 on v0

--- a/solution.py
+++ b/solution.py
@@ -299,6 +299,205 @@
     )
 
 
+def tp_device(
+    history, cotangent, bucket_len, valid_len, gen_gain, gen_in, gen_out, gen_bias,
+    norm_gain, norm_bias, w_in, in_bias, w_out, w_down, out_bias,
+):
+    f32, bf16 = jnp.float32, jnp.bfloat16
+    n = lax.axis_size("seq")
+    me = lax.axis_index("seq")
+    states, feats, tokens = history.shape
+    width = n * feats
+    block = tokens // n
+    heads = feats // HEAD_DIM
+
+    def local(array, axis):
+        return lax.dynamic_slice_in_dim(array, me * feats, feats, axis)
+
+    def sum_feats(part):
+        return lax.psum(part, "seq")
+
+    lens = lax.all_gather(
+        jnp.concatenate([bucket_len.reshape(2), valid_len.reshape(2)]), "seq"
+    )
+    index = jnp.arange(block, dtype=jnp.int32)[None, :]
+    second = index >= lens[:, 0:1]
+    position = index - jnp.where(second, lens[:, 0:1], 0)
+    valid = position < jnp.where(second, lens[:, 3:4], lens[:, 2:3])
+    valid_float = valid.reshape(tokens).astype(f32)
+    cot_all = lax.all_gather(cotangent, "seq", axis=0, tiled=True)
+    grad_out = jnp.where(valid.reshape(1, tokens), cot_all, jnp.zeros_like(cot_all))
+    grad_out_local = jnp.where(valid.reshape(1, tokens), cotangent, jnp.zeros_like(cotangent))
+    rows = jnp.concatenate([w_out[:, None], w_down.reshape(feats, 4, width)], axis=1)
+    cols = lax.all_to_all(
+        rows.reshape(feats, 5, n, feats), "seq", split_axis=2, concat_axis=0, tiled=True
+    ).reshape(width, 5, feats)
+    last = history[states - 1].astype(f32)
+    gain_l = local(gen_gain, 0)[:, None]
+    gen_in_l = local(gen_in, 0)
+    lg = (last * gain_l).astype(bf16)
+    part = jnp.einsum("dh,dt->ht", gen_in_l, lg, preferred_element_type=f32)
+    part = sum_feats(jnp.concatenate([part, jnp.sum(last * last, axis=0, keepdims=True)], axis=0))
+    raw, square = part[:-1], part[-1:]
+    rms = lax.rsqrt(square / width + rms_eps)
+    gen_pre = raw * rms
+    gen_hidden, gen_pull = jax.vjp(gelu_exact, gen_pre)
+    out_flat = gen_out.reshape(gen_out.shape[0], 4 * states)
+    mixing = jnp.einsum("hm,ht->mt", out_flat, gen_hidden, precision=highest) + gen_bias.reshape(-1, 1)
+    weighted = mixing * valid_float
+    stat_sums = jnp.sum(weighted, axis=1)
+    stat_squares = jnp.sum(weighted * mixing, axis=1)
+    stat_count = jnp.sum(valid_float)
+    mix = mixing.reshape(4, states, 1, tokens)
+    streams = mix[:, 0] * history[0]
+    for state in range(1, states):
+        streams = streams + mix[:, state] * history[state]
+    mean_l = jnp.mean(streams, axis=1)
+    m2_l = jnp.sum((streams - mean_l[:, None]) ** 2, axis=1)
+    both = lax.all_gather(jnp.stack([mean_l, m2_l]), "seq")
+    centre = jnp.mean(both[:, 0], axis=0)
+    m2 = jnp.sum(both[:, 1] + feats * (both[:, 0] - centre) ** 2, axis=0)
+    inverse = lax.rsqrt(m2 / width + ln_eps)[:, None]
+    scaled = (streams - centre[:, None]) * inverse
+    which = jnp.array([0, 0, 0, 1])
+    ng = local(norm_gain, 1)[which][:, :, None]
+    nb = local(norm_bias, 1)[which][:, :, None]
+    normed = lax.all_gather((scaled * ng + nb).astype(bf16), "seq", axis=1, tiled=True)
+    slot_stream = [0, 1, 2, 3, 3, 3, 3]
+    proj = jnp.stack(
+        [jnp.dot(w_in[:, s], normed[slot_stream[s]], preferred_element_type=f32) for s in range(7)]
+    ) + local(in_bias, 1)[:, :, None]
+    cosine, sine = rotary_tables(position.reshape(tokens))
+    cosine, sine = cosine.T, sine.T
+
+    def rot(value, sine):
+        value = value.reshape(heads, HEAD_DIM, tokens)
+        a, b, rest = value[:, :8], value[:, 8:16], value[:, 16:]
+        return jnp.concatenate([a * cosine - b * sine, b * cosine + a * sine, rest], axis=1)
+
+    scale = HEAD_DIM ** (-0.5)
+    shape = (heads, HEAD_DIM, n, block)
+    queries = (rot(proj[0], sine) * scale).astype(bf16).reshape(shape)
+    keys = rot(proj[1], sine).astype(bf16).reshape(shape)
+    values = proj[2].astype(bf16).reshape(shape)
+    ar = jnp.arange(block, dtype=jnp.int32)
+    allowed = (
+        (second[:, :, None] == second[:, None, :])
+        & (ar[:, None] <= ar[None, :])
+        & valid[:, :, None]
+    )
+    scores = jnp.einsum("hdbk,hdbq->hbkq", keys, queries, preferred_element_type=f32)
+    scores = jnp.where(allowed, scores, masked_score)
+    top = jnp.max(scores, axis=2, keepdims=True)
+    weights = jnp.exp(scores - top)
+    probs = jnp.where(allowed, weights / jnp.sum(weights, axis=2, keepdims=True), 0.0)
+    probs_low = probs.astype(bf16)
+    attended = jnp.einsum("hdbk,hbkq->hdbq", values, probs_low, preferred_element_type=f32)
+    attn_low = attended.astype(bf16).reshape(feats, tokens)
+    gelu_up, up_pull = jax.vjp(gelu_exact, proj[3:])
+    act = jnp.concatenate([attn_low[None], gelu_up.astype(bf16)], axis=0)
+    branch = jnp.einsum("njk,jkt->nt", cols, act, preferred_element_type=f32)
+    branch = lax.psum_scatter(branch.astype(bf16), "seq", scatter_dimension=0, tiled=True)
+    new_state = (streams[3] + branch.astype(f32) + local(out_bias, 0)[:, None]).astype(bf16)
+    back = jnp.einsum("njk,nt->jkt", cols, grad_out, preferred_element_type=f32)
+    col_grads = jnp.einsum("nt,jkt->njk", grad_out, act, preferred_element_type=f32).astype(bf16)
+    row_grads = lax.all_to_all(
+        col_grads.reshape(n, feats, 5, feats), "seq", split_axis=0, concat_axis=3, tiled=True
+    ).reshape(feats, 5 * width)
+    row_grads = lax.psum(row_grads, "dp").astype(f32)
+    grad_attn = back[0].astype(bf16).reshape(shape)
+    grad_values = jnp.einsum("hbkq,hdbq->hdbk", probs_low, grad_attn, preferred_element_type=f32)
+    dprob = jnp.einsum("hdbk,hdbq->hbkq", values, grad_attn, preferred_element_type=f32)
+    grad_scores = (probs * (dprob - jnp.sum(probs * dprob, axis=2, keepdims=True))).astype(bf16)
+    grad_queries = jnp.einsum("hdbk,hbkq->hdbq", keys, grad_scores, preferred_element_type=f32) * scale
+    grad_keys = jnp.einsum("hdbq,hbkq->hdbk", queries, grad_scores, preferred_element_type=f32)
+    flat = (feats, tokens)
+    grad_proj = jnp.concatenate(
+        [
+            rot(grad_queries.reshape(flat), -sine).reshape((1,) + flat),
+            rot(grad_keys.reshape(flat), -sine).reshape((1,) + flat),
+            grad_values.reshape((1,) + flat),
+            up_pull(back[1:])[0],
+        ],
+        axis=0,
+    )
+    in_bias_grad = jnp.sum(grad_proj, axis=2)
+    low = grad_proj.astype(bf16)
+    w_in_grad = jnp.stack(
+        [
+            jnp.einsum("nt,kt->nk", low[s], normed[slot_stream[s]], preferred_element_type=f32)
+            for s in range(7)
+        ],
+        axis=1,
+    )
+    w_in_grad = lax.psum(w_in_grad.astype(bf16), "dp").astype(f32)
+    grad_normed = jnp.concatenate(
+        [
+            jnp.einsum("nsk,snt->skt", w_in[:, :3], low[:3], preferred_element_type=f32),
+            jnp.einsum("njk,jnt->kt", w_in[:, 3:], low[3:], preferred_element_type=f32)[None],
+        ],
+        axis=0,
+    ).astype(bf16)
+    grad_normed = lax.psum_scatter(grad_normed, "seq", scatter_dimension=1, tiled=True).astype(f32)
+    gx = jnp.sum(grad_normed * scaled, axis=2)
+    gs = jnp.sum(grad_normed, axis=2)
+    norm_gain_grad = jnp.stack([gx[0] + gx[1] + gx[2], gx[3]])
+    norm_bias_grad = jnp.stack([gs[0] + gs[1] + gs[2], gs[3]])
+    g = grad_normed * ng
+    means = sum_feats(jnp.stack([jnp.sum(g, axis=1), jnp.sum(g * scaled, axis=1)])) / width
+    grad_streams = inverse * (g - means[0][:, None] - scaled * means[1][:, None])
+    grad_streams = grad_streams.at[3].add(grad_out_local.astype(f32))
+    grad_mixing = sum_feats(
+        jnp.stack(
+            [jnp.sum(grad_streams * history[j].astype(f32), axis=1) for j in range(states)], axis=1
+        ).reshape(4 * states, tokens)
+    )
+    gen_bias_grad = jnp.sum(grad_mixing, axis=1)
+    gen_out_grad = jnp.einsum("ht,mt->hm", gen_hidden, grad_mixing, precision=highest)
+    grad_hidden = jnp.einsum("hm,mt->ht", out_flat, grad_mixing, precision=highest)
+    grad_pre = gen_pull(grad_hidden)[0].astype(bf16)
+    gen_normed = (last * rms * gain_l).astype(bf16)
+    gen_in_grad = jnp.einsum("dt,ht->dh", gen_normed, grad_pre, preferred_element_type=f32)
+    grad_gen = jnp.einsum("dh,ht->dt", gen_in_l, grad_pre, preferred_element_type=f32)
+    gen_gain_grad = jnp.sum(grad_gen * last * rms, axis=1)
+    mz = jnp.sum(grad_pre.astype(f32) * raw, axis=0, keepdims=True) / width
+    hist_terms = []
+    for j in range(states):
+        term = jnp.sum(mix[:, j] * grad_streams, axis=0)
+        if j == states - 1:
+            term = term + rms * grad_gen * gain_l - last * (rms * rms * rms) * mz
+        hist_terms.append(term.astype(bf16))
+    history_grad = jnp.stack(hist_terms)
+    out_bias_grad = jnp.sum(grad_out_local.astype(f32), axis=1)
+    vec = jnp.concatenate(
+        [
+            in_bias_grad, norm_gain_grad, norm_bias_grad, gen_gain_grad[None],
+            out_bias_grad[None], gen_in_grad.T,
+        ],
+        axis=0,
+    )
+    vec = lax.all_gather(lax.psum(vec, "dp"), "seq", axis=1, tiled=True)
+    shared = lax.psum(
+        jnp.concatenate(
+            [gen_out_grad.reshape(-1), gen_bias_grad, stat_sums, stat_squares, stat_count[None]]
+        ),
+        "dp",
+    )
+    m = 4 * states
+    hid = gen_out.shape[0]
+    count = shared[-1]
+    mix_mean = shared[hid * m + m : hid * m + 2 * m] / count
+    mix_var = shared[hid * m + 2 * m : hid * m + 3 * m] / count - mix_mean * mix_mean
+    return (
+        new_state, history_grad,
+        mix_mean.reshape(4, states), mix_var.reshape(4, states),
+        vec[11], vec[13:].T, shared[: hid * m].reshape(hid, 4, states),
+        shared[hid * m : hid * m + m].reshape(4, states),
+        vec[7:9], vec[9:11], w_in_grad, vec[0:7],
+        row_grads[:, :width], row_grads[:, width:], vec[12],
+    )
+
+
 def solution(mesh):
     in_specs = (
         P(None, "seq", "dp"),
@@ -334,6 +533,8 @@
         P("seq", None),
         P(),
     )
+    split_heads = HEADS % mesh.shape["seq"] == 0
+    body = tp_device if split_heads else per_device
     return jax.shard_map(
-        per_device, mesh=mesh, in_specs=in_specs, out_specs=out_specs, check_vma=False
-    )
+        body, mesh=mesh, in_specs=in_specs, out_specs=out_specs, check_vma=False
+    )

time: 712 us -> 595 us (0.84)
  matrix products: 147 us -> 65.6 us
  local copies, waits for them, and re-layouts: 115 us -> 50.3 us
  waiting for transfers between devices: 287 us -> 314 us
  other arithmetic: 45.8 us -> 61.8 us
  blocking collectives: 82.3 us -> 71.9 us
    dot_general x42 -> x30, matrix products: 147 us -> 62.3 us  [the longest x7 17 us: tp_device(): jnp.einsum('nt,kt->nk', low[s], normed[slot_stream[s]], preferred_element...]
    psum x2 -> x3, waiting for transfers between devices: 118 us -> 200 us  [the longest x1 111 us: tp_device(): row_grads = lax.psum(row_grads, 'dp').astype(f32)]
    all_to_all x2, waiting for transfers between devices: 65.4 us -> 20.1 us  [the longest x1 17.7 us: tp_device(): lax.all_to_all(rows.reshape(feats, 5, n, feats), 'seq', split_axis=2, con...]
    psum x1 -> x2, blocking collectives: 82.3 us -> 42.8 us  [the longest x1 23.5 us: sum_feats(): return lax.psum(part, 'seq')]
    unnamed x218 -> x239, local copies, waits for them, and re-layouts: 50.6 us -> 20.2 us
    all_gather x3 -> x2, waiting for transfers between devices: 50.3 us -> 30.6 us  [the longest x1 30.6 us: tp_device(): lax.all_gather((scaled * ng + nb).astype(bf16), 'seq', axis=1, tiled=True)]
    all_gather x0 -> x2, blocking collectives: none -> 19.6 us  [the longest x1 10.4 us: tp_device(): vec = lax.all_gather(lax.psum(vec, 'dp'), 'seq', axis=1, tiled=True)]
    slice x20 -> x11, local copies, waits for them, and re-layouts: 20.8 us -> 8.02 us  [the longest x1 2.68 us: tp_device(): row_grads[:, width:]]
  transfers between devices with their start and end apart: 9 -> 9, of which waited for: 5 -> 7; matrix products, arithmetic and copies ran while one was open for 36% -> 16% of each run, Pallas kernels for 0% -> 0%
where the time goes in v1:
time: 595 us; the launch traced here: 588 us
  waiting for transfers between devices  314 us (53%)
  blocking collectives  71.9 us (12%)
  matrix products  65.6 us (11%)
  other arithmetic  61.8 us (10%)
  local copies, waits for them, and re-layouts  50.3 us (8%)
  between operations  16.9 us (3%)
  starting transfers between devices  7.85 us (1%)
    psum x1, waiting for transfers between devices, tp_device(): row_grads = lax.psum(row_grads, 'dp').astype(f32)  111 us
    psum x2, waiting for transfers between devices, sum_feats(): return lax.psum(part, 'seq')  89 us
    reduce_scatter x1, waiting for transfers between devices, tp_device(): lax.psum_scatter(grad_normed, 'seq', scatter_dimension=1, tiled=True)  62.2 us
    all_gather x1, waiting for transfers between devices, tp_device(): lax.all_gather((scaled * ng + nb).astype(bf16), 'seq', axis=1, tiled=True)  30.6 us
    psum x1, blocking collectives, sum_feats(): return lax.psum(part, 'seq')  23.5 us
    unnamed x239, local copies, waits for them, and re-layouts  20.2 us
    psum x1, blocking collectives, tp_device(): lax.psum(jnp.concatenate([gen_out_grad.reshape(-1), gen_bias_grad, stat_s...  19.3 us
    all_to_all x1, waiting for transfers between devices, tp_device(): lax.all_to_all(rows.reshape(feats, 5, n, feats), 'seq', split_axis=2, con...  17.7 us
  transfers between devices with their start and end apart: 9, of which 7 were waited for; matrix products, arithmetic and copies ran while one was open for 16% of the time, Pallas kernels for 0%

profile of v1, /device:TPU:0, one launch (start us, length us, event | category | flops | bytes accessed | tf_op | source)
XLA Modules:
  0.0 588.4 jit_solution(17340611214779897451)
XLA Ops:
  12.3 3.5 bitcast_convert_fusion.9
  17.6 9.5 %all-reduce = s32[32]{0:T(128)S(1)} all-reduce(s32[32]{0:T(128)S(1)} %add_dynamic-update-slice_fusion), channel_id=2, replica_groups=mesh['seq'=8,'dp'=4] {'seq'}, use_global_device_ids=true, to_apply=%add | all-reduce | flops 32 | bytes 256
  29.9 38.2 %all-reduce.7.cloned.1.call-done = f32[41,1024]{1,0:T(8,128)} async-done(((f32[41,1024]{1,0:T(8,128)}), f32[41,1024]{1,0:T(8,128)}) %all-reduce.7.cloned.1.call-update) | async-done | bytes 167952 | tf_op jit(solution)/shard_map/psum | solution.py:318
  73.7 3.3 fusion.164
  77.4 9.1 %all-gather.1 = f32[16,4,1024]{2,1,0:T(4,128)S(1)} all-gather(f32[2,4,1024]{2,1,0:T(4,128)S(1)} %pad_maximum_fusion.14), channel_id=3, replica_groups=mesh['seq'=8,'dp'=4] {'seq'}, dimensions={0}, use_global_device_ids=true | all-gather | bytes 294912 | tf_op jit(solution)/shard_map/all_gather | solution.py:357
  93.0 3.6 all-to-all-start
  100.8 17.7 %all-to-all-done = bf16[128,5,8,128]{3,0,1,2:T(8,128)(2,1)S(1)} async-done(((bf16[128,5,8,128]{3,0,1,2:T(8,128)(2,1)}), bf16[128,5,8,128]{3,0,1,2:T(8,128)(2,1)S(1)}, u32[]{:S(2)}, u32[]{:S(2)}) %all-to-all-start) | async-done | bytes 1310752 | tf_op jit(solution)/shard_map/all_to_all | solution.py:332
  121.0 3.1 fusion.13
  126.6 30.6 %all-gather.5.cloned.1.call-done = bf16[4,1024,1024]{2,1,0:T(8,128)(2,1)} async-done(((bf16[4,128,1024]{2,1,0:T(8,128)(2,1)}), bf16[4,1024,1024]{2,1,0:T(8,128)(2,1)}) %all-gather.5.cloned.1.call-update) | async-done | bytes 8388624 | tf_op jit(solution)/shard_map/all_gather | solution.py:365
  159.4 2.5 fusion.35
  173.5 3.3 fusion.172
  182.5 6.4 %multiply_add_fusion = (f32[4,128,1024]{2,1,0:T(8,128)}, f32[4,128,1024]{2,1,0:T(8,128)}) fusion(f32[5,128,1024]{2,1,0:T(8,128)S(1)} %copy-done.6, f32[7,128,1024]{2,1,0:T(8,128)S(1)} %copy-done.2), kind=kLoop, calls=%fused_computation.48 | loop fusion | flops 37224448 | bytes 8388608 | tf_op jit(solution)/shard_map/transpose(jvp())/add_any | solution.py:20
  198.7 2.9 bitcast_convert_fusion.1
  212.9 3.6 all-to-all-start.1
  220.8 4.7 fusion.56
  225.5 3.1 fusion.58
  228.6 3.1 fusion.60
  242.0 3.0 fusion.26
  245.0 5.8 convert_bitcast_fusion
  250.8 6.8 %pad_maximum_fusion = bf16[4,1024,1024]{2,1,0:T(8,128)(2,1)} fusion(bf16[1,1024,1024]{2,1,0:T(8,128)(2,1)S(1)} %fusion.26, bf16[3,1024,1024]{2,1,0:T(8,128)(2,1)} %convert_bitcast_fusion), kind=kLoop, calls=%fused_computation.3 | loop fusion | flops 4194304 | bytes 16777216 | tf_op jit(solution)/shard_map/concatenate | solution.py:434
  259.2 2.7 fusion.4
  263.7 111.4 %all-reduce.11.cloned.1.call-done = (bf16[128,5120]{0,1:T(8,128)(2,1)}, bf16[128,7,1024]{2,0,1:T(8,128)(2,1)}) async-done(((bf16[128,5120]{0,1:T(8,128)(2,1)}, bf16[128,7,1024]{2,0,1:T(8,128)(2,1)}), (bf16[128,5120]{0,1:T(8,128)(2,1)}, bf16[128,7,1024]{2,0,1:T(8,128)(2,1)})) %all-reduce.11.cloned.1.call-update) | async-done | bytes 3145744 | tf_op jit(solution)/shard_map/psum | solution.py:407
  376.1 2.7 slice.483
  379.7 2.9 copy.112
  382.6 4.1 convert_element_type.274
  386.8 62.2 %reduce-scatter.5.cloned.1.call-done = bf16[4,128,1024]{2,1,0:T(8,128)(2,1)} async-done(((bf16[4,1024,1024]{2,1,0:T(8,128)(2,1)}), bf16[4,128,1024]{2,1,0:T(8,128)(2,1)}) %reduce-scatter.5.cloned.1.call-update) | async-done | bytes 1048592 | tf_op jit(solution)/shard_map/reduce_scatter | solution.py:441
  448.9 2.9 fusion.10
  452.3 23.5 %psum.50 = f32[2,4,1024]{2,1,0:T(4,128)} all-reduce(f32[2,4,1024]{2,1,0:T(4,128)S(1)} %pad_maximum_fusion.15), channel_id=1, replica_groups=mesh['seq'=8,'dp'=4] {'seq'}, use_global_device_ids=true, to_apply=%region_13.14 | all-reduce | flops 8192 | bytes 65536 | tf_op jit(solution)/shard_map/psum | solution.py:318
  479.0 4.3 multiply_reduce_fusion
  486.2 50.8 %all-reduce.9.cloned.1.call-done = f32[36,1024]{1,0:T(8,128)} async-done(((f32[36,1024]{1,0:T(8,128)}), f32[36,1024]{1,0:T(8,128)}) %all-reduce.9.cloned.1.call-update) | async-done | bytes 147472 | tf_op jit(solution)/shard_map/psum | solution.py:318
  545.1 19.3 %all-reduce.1 = (f32[1549]{0:T(1024)S(1)}, f32[53,128]{1,0:T(8,128)S(1)}) all-reduce(f32[1549]{0:T(1024)S(1)} %concatenate.77, f32[53,128]{1,0:T(8,128)S(1)} %concatenate.78), channel_id=1, replica_groups=mesh['seq'=8,'dp'=4] {'dp'}, use_global_device_ids=true, to_apply=%region_38.39 | all-reduce | flops 8333 | bytes 66664 | tf_op jit(solution)/shard_map/psum | solution.py:480
  564.4 10.4 %all_gather.27 = f32[53,1024]{1,0:T(8,128)S(1)} all-gather(f32[53,128]{1,0:T(8,128)S(1)} %get-tuple-element.100), channel_id=1, replica_groups=mesh['seq'=8,'dp'=4] {'seq'}, dimensions={1}, use_global_device_ids=true | all-gather | bytes 244224 | tf_op jit(solution)/shard_map/all_gather | solution.py:479
  (374 shorter events, 110.3 us)
Async XLA Ops:
  7.2 60.9 %all-reduce.7.cloned.1.call-start = ((), (), s32[]{:S(2)}) async-start(), calls=%async_computation.4 | async-start | bytes 393216 | tf_op jit(solution)/shard_map/psum | solution.py:318
  11.5 109.5 %all-gather.7.cloned.1.call-start = ((), (), s32[]{:S(2)}) async-start(), calls=%async_computation.7 | async-start | bytes 2359296 | tf_op jit(solution)/shard_map/all_gather | solution.py:328
  12.2 144.9 %all-gather.5.cloned.1.call-start = ((), (), s32[]{:S(2)}) async-start(), calls=%async_computation.5 | async-start | bytes 9437184 | tf_op jit(solution)/shard_map/all_gather | solution.py:365
  12.3 15.0 %copy-start.100 = (s32[4]{0:T(128)S(1)}, s32[4]{0:T(128)}, u32[]{:S(2)}) copy-start(s32[4]{0:T(128)} %constant.177) | copy-start | bytes 52
  12.3 16.9 %copy-start.80 = (f32[40,4,9]{0,1,2:T(4,128)S(1)}, f32[40,4,9]{0,1,2:T(4,128)}, u32[]{:S(2)}) copy-start(f32[40,4,9]{0,1,2:T(4,128)} %param.24) | copy-start | bytes 17284
  15.9 61.1 %copy-start.10 = (f32[128,1024]{1,0:T(8,128)}, f32[128,1024]{1,0:T(8,128)S(1)}, u32[]{:S(2)}) copy-start(f32[128,1024]{1,0:T(8,128)S(1)} %get-tuple-element.115) | copy-start | bytes 1572868
  15.9 61.1 %copy-start.12 = (f32[128,1024]{1,0:T(8,128)}, f32[128,1024]{1,0:T(8,128)S(1)}, u32[]{:S(2)}) copy-start(f32[128,1024]{1,0:T(8,128)S(1)} %get-tuple-element.116) | copy-start | bytes 1572868
  27.4 43.4 %copy-start.90 = (s32[8]{0:T(128)}, s32[8]{0:T(128)S(1)}, u32[]{:S(2)}) copy-start(s32[8]{0:T(128)S(1)} %get-tuple-element.98) | copy-start | bytes 100
  28.7 59.4 %copy-start.77 = (f32[4,128]{1,0:T(4,128)}, f32[4,128]{1,0:T(4,128)S(1)}, u32[]{:S(2)}) copy-start(f32[4,128]{1,0:T(4,128)S(1)} %gather_fusion) | copy-start | bytes 6148
  29.3 44.1 %copy-start.75 = (f32[40,36]{0,1:T(8,128)}, f32[40,36]{0,1:T(8,128)S(1)}, u32[]{:S(2)}) copy-start(f32[40,36]{0,1:T(8,128)S(1)} %reshape.559) | copy-start | bytes 17284
  91.6 6.7 %copy-start.91 = (s32[8]{0:T(128)S(1)}, s32[8]{0:T(128)}, u32[]{:S(2)}) copy-start(s32[8]{0:T(128)} %copy-done.90) | copy-start | bytes 100
  93.0 25.5 %all-to-all-start = ((bf16[128,5,8,128]{3,0,1,2:T(8,128)(2,1)}), bf16[128,5,8,128]{3,0,1,2:T(8,128)(2,1)S(1)}, u32[]{:S(2)}, u32[]{:S(2)}) async-start(bf16[128,5,8,128]{3,0,1,2:T(8,128)(2,1)} %copy.90), calls=%async_computation | async-start | bytes 2621440 | tf_op jit(solution)/shard_map/all_to_all | solution.py:332
  96.6 165.3 %reduce-scatter.3.cloned.1.call-start = ((), (), s32[]{:S(2)}) async-start(), calls=%async_computation.6 | async-start | bytes 2359296 | tf_op jit(solution)/shard_map/reduce_scatter | solution.py:400
  157.2 7.0 %copy-start.103 = (bf16[4,1024,1024]{2,1,0:T(8,128)(2,1)S(1)}, bf16[4,1024,1024]{2,1,0:T(8,128)(2,1)}, u32[]{:S(2)}) copy-start(bf16[4,1024,1024]{2,1,0:T(8,128)(2,1)} %all-gather.5.cloned.1.call-done) | copy-start | bytes 25165828
  212.9 27.3 %all-to-all-start.1 = ((bf16[8,128,5,128]{3,1,2,0:T(8,128)(2,1)}), bf16[8,128,5,128]{3,1,2,0:T(8,128)(2,1)S(1)}, u32[]{:S(2)}, u32[]{:S(2)}) async-start(bf16[8,128,5,128]{3,1,2,0:T(8,128)(2,1)} %copy.108), calls=%async_computation.3 | async-start | bytes 2621440 | tf_op jit(solution)/shard_map/all_to_all | solution.py:404
  216.5 158.6 %all-reduce.11.cloned.1.call-start = ((), (), s32[]{:S(2)}) async-start(), calls=%async_computation.10 | async-start | bytes 6291456 | tf_op jit(solution)/shard_map/psum | solution.py:407
  220.0 11.7 %slice-start = ((s8[8388608]{0:T(1024)(128)(4,1)}), s8[4194304]{0:T(1024)(128)(4,1)S(1)}, s32[]{:S(2)}) async-start(s8[8388608]{0:T(1024)(128)(4,1)} %bitcast.480), calls=%async_computation.11 | async-start | bytes 8388608
  220.8 15.5 %copy-start.32 = (bf16[7,128,1024]{2,1,0:T(8,128)(2,1)}, bf16[7,128,1024]{2,1,0:T(8,128)(2,1)S(1)}, u32[]{:S(2)}) copy-start(bf16[7,128,1024]{2,1,0:T(8,128)(2,1)S(1)} %fusion.5) | copy-start | bytes 5505028
  220.8 10.9 %slice-start.1 = ((s8[8388608]{0:T(1024)(128)(4,1)}), s8[4194304]{0:T(1024)(128)(4,1)S(1)}, s32[]{:S(2)}) async-start(s8[8388608]{0:T(1024)(128)(4,1)} %bitcast.480), calls=%async_computation.12 | async-start | bytes 8388608
  241.7 207.2 %reduce-scatter.5.cloned.1.call-start = ((), (), s32[]{:S(2)}) async-start(), calls=%async_computation.8 | async-start | bytes 9437184 | tf_op jit(solution)/shard_map/reduce_scatter | solution.py:441
  257.6 279.4 %all-reduce.9.cloned.1.call-start = ((), (), s32[]{:S(2)}) async-start(), calls=%async_computation.9 | async-start | bytes 327680 | tf_op jit(solution)/shard_map/psum | solution.py:318
  382.6 66.3 %copy-start.78 = (f32[4,128]{1,0:T(4,128)S(1)}, f32[4,128]{1,0:T(4,128)}, u32[]{:S(2)}) copy-start(f32[4,128]{1,0:T(4,128)} %copy-done.77) | copy-start | bytes 6148
  448.9 27.7 %copy-start.26 = (bf16[4,128,1024]{2,1,0:T(8,128)(2,1)S(1)}, bf16[4,128,1024]{2,1,0:T(8,128)(2,1)}, u32[]{:S(2)}) copy-start(bf16[4,128,1024]{2,1,0:T(8,128)(2,1)} %reduce-scatter.5.cloned.1.call-done) | copy-start | bytes 3145732
  484.5 52.5 %copy-start.36 = (f32[40,1024]{1,0:T(8,128)S(1)}, f32[40,1024]{1,0:T(8,128)}, u32[]{:S(2)}) copy-start(f32[40,1024]{1,0:T(8,128)} %copy-done.35) | copy-start | bytes 491524
  484.5 52.5 %copy-start.37 = (f32[41,1024]{1,0:T(8,128)S(1)}, f32[41,1024]{1,0:T(8,128)}, u32[]{:S(2)}) copy-start(f32[41,1024]{1,0:T(8,128)} %all-reduce.7.cloned.1.call-done) | copy-start | bytes 503812
  484.6 52.5 %copy-start.71 = (f32[1,1024]{1,0:T(1,128)S(1)}, f32[1,1024]{1,0:T(1,128)}, u32[]{:S(2)}) copy-start(f32[1,1024]{1,0:T(1,128)} %copy-done.70) | copy-start | bytes 12292
  484.6 53.8 %copy-start.76 = (f32[40,36]{0,1:T(8,128)S(1)}, f32[40,36]{0,1:T(8,128)}, u32[]{:S(2)}) copy-start(f32[40,36]{0,1:T(8,128)} %copy-done.75) | copy-start | bytes 17284
  484.7 55.1 %copy-start.93 = (f32[128]{0:T(128)S(1)}, f32[128]{0:T(128)}, u32[]{:S(2)}) copy-start(f32[128]{0:T(128)} %copy-done.92) | copy-start | bytes 1540
  484.7 56.3 %copy-start.81 = (f32[1,1024]{1,0:T(1,128)S(1)}, f32[1,1024]{1,0:T(1,128)}, u32[]{:S(2)}) copy-start(f32[1,1024]{1,0:T(1,128)} %get-tuple-element.107) | copy-start | bytes 12292
  538.3 6.6 %copy-start.86 = (f32[7,128]{1,0:T(8,128)S(1)}, f32[7,128]{1,0:T(8,128)}, u32[]{:S(2)}) copy-start(f32[7,128]{1,0:T(8,128)} %fusion.4) | copy-start | bytes 10756
  538.3 6.6 %copy-start.94 = (f32[128]{0:T(128)S(1)}, f32[128]{0:T(128)}, u32[]{:S(2)}) copy-start(f32[128]{0:T(128)} %convert_reduce_fusion.1) | copy-start | bytes 1540
  538.3 6.6 %copy-start.97 = (f32[1,128]{1,0:T(1,128)S(1)}, f32[1,128]{1,0:T(1,128)}, u32[]{:S(2)}) copy-start(f32[1,128]{1,0:T(1,128)} %get-tuple-element.161) | copy-start | bytes 1540
  (84 other events, 216.0 us)
Sparse Core Ops, SparseCore 0:
  11.6 56.4 all-reduce.6
  70.0 27.5 all-gather.6
  100.1 57.0 all-gather.4
  201.8 49.8 reduce-scatter.2
  254.0 121.0 all-reduce.10
  378.4 70.4 reduce-scatter.4
  484.6 52.3 all-reduce.8

commit v2 on v1

--- a/solution.py
+++ b/solution.py
@@ -1,8 +1,11 @@
+import functools
 import math
 
 import jax
 import jax.numpy as jnp
 from jax import lax
+from jax.experimental import pallas as pl
+from jax.experimental.pallas import tpu as pltpu
 from jax.sharding import PartitionSpec as P
 
 HEADS = 16
@@ -299,6 +302,354 @@
     )
 
 
+MESH = pl.DeviceIdType.MESH
+HIDDEN_ROWS = 40
+ROOT_HALF = math.sqrt(0.5)
+INV_ROOT_2PI = 1.0 / math.sqrt(2.0 * math.pi)
+
+
+def gelu_pair(x):
+    half = 0.5 + 0.5 * lax.erf(x * ROOT_HALF)
+    return x * half, half + x * (jnp.exp(-0.5 * x * x) * INV_ROOT_2PI)
+
+
+def contract(a, b, dim_a, dim_b, precision=None):
+    return lax.dot_general(
+        a, b, (((dim_a,), (dim_b,)), ((), ())),
+        precision=precision, preferred_element_type=jnp.float32,
+    )
+
+
+class Links:
+    def __init__(self, n):
+        self.n = n
+        self.me = lax.axis_index("seq")
+        core = self.me % 2
+        xbit = (self.me // 2) % 2
+        ybit = (self.me // 4) % 2
+        flip = 1 - 2 * core
+        x = self.me + 2 - 4 * xbit
+        y = self.me + 4 - 8 * ybit
+        self.core = core
+        self.a = x * (1 - core) + y * core
+        self.b = y * (1 - core) + x * core
+        self.dg = x + y - self.me
+        self.p = self.me + flip
+        self.pa = self.b + flip
+        self.pb = self.a + flip
+        self.pdg = self.dg + flip
+
+    def greet(self):
+        barrier = pltpu.get_barrier_semaphore()
+        for k in range(1, self.n):
+            pl.semaphore_signal(
+                barrier, inc=1, device_id={"seq": (self.me + k) % self.n}, device_id_type=MESH
+            )
+        pl.semaphore_wait(barrier, self.n - 1)
+
+    def copy(self, src, dst, send, recv, to):
+        return pltpu.make_async_remote_copy(
+            src_ref=src, dst_ref=dst, send_sem=send, recv_sem=recv,
+            device_id={"seq": to}, device_id_type=MESH,
+        )
+
+
+class Gather:
+    def __init__(self, links, place, send, recv):
+        self.links, self.place, self.send, self.recv = links, place, send, recv
+
+    def _go(self, src, owner, slot, index, to):
+        self.links.copy(
+            src, self.place(owner), self.send.at[slot], self.recv.at[index], to
+        ).start()
+
+    def _got(self, owner, index):
+        place = self.place(owner)
+        self.links.copy(place, place, self.send.at[0], self.recv.at[index], self.links.p).wait_recv()
+
+    def start(self, src):
+        at = self.links
+        self._go(src, at.me, 0, 0, at.a)
+        self._go(src, at.me, 1, 1, at.b)
+        self._go(src, at.me, 2, 3, at.p)
+
+    def near(self):
+        at = self.links
+        self._got(at.a, 0)
+        self._go(self.place(at.a), at.a, 3, 2, at.b)
+        self._go(self.place(at.a), at.a, 4, 4, at.p)
+        self._got(at.b, 1)
+        self._go(self.place(at.b), at.b, 5, 5, at.p)
+
+    def far(self):
+        at = self.links
+        self._got(at.dg, 2)
+        self._go(self.place(at.dg), at.dg, 6, 6, at.p)
+
+    def other(self):
+        at = self.links
+        for owner, index in ((at.p, 3), (at.pa, 4), (at.pb, 5), (at.pdg, 6)):
+            self._got(owner, index)
+
+    def drain(self):
+        place = self.place(self.links.me)
+        for slot in range(7):
+            self.links.copy(
+                place, place, self.send.at[slot], self.recv.at[0], self.links.p
+            ).wait_send()
+
+
+class Everyone:
+    def __init__(self, links, source, target, arrived, send, recv):
+        self.links, self.source, self.target, self.arrived = links, source, target, arrived
+        self.send, self.recv = send, recv
+
+    def start(self):
+        at = self.links
+        for k in range(1, at.n):
+            to = (at.me + k) % at.n
+            at.copy(
+                self.source(to), self.target(k), self.send.at[k], self.recv.at[k], to
+            ).start()
+
+    def wait(self, k):
+        at = self.links
+        origin = (at.me + at.n - k) % at.n
+        place = self.arrived(k, origin)
+        at.copy(place, place, self.send.at[k], self.recv.at[k], at.p).wait_recv()
+        return origin
+
+    def drain(self):
+        at = self.links
+        for k in range(1, at.n):
+            to = (at.me + k) % at.n
+            place = self.source(to)
+            at.copy(place, place, self.send.at[k], self.recv.at[k], at.p).wait_send()
+
+
+def front_kernel(
+    n,
+    hist, cot, lens, vals, gain, gin, gout, gbias, ng, nb, w_out, w_down,
+    nbuf, cot_all, cols, pk, raw_out, scaled, st3, stat_out,
+    prm, colp, part, part_in, stat, stat_in, streams, nown,
+    ex_send, ex_recv, ag_send, ag_recv, local_sem,
+):
+    f32, bf16 = jnp.float32, jnp.bfloat16
+    states, feats, tokens = hist.shape
+    block = tokens // n
+    width = n * feats
+    hid = gin.shape[0]
+    at = Links(n)
+    me = at.me
+    mine = pl.ds(pl.multiple_of(me * feats, feats), feats)
+
+    def rows(owner):
+        return pl.ds(pl.multiple_of(owner * feats, feats), feats)
+
+    def lanes(owner):
+        return pl.ds(pl.multiple_of(owner * block, block), block)
+
+    gathers = [
+        Gather(at, lambda owner, s=s: nbuf.at[s, rows(owner), :], ag_send.at[s], ag_recv.at[s])
+        for s in range(4)
+    ]
+    cots = Gather(at, lambda owner: cot_all.at[rows(owner), :], ag_send.at[4], ag_recv.at[4])
+    parts = Everyone(
+        at, lambda to: part.at[to], lambda k: part_in.at[k], lambda k, origin: part_in.at[k],
+        ex_send.at[0], ex_recv.at[0],
+    )
+    mixes = Everyone(
+        at, lambda to: pk.at[me], lambda k: pk.at[me], lambda k, origin: pk.at[origin],
+        ex_send.at[1], ex_recv.at[1],
+    )
+    stats = Everyone(
+        at, lambda to: stat, lambda k: stat_in.at[me], lambda k, origin: stat_in.at[origin],
+        ex_send.at[2], ex_recv.at[2],
+    )
+
+    at.greet()
+    cots.start(cot)
+    keep_cot = pltpu.make_async_copy(cot, cot_all.at[mine, :], local_sem.at[0])
+    keep_cot.start()
+
+    prm[...] = jnp.zeros_like(prm)
+    prm[0:1, :] = gain[:, mine]
+    prm[1:3, :] = ng[:, mine]
+    prm[3:5, :] = nb[:, mine]
+    colp[...] = prm[...].T
+    gin_mine = gin[:, mine]
+    for b in range(n):
+        last = hist[states - 1, :, b * block : (b + 1) * block].astype(f32)
+        product = (last * colp[:, 0:1]).astype(bf16)
+        part[b, 0:hid, :] = jnp.dot(gin_mine, product, preferred_element_type=f32)
+        part[b, hid : hid + 8, :] = jnp.broadcast_to(
+            jnp.sum(last * last, axis=0, keepdims=True), (8, block)
+        )
+    parts.start()
+    total = part[me]
+    for k in range(1, n):
+        parts.wait(k)
+        total = total + part_in[k]
+    raw_out[...] = total
+    rms = lax.rsqrt(total[hid : hid + 1] * (1.0 / width) + rms_eps)
+    hidden, _ = gelu_pair(total[0:hid] * rms)
+    table = jnp.concatenate([gout[j] for j in range(states)], axis=0)
+    mixing = jnp.dot(table, hidden, precision=highest, preferred_element_type=f32)
+    for j in range(states):
+        pk[me, 4 * j : 4 * j + 4, :] = mixing[4 * j : 4 * j + 4] + gbias[:, j : j + 1]
+    row = 4 * states
+    pk[me, row : row + 1, :] = rms
+    for offset, value in ((1, lens[0, 0, 0]), (2, vals[0, 0, 0]), (3, vals[0, 0, 1])):
+        pk[me, row + offset : row + offset + 1, :] = jnp.full((1, block), value.astype(f32))
+    mixes.start()
+
+    def column_copies(to, send, recv):
+        out = []
+        for j in range(5):
+            if j == 0:
+                src = w_out.at[:, rows(to)]
+            else:
+                src = w_down.at[:, pl.ds(pl.multiple_of((j - 1) * width + to * feats, feats), feats)]
+            out.append((src, cols.at[mine, pl.ds(j * feats, feats)]))
+        return out
+
+    for k in range(1, n):
+        to = (me + k) % n
+        for src, dst in column_copies(to, None, None):
+            at.copy(src, dst, ex_send.at[3, k], ex_recv.at[3, k], to).start()
+    own_cols = [
+        pltpu.make_async_copy(src, dst, local_sem.at[1 + j])
+        for j, (src, dst) in enumerate(column_copies(me, None, None))
+    ]
+    for copy in own_cols:
+        copy.start()
+    cots.near()
+
+    def mix_block(owner):
+        where = lanes(owner)
+        for half in range(2):
+            part_rows = pl.ds(half * (feats // 2), feats // 2)
+            sums = [None] * 4
+            for j in range(states):
+                value = hist[j, part_rows, where].astype(f32)
+                for s in range(4):
+                    weight = pk[owner, pl.ds(4 * j + s, 1), :]
+                    term = weight * value
+                    sums[s] = term if sums[s] is None else sums[s] + term
+            for s in range(4):
+                streams[s, part_rows, where] = sums[s]
+        for s in range(4):
+            value = streams[s, :, where]
+            mean = jnp.sum(value, axis=0, keepdims=True) * (1.0 / feats)
+            off = value - mean
+            stat[pl.ds(s, 1), where] = mean
+            stat[pl.ds(4 + s, 1), where] = jnp.sum(off * off, axis=0, keepdims=True)
+
+    mix_block(me)
+
+    @pl.loop(1, n)
+    def _(k):
+        mix_block(mixes.wait(k))
+
+    stats.start()
+    cots.far()
+    for k in range(1, n):
+        stats.wait(k)
+    stat_in[me] = stat[...]
+    means = stat_in[0, 0:4, :]
+    for k in range(1, n):
+        means = means + stat_in[k, 0:4, :]
+    means = means * (1.0 / n)
+    spread = jnp.zeros_like(means)
+    for k in range(n):
+        away = stat_in[k, 0:4, :] - means
+        spread = spread + (stat_in[k, 4:8, :] + feats * (away * away))
+    stat_out[0:4, :] = means
+    stat_out[4:8, :] = lax.rsqrt(spread * (1.0 / width) + ln_eps)
+
+    keeps = []
+    for s in range(4):
+        which = 0 if s < 3 else 1
+        for b in range(n):
+            where = pl.ds(b * block, block)
+            xhat = (streams[s, :, where] - stat_out[s : s + 1, where]) * stat_out[4 + s : 5 + s, where]
+            scaled[s, :, where] = xhat
+            nown[s, :, where] = (
+                xhat * colp[:, 1 + which : 2 + which] + colp[:, 3 + which : 4 + which]
+            ).astype(bf16)
+        gathers[s].start(nown.at[s])
+        keep = pltpu.make_async_copy(nown.at[s], nbuf.at[s, mine, :], local_sem.at[6 + s])
+        keep.start()
+        keeps.append(keep)
+    st3[...] = streams[3]
+    for s in range(4):
+        gathers[s].near()
+        if s >= 1:
+            gathers[s - 1].far()
+    gathers[3].far()
+    for g in [cots] + gathers:
+        g.other()
+    for k in range(1, n):
+        place = cols.at[rows((me + n - k) % n), :]
+        at.copy(place, place, ex_send.at[3, k], ex_recv.at[3, k], at.p).wait()
+    for g in [cots] + gathers:
+        g.drain()
+    for exchange in (parts, mixes, stats):
+        exchange.drain()
+    keep_cot.wait()
+    for copy in own_cols + keeps:
+        copy.wait()
+
+
+def front(n, history, cotangent, bucket_len, valid_len, gen_gain, gen_in, gen_out, gen_bias, norm_gain, norm_bias, w_out, w_down):
+    f32, bf16 = jnp.float32, jnp.bfloat16
+    states, feats, tokens = history.shape
+    block = tokens // n
+    width = n * feats
+    hid = gen_in.shape[1]
+    vmem = pl.BlockSpec(memory_space=pltpu.VMEM)
+    smem = pl.BlockSpec(memory_space=pltpu.SMEM)
+    anys = pl.BlockSpec(memory_space=pl.ANY)
+    shape = jax.ShapeDtypeStruct
+    return pl.pallas_call(
+        functools.partial(front_kernel, n),
+        out_shape=(
+            shape((4, width, tokens), bf16),
+            shape((width, tokens), bf16),
+            shape((width, 5 * feats), bf16),
+            shape((n, 40, block), f32),
+            shape((hid + 8, block), f32),
+            shape((4, feats, tokens), f32),
+            shape((feats, tokens), f32),
+            shape((8, tokens), f32),
+        ),
+        in_specs=[vmem, vmem, smem, smem] + [vmem] * 6 + [anys] * 2,
+        out_specs=(anys, anys, anys, vmem, vmem, vmem, vmem, vmem),
+        scratch_shapes=[
+            pltpu.VMEM((feats, feats), f32),
+            pltpu.VMEM((feats, feats), f32),
+            pltpu.VMEM((n, hid + 8, block), f32),
+            pltpu.VMEM((n, hid + 8, block), f32),
+            pltpu.VMEM((8, tokens), f32),
+            pltpu.VMEM((n, 8, tokens), f32),
+            pltpu.VMEM((4, feats, tokens), f32),
+            pltpu.VMEM((4, feats, tokens), bf16),
+            pltpu.SemaphoreType.DMA((4, n)),
+            pltpu.SemaphoreType.DMA((4, n)),
+            pltpu.SemaphoreType.DMA((5, 7)),
+            pltpu.SemaphoreType.DMA((5, 7)),
+            pltpu.SemaphoreType.DMA((10,)),
+        ],
+        compiler_params=pltpu.CompilerParams(
+            collective_id=1, has_side_effects=True, vmem_limit_bytes=60 * 2**20
+        ),
+        name="front",
+    )(
+        history, cotangent, bucket_len, valid_len, gen_gain.reshape(1, width), gen_in.T,
+        gen_out.transpose(2, 1, 0), gen_bias, norm_gain, norm_bias, w_out, w_down,
+    )
+
+
 def tp_device(
     history, cotangent, bucket_len, valid_len, gen_gain, gen_in, gen_out, gen_bias,
     norm_gain, norm_bias, w_in, in_bias, w_out, w_down, out_bias,
@@ -317,52 +668,38 @@
     def sum_feats(part):
         return lax.psum(part, "seq")
 
-    lens = lax.all_gather(
-        jnp.concatenate([bucket_len.reshape(2), valid_len.reshape(2)]), "seq"
-    )
-    index = jnp.arange(block, dtype=jnp.int32)[None, :]
-    second = index >= lens[:, 0:1]
-    position = index - jnp.where(second, lens[:, 0:1], 0)
-    valid = position < jnp.where(second, lens[:, 3:4], lens[:, 2:3])
+    normed, cot_all, cols, pk, own, scaled, stream3, stat = front(
+        n, history, cotangent, bucket_len, valid_len, gen_gain, gen_in, gen_out, gen_bias,
+        norm_gain, norm_bias, w_out, w_down,
+    )
+    cols = cols.reshape(width, 5, feats)
+    m = 4 * states
+    hid = gen_out.shape[0]
+    index = jnp.arange(block, dtype=jnp.int32)[None, :].astype(f32)
+    second = index >= pk[:, m + 1]
+    position = index - jnp.where(second, pk[:, m + 1], 0.0)
+    valid = position < jnp.where(second, pk[:, m + 3], pk[:, m + 2])
     valid_float = valid.reshape(tokens).astype(f32)
-    cot_all = lax.all_gather(cotangent, "seq", axis=0, tiled=True)
     grad_out = jnp.where(valid.reshape(1, tokens), cot_all, jnp.zeros_like(cot_all))
     grad_out_local = jnp.where(valid.reshape(1, tokens), cotangent, jnp.zeros_like(cotangent))
-    rows = jnp.concatenate([w_out[:, None], w_down.reshape(feats, 4, width)], axis=1)
-    cols = lax.all_to_all(
-        rows.reshape(feats, 5, n, feats), "seq", split_axis=2, concat_axis=0, tiled=True
-    ).reshape(width, 5, feats)
     last = history[states - 1].astype(f32)
     gain_l = local(gen_gain, 0)[:, None]
     gen_in_l = local(gen_in, 0)
-    lg = (last * gain_l).astype(bf16)
-    part = jnp.einsum("dh,dt->ht", gen_in_l, lg, preferred_element_type=f32)
-    part = sum_feats(jnp.concatenate([part, jnp.sum(last * last, axis=0, keepdims=True)], axis=0))
-    raw, square = part[:-1], part[-1:]
-    rms = lax.rsqrt(square / width + rms_eps)
+    mixing = jnp.swapaxes(pk[:, :m], 0, 1).reshape(m, tokens)
+    rms = pk[:, m].reshape(1, tokens)
+    raw = lax.all_gather(own[:hid], "seq", axis=1, tiled=True)
     gen_pre = raw * rms
     gen_hidden, gen_pull = jax.vjp(gelu_exact, gen_pre)
-    out_flat = gen_out.reshape(gen_out.shape[0], 4 * states)
-    mixing = jnp.einsum("hm,ht->mt", out_flat, gen_hidden, precision=highest) + gen_bias.reshape(-1, 1)
+    out_flat = gen_out.transpose(0, 2, 1).reshape(hid, m)
     weighted = mixing * valid_float
     stat_sums = jnp.sum(weighted, axis=1)
     stat_squares = jnp.sum(weighted * mixing, axis=1)
     stat_count = jnp.sum(valid_float)
-    mix = mixing.reshape(4, states, 1, tokens)
-    streams = mix[:, 0] * history[0]
-    for state in range(1, states):
-        streams = streams + mix[:, state] * history[state]
-    mean_l = jnp.mean(streams, axis=1)
-    m2_l = jnp.sum((streams - mean_l[:, None]) ** 2, axis=1)
-    both = lax.all_gather(jnp.stack([mean_l, m2_l]), "seq")
-    centre = jnp.mean(both[:, 0], axis=0)
-    m2 = jnp.sum(both[:, 1] + feats * (both[:, 0] - centre) ** 2, axis=0)
-    inverse = lax.rsqrt(m2 / width + ln_eps)[:, None]
-    scaled = (streams - centre[:, None]) * inverse
+    mix = mixing.reshape(states, 4, 1, tokens).swapaxes(0, 1)
+    streams = [None, None, None, stream3]
+    inverse = stat[4:, None]
     which = jnp.array([0, 0, 0, 1])
     ng = local(norm_gain, 1)[which][:, :, None]
-    nb = local(norm_bias, 1)[which][:, :, None]
-    normed = lax.all_gather((scaled * ng + nb).astype(bf16), "seq", axis=1, tiled=True)
     slot_stream = [0, 1, 2, 3, 3, 3, 3]
     proj = jnp.stack(
         [jnp.dot(w_in[:, s], normed[slot_stream[s]], preferred_element_type=f32) for s in range(7)]
@@ -449,7 +786,7 @@
     grad_streams = grad_streams.at[3].add(grad_out_local.astype(f32))
     grad_mixing = sum_feats(
         jnp.stack(
-            [jnp.sum(grad_streams * history[j].astype(f32), axis=1) for j in range(states)], axis=1
+            [jnp.sum(grad_streams * history[j].astype(f32), axis=1) for j in range(states)], axis=0
         ).reshape(4 * states, tokens)
     )
     gen_bias_grad = jnp.sum(grad_mixing, axis=1)
@@ -483,16 +820,14 @@
         ),
         "dp",
     )
-    m = 4 * states
-    hid = gen_out.shape[0]
     count = shared[-1]
     mix_mean = shared[hid * m + m : hid * m + 2 * m] / count
     mix_var = shared[hid * m + 2 * m : hid * m + 3 * m] / count - mix_mean * mix_mean
     return (
         new_state, history_grad,
-        mix_mean.reshape(4, states), mix_var.reshape(4, states),
-        vec[11], vec[13:].T, shared[: hid * m].reshape(hid, 4, states),
-        shared[hid * m : hid * m + m].reshape(4, states),
+        mix_mean.reshape(states, 4).T, mix_var.reshape(states, 4).T,
+        vec[11], vec[13:].T, shared[: hid * m].reshape(hid, states, 4).swapaxes(1, 2),
+        shared[hid * m : hid * m + m].reshape(states, 4).T,
         vec[7:9], vec[9:11], w_in_grad, vec[0:7],
         row_grads[:, :width], row_grads[:, width:], vec[12],
     )

time: 595 us -> 433 us (0.73)
  waiting for transfers between devices: 314 us -> 128 us
  Pallas kernels: 0 us -> 79.8 us
  other arithmetic: 61.8 us -> 42.1 us
  matrix products: 65.6 us -> 55.2 us
  blocking collectives: 71.9 us -> 63.4 us
  local copies, waits for them, and re-layouts: 50.3 us -> 43.2 us
    pallas_call x0 -> x1, Pallas kernels: none -> 79.8 us  [front(): pl.pallas_call(functools.partial(front_kernel, n), out_shape=(shape((4, w...]
    reduce_scatter x1, waiting for transfers between devices: 62.2 us -> 0.01 us  [tp_device(): lax.psum_scatter(grad_normed, 'seq', scatter_dimension=1, tiled=True)]
    psum x2 -> x1, waiting for transfers between devices: 89 us -> 48.3 us  [sum_feats(): return lax.psum(part, 'seq')]
    psum x1, waiting for transfers between devices: 111 us -> 79.6 us  [tp_device(): row_grads = lax.psum(row_grads, 'dp').astype(f32)]
    all_gather x2 -> x0, waiting for transfers between devices: 30.6 us -> none  [the longest x1 30.6 us: tp_device(): lax.all_gather((scaled * ng + nb).astype(bf16), 'seq', axis=1, tiled=True)]
    all_to_all x1 -> x0, waiting for transfers between devices: 17.7 us -> none  [tp_device(): lax.all_to_all(rows.reshape(feats, 5, n, feats), 'seq', split_axis=2, con...]
    unnamed x1 -> x0, blocking collectives: 9.49 us -> none
    dot_general x7, matrix products: 17 us -> 10.7 us  [tp_device(): jnp.einsum('nt,kt->nk', low[s], normed[slot_stream[s]], preferred_element...]
  transfers between devices with their start and end apart: 9 -> 5, of which waited for: 7 -> 2; matrix products, arithmetic and copies ran while one was open for 16% -> 16% of each run, Pallas kernels for 0% -> 0%
where the time goes in v2:
time: 433 us; the launch traced here: 432 us
  waiting for transfers between devices  128 us (30%)
  Pallas kernels  79.8 us (18%)
  blocking collectives  63.4 us (15%)
  matrix products  55.2 us (13%)
  local copies, waits for them, and re-layouts  43.2 us (10%)
  other arithmetic  42.1 us (10%)
  between operations  16.5 us (4%)
    pallas_call x1, Pallas kernels, front(): pl.pallas_call(functools.partial(front_kernel, n), out_shape=(shape((4, w...  79.8 us
    psum x1, waiting for transfers between devices, tp_device(): row_grads = lax.psum(row_grads, 'dp').astype(f32)  79.6 us
    psum x1, waiting for transfers between devices, sum_feats(): return lax.psum(part, 'seq')  48.3 us
    psum x1, blocking collectives, sum_feats(): return lax.psum(part, 'seq')  23.8 us
    psum x1, blocking collectives, tp_device(): lax.psum(jnp.concatenate([gen_out_grad.reshape(-1), gen_bias_grad, stat_s...  19.3 us
    unnamed x182, local copies, waits for them, and re-layouts  16.9 us
    dot_general x7, matrix products, tp_device(): jnp.dot(w_in[:, s], normed[slot_stream[s]], preferred_element_type=f32)  13.9 us
    dot_general x7, matrix products, tp_device(): jnp.einsum('nt,kt->nk', low[s], normed[slot_stream[s]], preferred_element...  10.7 us
  transfers between devices with their start and end apart: 5, of which 2 were waited for; matrix products, arithmetic and copies ran while one was open for 16% of the time, Pallas kernels for 0%

profile of v2, /device:TPU:0, one launch (start us, length us, event | category | flops | bytes accessed | tf_op | source)
XLA Modules:
  0.0 432.0 jit_solution(10221441874045054956)
XLA Ops:
  8.1 79.8 %front.1 = (bf16[4,1024,1024]{2,1,0:T(8,128)(2,1)}, bf16[1024,1024]{1,0:T(8,128)(2,1)}, bf16[1024,640]{1,0:T(8,128)(2,1)}, f32[8,40,128]{2,1,0:T(8,128)}, f32[48...) custom-call(bf16[9,128,1024]{2,1,0:T(8,128)(2,1)} %hist.1, ...), custom_call_target="tpu_custom_call" | custom-call | tf_op jit(solution)/shard_map/front/pallas_call | solution.py:614
  89.8 3.0 fusion.63
  92.8 3.1 fusion.69
  95.8 2.8 fusion.75
  103.6 2.3 broadcast_add_fusion
  106.1 1.8 copy-done.2
  115.0 3.3 fusion.13
  118.3 5.1 %multiply_add_fusion = (f32[4,128,1024]{2,1,0:T(8,128)S(1)}, f32[4,128,1024]{2,1,0:T(8,128)S(1)}) fusion(f32[5,128,1024]{2,1,0:T(8,128)S(1)} %fusion.13, f32[7,128,1024]{2,1,0:T(8,128)S(1)} %copy-done.3), kind=kLoop, calls=%fused_computation.71 | loop fusion | flops 37224448 | bytes 8388608 | tf_op jit(solution)/shard_map/transpose(jvp())/add_any | solution.py:23
  124.9 3.2 bitcast_convert_fusion.1
  129.3 3.4 fusion.55
  134.0 3.6 all-to-all-start
  138.9 1.9 convolution_bitcast_fusion
  140.8 2.0 multiply_reduce_fusion.18
  143.8 1.9 reshape.491
  145.8 1.9 multiply_convert_fusion.1
  164.1 3.0 fusion.54
  167.1 5.7 %convert_bitcast_fusion = bf16[3,1024,1024]{2,1,0:T(8,128)(2,1)} fusion(bf16[7,128,1024]{2,1,0:T(8,128)(2,1)S(1)} %copy-done.24, bf16[128,7,1024]{2,0,1:T(8,128)(2,1)} %param.28), kind=kOutput, calls=%fused_computation.3 | convolution fusion | flops 808452096 | bytes 8912896 | tf_op jit(solution)/shard_map/nsk,snt->skt/dot_general | solution.py:773
  172.8 6.7 %pad_maximum_fusion = bf16[4,1024,1024]{2,1,0:T(8,128)(2,1)} fusion(bf16[1,1024,1024]{2,1,0:T(8,128)(2,1)S(1)} %fusion.54, bf16[3,1024,1024]{2,1,0:T(8,128)(2,1)} %convert_bitcast_fusion), kind=kLoop, calls=%fused_computation.2 | loop fusion | flops 4194304 | bytes 16777216 | tf_op jit(solution)/shard_map/concatenate | solution.py:771
  187.5 9.8 %all_gather.6 = f32[40,1024]{1,0:T(8,128)S(1)} all-gather(f32[40,128]{1,0:T(8,128)S(1)} %slice.352), channel_id=1, replica_groups=mesh['seq'=8,'dp'=4] {'seq'}, dimensions={1}, use_global_device_ids=true | all-gather | bytes 184320 | tf_op jit(solution)/shard_map/all_gather | solution.py:690
  197.3 1.7 fusion.213
  202.8 2.3 bitcast_convert_fusion.9
  205.1 1.8 add_convert_fusion
  206.8 79.6 %all-reduce.7.cloned.1.call-done = (bf16[128,5120]{0,1:T(8,128)(2,1)}, bf16[128,7,1024]{2,0,1:T(8,128)(2,1)}) async-done(((bf16[128,5120]{0,1:T(8,128)(2,1)}, bf16[128,7,1024]{2,0,1:T(8,128)(2,1)}), (bf16[128,5120]{0,1:T(8,128)(2,1)}, bf16[128,7,1024]{2,0,1:T(8,128)(2,1)})) %all-reduce.7.cloned.1.call-update) | async-done | bytes 3145744 | tf_op jit(solution)/shard_map/psum | solution.py:744
  289.7 1.8 copy.150
  291.6 3.9 convert_element_type.257
  295.5 2.7 fusion.10
  298.7 23.8 %psum.42 = f32[2,4,1024]{2,1,0:T(4,128)S(1)} all-reduce(f32[2,4,1024]{2,1,0:T(4,128)S(1)} %pad_maximum_fusion.12), channel_id=1, replica_groups=mesh['seq'=8,'dp'=4] {'seq'}, use_global_device_ids=true, to_apply=%region_7.8 | all-reduce | flops 8192 | bytes 65536 | tf_op jit(solution)/shard_map/psum | solution.py:669
  324.9 4.3 %multiply_reduce_fusion = (f32[4,1024]{1,0:T(4,128)S(1)}, f32[4,1024]{1,0:T(4,128)S(1)}, f32[4,1024]{1,0:T(4,128)S(1)}, f32[4,1024]{1,0:T(4,128)S(1)}, f32[4,102...) fusion(f32[4,128,1024]{2,1,0:T(8,128)S(1)} %fusion.172, ...), kind=kLoop, calls=%fused_computation.53 | loop fusion | flops 17657856 | bytes 9732096 | tf_op jit(solution)/shard_map/reduce_sum | solution.py:789
  331.8 48.3 %all-reduce.5.cloned.1.call-done = f32[36,1024]{1,0:T(8,128)} async-done(((f32[36,1024]{1,0:T(8,128)}), f32[36,1024]{1,0:T(8,128)}) %all-reduce.5.cloned.1.call-update) | async-done | bytes 147472 | tf_op jit(solution)/shard_map/psum | solution.py:669
  384.0 2.0 fusion.183
  388.1 19.3 %all-reduce = (f32[1549]{0:T(1024)S(1)}, f32[53,128]{1,0:T(8,128)S(1)}) all-reduce(f32[1549]{0:T(1024)S(1)} %concatenate.58, f32[53,128]{1,0:T(8,128)S(1)} %concatenate.59), channel_id=1, replica_groups=mesh['seq'=8,'dp'=4] {'dp'}, use_global_device_ids=true, to_apply=%region_32.33 | all-reduce | flops 8333 | bytes 66664 | tf_op jit(solution)/shard_map/psum | solution.py:817
  407.4 10.5 %all_gather.7 = f32[53,1024]{1,0:T(8,128)S(1)} all-gather(f32[53,128]{1,0:T(8,128)S(1)} %get-tuple-element.143), channel_id=1, replica_groups=mesh['seq'=8,'dp'=4] {'seq'}, dimensions={1}, use_global_device_ids=true | all-gather | bytes 244224 | tf_op jit(solution)/shard_map/all_gather | solution.py:816
  (285 shorter events, 69.5 us)
Async XLA Ops:
  8.0 95.6 %copy-start = (f32[7,1024]{1,0:T(8,128)S(1)}, f32[7,1024]{1,0:T(8,128)}, u32[]{:S(2)}) copy-start(f32[7,1024]{1,0:T(8,128)} %param.29) | copy-start | bytes 86020
  8.0 197.0 %reduce-scatter.3.cloned.1.call-start = ((), (), s32[]{:S(2)}) async-start(), calls=%async_computation.3 | async-start | bytes 2359296 | tf_op jit(solution)/shard_map/reduce_scatter | solution.py:737
  8.1 81.6 %copy-start.75 = (bf16[128,7,1024]{2,0,1:T(8,128)(2,1)S(1)}, bf16[128,7,1024]{2,0,1:T(8,128)(2,1)}, u32[]{:S(2)}) copy-start(bf16[128,7,1024]{2,0,1:T(8,128)(2,1)} %param.28) | copy-start | bytes 5505028
  89.8 8.9 %copy-start.74 = (bf16[4,1024,1024]{2,1,0:T(8,128)(2,1)S(1)}, bf16[4,1024,1024]{2,1,0:T(8,128)(2,1)}, u32[]{:S(2)}) copy-start(bf16[4,1024,1024]{2,1,0:T(8,128)(2,1)} %get-tuple-element.38) | copy-start | bytes 25165828
  107.9 91.1 %copy-start.61 = (pred[1024]{0:T(1024)(128)(4,1)}, pred[1024]{0:T(1024)(128)(4,1)S(1)}, u32[]{:S(2)}) copy-start(pred[1024]{0:T(1024)(128)(4,1)S(1)} %fusion.233) | copy-start | bytes 3076
  118.3 5.1 %copy-start.13 = (f32[5,128,1024]{2,1,0:T(8,128)}, f32[5,128,1024]{2,1,0:T(8,128)S(1)}, u32[]{:S(2)}) copy-start(f32[5,128,1024]{2,1,0:T(8,128)S(1)} %fusion.13) | copy-start | bytes 7864324
  134.0 28.3 %all-to-all-start = ((bf16[8,128,5,128]{3,1,2,0:T(8,128)(2,1)}), bf16[8,128,5,128]{3,1,2,0:T(8,128)(2,1)S(1)}, u32[]{:S(2)}, u32[]{:S(2)}) async-start(bf16[8,128,5,128]{3,1,2,0:T(8,128)(2,1)} %copy.143), calls=%async_computation.2 | async-start | bytes 2621440 | tf_op jit(solution)/shard_map/all_to_all | solution.py:741
  137.6 148.8 %all-reduce.7.cloned.1.call-start = ((), (), s32[]{:S(2)}) async-start(), calls=%async_computation.6 | async-start | bytes 6291456 | tf_op jit(solution)/shard_map/psum | solution.py:744
  145.8 4.2 slice-start
  151.6 9.2 %copy-start.23 = (bf16[7,128,1024]{2,1,0:T(8,128)(2,1)}, bf16[7,128,1024]{2,1,0:T(8,128)(2,1)S(1)}, u32[]{:S(2)}) copy-start(bf16[7,128,1024]{2,1,0:T(8,128)(2,1)S(1)} %fusion.5) | copy-start | bytes 5505028
  163.8 131.7 %reduce-scatter.5.cloned.1.call-start = ((), (), s32[]{:S(2)}) async-start(), calls=%async_computation.4 | async-start | bytes 9437184 | tf_op jit(solution)/shard_map/reduce_scatter | solution.py:778
  179.5 3.5 copy-start.60
  179.5 7.4 %copy-start.73 = (s32[4]{0:T(128)S(1)}, s32[4]{0:T(128)}, u32[]{:S(2)}) copy-start(s32[4]{0:T(128)} %constant.163) | copy-start | bytes 52
  179.5 19.5 %copy-start.12 = (bf16[128,1024]{1,0:T(8,128)(2,1)S(1)}, bf16[128,1024]{1,0:T(8,128)(2,1)}, u32[]{:S(2)}) copy-start(bf16[128,1024]{1,0:T(8,128)(2,1)} %cot.1) | copy-start | bytes 786436
  179.5 20.1 %copy-start.7 = (f32[1,128,1024]{2,1,0:T(8,128)S(1)}, f32[1,128,1024]{2,1,0:T(8,128)}, u32[]{:S(2)}) copy-start(f32[1,128,1024]{2,1,0:T(8,128)} %reshape.491) | copy-start | bytes 1572868
  179.5 20.1 %copy-start.9 = (f32[2,64,1024]{2,1,0:T(8,128)S(1)}, f32[2,64,1024]{2,1,0:T(8,128)}, u32[]{:S(2)}) copy-start(f32[2,64,1024]{2,1,0:T(8,128)} %copy-done.8) | copy-start | bytes 1572868
  179.6 200.5 %all-reduce.5.cloned.1.call-start = ((), (), s32[]{:S(2)}) async-start(), calls=%async_computation.5 | async-start | bytes 327680 | tf_op jit(solution)/shard_map/psum | solution.py:669
  197.3 4.4 %copy-start.27 = (f32[40,1024]{1,0:T(8,128)}, f32[40,1024]{1,0:T(8,128)S(1)}, u32[]{:S(2)}) copy-start(f32[40,1024]{1,0:T(8,128)S(1)} %all_gather.6) | copy-start | bytes 491524
  197.3 3.8 copy-start.39
  291.5 3.9 copy-start.5
  295.4 27.0 %copy-start.11 = (bf16[4,128,1024]{2,1,0:T(8,128)(2,1)S(1)}, bf16[4,128,1024]{2,1,0:T(8,128)(2,1)}, u32[]{:S(2)}) copy-start(bf16[4,128,1024]{2,1,0:T(8,128)(2,1)} %reduce-scatter.5.cloned.1.call-done) | copy-start | bytes 3145732
  330.1 49.9 %copy-start.28 = (f32[40,1024]{1,0:T(8,128)S(1)}, f32[40,1024]{1,0:T(8,128)}, u32[]{:S(2)}) copy-start(f32[40,1024]{1,0:T(8,128)} %copy-done.27) | copy-start | bytes 491524
  330.1 49.9 %copy-start.37 = (f32[40,1024]{1,0:T(8,128)S(1)}, f32[40,1024]{1,0:T(8,128)}, u32[]{:S(2)}) copy-start(f32[40,1024]{1,0:T(8,128)} %fusion.214) | copy-start | bytes 491524
  330.1 51.3 %copy-start.59 = (f32[40,36]{0,1:T(8,128)S(1)}, f32[40,36]{0,1:T(8,128)}, u32[]{:S(2)}) copy-start(f32[40,36]{0,1:T(8,128)} %reshape.494) | copy-start | bytes 17284
  330.2 52.5 %copy-start.72 = (f32[128]{0:T(128)S(1)}, f32[128]{0:T(128)}, u32[]{:S(2)}) copy-start(f32[128]{0:T(128)} %dynamic_slice.19) | copy-start | bytes 1540
  381.2 5.8 %copy-start.38 = (f32[36,1024]{1,0:T(8,128)S(1)}, f32[36,1024]{1,0:T(8,128)}, u32[]{:S(2)}) copy-start(f32[36,1024]{1,0:T(8,128)} %all-reduce.5.cloned.1.call-done) | copy-start | bytes 442372
  381.2 5.9 %copy-start.68 = (f32[36]{0:T(128)S(1)}, f32[36]{0:T(128)}, u32[]{:S(2)}) copy-start(f32[36]{0:T(128)} %get-tuple-element.140) | copy-start | bytes 436
  381.2 5.9 %copy-start.69 = (f32[36]{0:T(128)S(1)}, f32[36]{0:T(128)}, u32[]{:S(2)}) copy-start(f32[36]{0:T(128)} %get-tuple-element.141) | copy-start | bytes 436
  381.3 6.6 %copy-start.67 = (f32[128]{0:T(128)S(1)}, f32[128]{0:T(128)}, u32[]{:S(2)}) copy-start(f32[128]{0:T(128)} %convert_reduce_fusion.1) | copy-start | bytes 1540
  381.3 6.6 %copy-start.70 = (f32[1,128]{1,0:T(1,128)S(1)}, f32[1,128]{1,0:T(1,128)}, u32[]{:S(2)}) copy-start(f32[1,128]{1,0:T(1,128)} %get-tuple-element.199) | copy-start | bytes 1540
  381.3 6.6 %copy-start.71 = (f32[1,128]{1,0:T(1,128)S(1)}, f32[1,128]{1,0:T(1,128)}, u32[]{:S(2)}) copy-start(f32[1,128]{1,0:T(1,128)} %get-tuple-element.200) | copy-start | bytes 1540
  383.9 40.9 %copy-start.1 = (f32[7,1024]{1,0:T(8,128)S(1)}, f32[7,1024]{1,0:T(8,128)}, u32[]{:S(2)}) copy-start(f32[7,1024]{1,0:T(8,128)} %param.29) | copy-start | bytes 86020
  (51 other events, 96.2 us)
Sparse Core Ops, SparseCore 0:
  128.2 44.9 reduce-scatter.2
  179.7 73.0 reduce-scatter.4
  330.2 49.7 all-reduce.4
Sparse Core Ops, SparseCore 1:
  163.9 122.5 all-reduce.6

commit v3 on v2

--- a/solution.py
+++ b/solution.py
@@ -450,7 +450,7 @@
         return pl.ds(pl.multiple_of(owner * block, block), block)
 
     gathers = [
-        Gather(at, lambda owner, s=s: nbuf.at[s, rows(owner), :], ag_send.at[s], ag_recv.at[s])
+        Gather(at, lambda owner, s=s: nbuf.at[s * n + owner], ag_send.at[s], ag_recv.at[s])
         for s in range(4)
     ]
     cots = Gather(at, lambda owner: cot_all.at[rows(owner), :], ag_send.at[4], ag_recv.at[4])
@@ -578,7 +578,7 @@
                 xhat * colp[:, 1 + which : 2 + which] + colp[:, 3 + which : 4 + which]
             ).astype(bf16)
         gathers[s].start(nown.at[s])
-        keep = pltpu.make_async_copy(nown.at[s], nbuf.at[s, mine, :], local_sem.at[6 + s])
+        keep = pltpu.make_async_copy(nown.at[s], nbuf.at[s * n + me], local_sem.at[6 + s])
         keep.start()
         keeps.append(keep)
     st3[...] = streams[3]
@@ -614,7 +614,7 @@
     return pl.pallas_call(
         functools.partial(front_kernel, n),
         out_shape=(
-            shape((4, width, tokens), bf16),
+            shape((4 * n, feats, tokens), bf16),
             shape((width, tokens), bf16),
             shape((width, 5 * feats), bf16),
             shape((n, 40, block), f32),
@@ -650,186 +650,737 @@
     )
 
 
+def back_kernel(
+    n, zn,
+    nbuf, cot_all, cols_in, history, scaled_in,
+    w_in, pk, raw, st3, stat, gain, gin, gout, ng, in_bias, out_bias,
+    new_state, hist_grad, totals,
+    bias_tot, ngain_tot, nbias_tot, gain_tot, outb_tot, gin_tot, gout_tot,
+    gbias_tot, mean_tot, var_tot,
+    big, cot, cols, prm, colp, qkv, act, deriv, probs, gattn, gp, gcol, rope, accs, gn,
+    ybuf, abuf, from_a, from_b, zown, zin, zmid,
+    gsum, gsum_in, gmix, gmix_in, pre, genmsg, gen_in_all, vec, vec_z, vec_sum, vec_all,
+    load_sem, rs_send, rs_recv, ex_send, ex_recv, z_send, z_recv, out_sem,
+):
+    f32, bf16 = jnp.float32, jnp.bfloat16
+    states = history.shape[0]
+    feats, tokens = st3.shape
+    block = tokens // n
+    width = n * feats
+    hid = gin.shape[0]
+    heads = feats // HEAD_DIM
+    scale = HEAD_DIM ** (-0.5)
+    m = 4 * states
+    wide = 2 * block
+    chunks = tokens // wide
+    at = Links(n)
+    me = at.me
+    zc = lax.axis_index("dp")
+
+    def rows(owner):
+        return pl.ds(pl.multiple_of(owner * feats, feats), feats)
+
+    def lanes(index, size=block):
+        return pl.ds(pl.multiple_of(index * size, size), size)
+
+    loads = [
+        pltpu.make_async_copy(
+            nbuf.at[pl.ds(s * n, n)], big.at[pl.ds(s * n, n)], load_sem.at[s]
+        )
+        for s in range(4)
+    ]
+    loads.append(pltpu.make_async_copy(cot_all, cot, load_sem.at[4]))
+    loads.append(pltpu.make_async_copy(cols_in, cols, load_sem.at[5]))
+    for index in (0, 1, 2, 3, 5, 4):
+        loads[index].start()
+    load_scaled = pltpu.make_async_copy(scaled_in, deriv, load_sem.at[6])
+    load_hist = pltpu.make_async_copy(history, big.at[pl.ds(0, states)], load_sem.at[7])
+
+    barrier = pltpu.get_barrier_semaphore()
+    for k in range(1, n):
+        pl.semaphore_signal(
+            barrier, inc=1, device_id={"seq": (me + k) % n}, device_id_type=MESH
+        )
+    for k in range(1, zn):
+        pl.semaphore_signal(
+            barrier, inc=1, device_id={"dp": (zc + k) % zn}, device_id_type=MESH
+        )
+
+    prm[...] = jnp.zeros_like(prm)
+    prm[0:1, :] = gain[:, rows(me)]
+    prm[1:3, :] = ng[:, rows(me)]
+    prm[3:4, :] = out_bias[:, rows(me)]
+    prm[8:15, :] = in_bias[:, rows(me)]
+    colp[...] = prm[...].T
+    accs[...] = jnp.zeros_like(accs)
+
+    spot = lax.broadcasted_iota(jnp.int32, (1, block), 1).astype(f32)
+    freq = jnp.exp(
+        lax.broadcasted_iota(jnp.int32, (8, block), 0).astype(f32)
+        * (-2.0 * math.log(10000.0) / ROT)
+    )
+
+    def place(owner, index):
+        cut = pk[owner, m + 1 : m + 2, :]
+        second = index >= cut
+        position = index - jnp.where(second, cut, 0.0)
+        limit = jnp.where(second, pk[owner, m + 3 : m + 4, :], pk[owner, m + 2 : m + 3, :])
+        return second, position, position < limit
+
+    for b in range(n):
+        where = pl.ds(b * block, block)
+        _, position, valid = place(b, spot)
+        angle = freq * position
+        rope[0:8, where] = jnp.cos(angle)
+        rope[8:16, where] = jnp.sin(angle)
+        rope[16:17, where] = jnp.where(valid, 1.0, 0.0)
+
+    def rotated(value, where, sign):
+        cosine, sine = rope[0:8, where], rope[8:16, where] * sign
+        out = []
+        for h in range(heads):
+            base = h * HEAD_DIM
+            former, latter = value[base : base + 8], value[base + 8 : base + 16]
+            out += [
+                former * cosine - latter * sine,
+                latter * cosine + former * sine,
+                value[base + 16 : base + HEAD_DIM],
+            ]
+        return jnp.concatenate(out, axis=0)
+
+    def stream(s, where):
+        return big[pl.ds(s * n, n), :, where].reshape(width, -1)
+
+    for s in range(3):
+        loads[s].wait()
+
+        @pl.loop(0, chunks)
+        def _(c, s=s):
+            where = lanes(c, wide)
+            value = jnp.dot(w_in[s], stream(s, where), preferred_element_type=f32)
+            value = value + colp[:, 8 + s : 9 + s]
+            if s < 2:
+                value = rotated(value, where, 1.0)
+            if s == 0:
+                value = value * scale
+            qkv[s, :, where] = value.astype(bf16)
+
+    loads[3].wait()
+    for j in range(4):
+
+        @pl.loop(0, chunks)
+        def _(c, j=j):
+            where = lanes(c, wide)
+            value = jnp.dot(w_in[3 + j], stream(3, where), preferred_element_type=f32)
+            up, slope = gelu_pair(value + colp[:, 11 + j : 12 + j])
+            act[pl.ds((1 + j) * feats, feats), where] = up.astype(bf16)
+            deriv[j, :, where] = slope
+
+    key_at = lax.broadcasted_iota(jnp.int32, (block, block), 0).astype(f32)
+    query_at = lax.broadcasted_iota(jnp.int32, (block, block), 1).astype(f32)
+
+    @pl.loop(0, n)
+    def _(b):
+        where = lanes(b)
+        cut = pk[b, m + 1 : m + 2, :]
+        _, _, valid = place(b, key_at)
+        same = jnp.where(key_at >= cut, 1.0, 0.0) == jnp.where(query_at >= cut, 1.0, 0.0)
+        allowed = same & (key_at <= query_at) & valid
+        for h in range(heads):
+            part = pl.ds(h * HEAD_DIM, HEAD_DIM)
+            scores = contract(qkv[1, part, where], qkv[0, part, where], 0, 0)
+            scores = jnp.where(allowed, scores, masked_score)
+            weights = jnp.exp(scores - jnp.max(scores, axis=0, keepdims=True))
+            soft = weights * (1.0 / jnp.sum(weights, axis=0, keepdims=True))
+            probs[b * heads + h] = soft
+            act[part, where] = jnp.dot(
+                qkv[2, part, where], soft.astype(bf16), preferred_element_type=f32
+            ).astype(bf16)
+
+    def rs_copy(i, src, dst, slot, to):
+        return at.copy(src, dst, rs_send.at[i, slot], rs_recv.at[i, slot], to)
+
+    def rs_first(i):
+        return [
+            rs_copy(i, ybuf.at[i, rows(owner), :], abuf.at[i, q], q, at.p)
+            for q, owner in enumerate((at.p, at.pa, at.pb, at.pdg))
+        ]
+
+    def rs_second(i):
+        return [
+            rs_copy(i, ybuf.at[i, rows(at.a), :], from_a.at[i, 0], 4, at.a),
+            rs_copy(i, ybuf.at[i, rows(at.dg), :], from_a.at[i, 1], 5, at.a),
+        ]
+
+    def rs_third(i):
+        return [rs_copy(i, ybuf.at[i, rows(at.b), :], from_b.at[i], 6, at.b)]
+
+    def rs_start(i):
+        for copy in rs_first(i):
+            copy.start()
+
+    def rs_fold(i):
+        for copy in rs_first(i):
+            copy.wait_recv()
+
+        @pl.loop(0, chunks)
+        def _(c):
+            where = lanes(c, wide)
+            for q, owner in ((1, at.a), (3, at.dg)):
+                ybuf[i, rows(owner), where] = (
+                    ybuf[i, rows(owner), where].astype(f32) + abuf[i, q, :, where].astype(f32)
+                ).astype(bf16)
+
+        for copy in rs_second(i):
+            copy.start()
+
+    def rs_pass(i):
+        for copy in rs_second(i):
+            copy.wait_recv()
+
+        @pl.loop(0, chunks)
+        def _(c):
+            where = lanes(c, wide)
+            ybuf[i, rows(at.b), where] = (
+                ybuf[i, rows(at.b), where].astype(f32)
+                + abuf[i, 2, :, where].astype(f32)
+                + from_a[i, 1, :, where].astype(f32)
+            ).astype(bf16)
+
+        for copy in rs_third(i):
+            copy.start()
+
+    def rs_end(i):
+        for copy in rs_third(i):
+            copy.wait_recv()
+
+    def rs_value(i, where):
+        return (
+            ybuf[i, rows(me), where].astype(f32)
+            + abuf[i, 0, :, where].astype(f32)
+            + from_a[i, 0, :, where].astype(f32)
+            + from_b[i, :, where].astype(f32)
+        )
+
+    def rs_drain(i):
+        for copy in rs_first(i) + rs_second(i) + rs_third(i):
+            copy.wait_send()
+
+    outer = (zc == 0) | (zc == 3)
+    z_in = 1 + zc // 3
+    z_out = 3 * (zc - 1)
+    z_over = 3 - zc
+
+    def z_copy(c, src, dst, slot, recv_slot, to):
+        return pltpu.make_async_remote_copy(
+            src_ref=src, dst_ref=dst, send_sem=z_send.at[c, slot], recv_sem=z_recv.at[c, recv_slot],
+            device_id={"dp": to}, device_id_type=MESH,
+        )
+
+    def z_up(c):
+        return z_copy(c, zown.at[c], zin.at[c], 0, 0, z_in)
+
+    def z_cross(c):
+        return z_copy(c, zown.at[c], zmid.at[c], 1, 1, z_over)
+
+    def z_down(c):
+        return z_copy(c, zin.at[c], zin.at[c], 2, 0, z_out)
+
+    def z_start(c):
+        if zn > 1:
+
+            @pl.when(outer)
+            def _():
+                z_up(c).start()
+
+    def z_fold(c):
+        if zn > 1:
+
+            @pl.when(jnp.logical_not(outer))
+            def _():
+                z_up(c).wait_recv()
+
+                @pl.loop(0, chunks)
+                def _(k):
+                    where = lanes(k, wide)
+                    zown[c, :, where] = (
+                        zown[c, :, where].astype(f32) + zin[c, :, where].astype(f32)
+                    ).astype(bf16)
+
+                z_cross(c).start()
+
+    stages = []
+
+    def z_end(c):
+        if zn > 1:
+
+            @pl.when(jnp.logical_not(outer))
+            def _():
+                z_cross(c).wait_recv()
+
+                @pl.loop(0, chunks)
+                def _(k):
+                    where = lanes(k, wide)
+                    zin[c, :, where] = (
+                        zown[c, :, where].astype(f32) + zmid[c, :, where].astype(f32)
+                    ).astype(bf16)
+
+                z_down(c).start()
+
+            @pl.when(outer)
+            def _():
+                z_up(c).wait_recv()
+
+        source = zin if zn > 1 else zown
+        stages.append(pltpu.make_async_copy(source.at[c], totals.at[c], out_sem.at[c]))
+        stages[-1].start()
+
+    def z_drain(c):
+        if zn > 1:
+
+            @pl.when(outer)
+            def _():
+                z_up(c).wait_send()
+
+            @pl.when(jnp.logical_not(outer))
+            def _():
+                z_cross(c).wait_send()
+                z_down(c).wait_send()
+
+    loads[5].wait()
+    quarter = width // 4
+
+    @pl.loop(0, chunks)
+    def _(c):
+        where = lanes(c, wide)
+        for r in range(4):
+            part = slice(r * quarter, (r + 1) * quarter)
+            ybuf[4, part, where] = jnp.dot(
+                cols[part, :], act[:, where], preferred_element_type=f32
+            ).astype(bf16)
+
+    pl.semaphore_wait(barrier, n - 1 + zn - 1)
+    rs_start(4)
+
+    loads[4].wait()
+
+    @pl.loop(0, n)
+    def _(b):
+        where = lanes(b)
+        mask = rope[16:17, where].astype(bf16)
+        cot[:, where] = cot[:, where] * mask
+
+    for j in range(5):
+        gn[0] = contract(cols[:, j * feats : (j + 1) * feats], cot[...], 0, 0)
+
+        @pl.loop(0, chunks)
+        def _(c, j=j):
+            where = lanes(c, wide)
+            value = gn[0, :, where]
+            if j == 0:
+                gattn[:, where] = value.astype(bf16)
+            else:
+                value = value * deriv[j - 1, :, where]
+                accs[2 + j] = accs[2 + j] + (value[:, :block] + value[:, block:])
+                gp[pl.ds((2 + j) * feats, feats), where] = value.astype(bf16)
+
+    load_scaled.start()
+    for r in range(4):
+        grads = contract(cot[r * quarter : (r + 1) * quarter, :], act[...], 1, 1).astype(bf16)
+        for j in range(5):
+            gcol[j, r * quarter : (r + 1) * quarter, :] = grads[:, j * feats : (j + 1) * feats]
+
+    turns = Everyone(
+        at,
+        lambda to: gcol.at[:, rows(to), :],
+        lambda k: zown.at[pl.ds(7, 5), :, rows(me)],
+        lambda k, origin: zown.at[pl.ds(7, 5), :, rows(origin)],
+        ex_send.at[0], ex_recv.at[0],
+    )
+    turns.start()
+    keep = pltpu.make_async_copy(
+        gcol.at[:, rows(me), :], zown.at[pl.ds(7, 5), :, rows(me)], load_sem.at[8]
+    )
+    keep.start()
+
+    def normed_grad(i, first, count):
+        @pl.loop(0, n)
+        def _(r):
+            weight = jnp.concatenate(
+                [w_in[first + s, :, lanes(r, feats)] for s in range(count)], axis=0
+            )
+            ybuf[i, rows(r), :] = contract(
+                weight, gp[first * feats : (first + count) * feats, :], 0, 0
+            ).astype(bf16)
+
+        rs_start(i)
+
+    def weight_grad(s, source):
+        @pl.loop(0, 4)
+        def _(r):
+            part = big[pl.ds(source * n + r * (n // 4), n // 4), :, :].reshape(quarter, tokens)
+            zown[s, :, lanes(r, quarter)] = contract(
+                gp[s * feats : (s + 1) * feats, :], part, 1, 1
+            ).astype(bf16)
+
+        z_start(s)
+
+    normed_grad(3, 3, 4)
+    for s in range(3, 7):
+        weight_grad(s, 3)
+    rs_fold(4)
+
+    @pl.loop(0, n)
+    def _(b):
+        where = lanes(b)
+        grads = [[], [], []]
+        for h in range(heads):
+            part = pl.ds(h * HEAD_DIM, HEAD_DIM)
+            soft = probs[b * heads + h]
+            grad = gattn[part, where]
+            grads[2].append(contract(grad, soft.astype(bf16), 1, 1))
+            dprob = contract(qkv[2, part, where], grad, 0, 0)
+            inner = jnp.sum(soft * dprob, axis=0, keepdims=True)
+            low = (soft * (dprob - inner)).astype(bf16)
+            grads[0].append(
+                jnp.dot(qkv[1, part, where], low, preferred_element_type=f32) * scale
+            )
+            grads[1].append(contract(qkv[0, part, where], low, 1, 1))
+        for s in range(3):
+            value = jnp.concatenate(grads[s], axis=0)
+            if s < 2:
+                value = rotated(value, where, -1.0)
+            accs[s] = accs[s] + value
+            gp[pl.ds(s * feats, feats), where] = value.astype(bf16)
+
+    rs_fold(3)
+    rs_pass(4)
+    for s in range(3):
+        normed_grad(s, s, 1)
+    z_fold(3)
+    for k in range(1, n):
+        turns.wait(k)
+    keep.wait()
+    for c in range(7, 12):
+        z_start(c)
+    for s in range(3):
+        weight_grad(s, s)
+    load_hist.start()
+    rs_fold(0)
+    z_fold(4)
+    rs_pass(3)
+    rs_fold(1)
+    z_fold(5)
+    rs_pass(0)
+    rs_fold(2)
+    z_fold(6)
+    rs_pass(1)
+    z_end(3)
+    rs_end(4)
+
+    @pl.loop(0, n)
+    def _(b):
+        where = lanes(b)
+        new_state[:, where] = (st3[:, where] + rs_value(4, where) + colp[:, 3:4]).astype(bf16)
+
+    rs_pass(2)
+    z_fold(7)
+    z_end(4)
+    load_scaled.wait()
+
+    def norm_sums(s):
+        which = 0 if s < 3 else 1
+
+        @pl.loop(0, n)
+        def _(b):
+            where = lanes(b)
+            value = rs_value(s, where)
+            xhat = deriv[s, :, where]
+            along = value * xhat
+            accs[7 + which] = accs[7 + which] + along
+            accs[9 + which] = accs[9 + which] + value
+            factor = colp[:, 1 + which : 2 + which]
+            gn[s, :, where] = value * factor
+            gsum[s : s + 1, where] = jnp.sum(value * factor, axis=0, keepdims=True)
+            gsum[4 + s : 5 + s, where] = jnp.sum(along * factor, axis=0, keepdims=True)
+
+    for s in (3, 0, 1, 2):
+        rs_end(s)
+        norm_sums(s)
+    sums = Everyone(
+        at, lambda to: gsum, lambda k: gsum_in.at[me], lambda k, origin: gsum_in.at[origin],
+        ex_send.at[1], ex_recv.at[1],
+    )
+    sums.start()
+    z_fold(8)
+    z_end(5)
+    load_hist.wait()
+    for k in range(1, n):
+        sums.wait(k)
+    gsum_in[me] = gsum[...]
+    total = gsum_in[0]
+    for k in range(1, n):
+        total = total + gsum_in[k]
+    pre[0:8, :] = total * (1.0 / width)
+
+    @pl.loop(0, n)
+    def _(b):
+        where = lanes(b)
+        for s in range(4):
+            xhat = deriv[s, :, where]
+            value = stat[4 + s : 5 + s, where] * (
+                gn[s, :, where] - pre[s : s + 1, where] - xhat * pre[4 + s : 5 + s, where]
+            )
+            if s == 3:
+                direct = cot[rows(me), where].astype(f32)
+                accs[12] = accs[12] + direct
+                value = value + direct
+            gn[s, :, where] = value
+        for j in range(states):
+            past = big[j, :, where].astype(f32)
+            for s in range(4):
+                gmix[b, 4 * j + s : 4 * j + s + 1, :] = jnp.sum(
+                    gn[s, :, where] * past, axis=0, keepdims=True
+                )
+
+    mixes = Everyone(
+        at, lambda to: gmix.at[to], lambda k: gmix_in.at[k], lambda k, origin: gmix_in.at[k],
+        ex_send.at[2], ex_recv.at[2],
+    )
+    mixes.start()
+    z_fold(9)
+    z_end(6)
+
+    @pl.loop(0, n)
+    def _(b):
+        where = lanes(b)
+        for j in range(states - 1):
+            value = pk[b, pl.ds(4 * j, 1), :] * gn[0, :, where]
+            for s in range(1, 4):
+                value = value + pk[b, pl.ds(4 * j + s, 1), :] * gn[s, :, where]
+            hist_grad[j, :, where] = value.astype(bf16)
+
+    total = gmix[me]
+    for k in range(1, n):
+        mixes.wait(k)
+        total = total + gmix_in[k]
+    grad_mix = total[0:m]
+    table = jnp.concatenate([gout[j] for j in range(states)], axis=0)
+    hidden, slope = gelu_pair(raw[0:hid, :] * pk[me, m : m + 1, :])
+    grad_hidden = contract(table, grad_mix, 0, 0, precision=highest)
+    low = (grad_hidden * slope).astype(bf16).astype(f32)
+    genmsg[0:hid, :] = low
+    genmsg[hid : hid + 8, :] = jnp.broadcast_to(
+        jnp.sum(low * raw[0:hid, :], axis=0, keepdims=True) * (1.0 / width), (8, block)
+    )
+    owns = Everyone(
+        at, lambda to: genmsg, lambda k: gen_in_all.at[me], lambda k, origin: gen_in_all.at[origin],
+        ex_send.at[3], ex_recv.at[3],
+    )
+    owns.start()
+    z_fold(10)
+    z_end(7)
+    _, _, valid = place(me, spot)
+    kept = jnp.where(valid, 1.0, 0.0)
+    ones = jnp.ones((8, block), f32)
+    mixing = pk[me, 0:m, :]
+    vec[...] = jnp.zeros_like(vec)
+    vec[56 : 56 + hid, 0:m] = contract(hidden, grad_mix, 1, 1, precision=highest)
+    for index, value in enumerate((grad_mix, mixing * kept, mixing * mixing * kept)):
+        vec[96 + index : 97 + index, 0:m] = contract(ones, value, 1, 1, precision=highest)[0:1]
+    vec[99:100, :] = jnp.broadcast_to(jnp.sum(kept, axis=1, keepdims=True), (1, block))
+    gen_in_all[me] = genmsg[...]
+    for k in range(1, n):
+        owns.wait(k)
+    gin_mine = gin[:, rows(me)]
+
+    @pl.loop(0, n)
+    def _(b):
+        where = lanes(b)
+        low_b = gen_in_all[b, 0:hid, :].astype(bf16)
+        rms = pk[b, m : m + 1, :]
+        last = big[states - 1, :, where].astype(f32)
+        grad_gen = contract(gin_mine, low_b, 0, 0)
+        accs[11] = accs[11] + grad_gen * last * rms
+        normed = (last * rms * colp[:, 0:1]).astype(bf16)
+        vec[16 : 16 + hid, :] = vec[16 : 16 + hid, :] + contract(low_b, normed, 1, 1)
+        value = rms * grad_gen * colp[:, 0:1]
+        value = value - last * (rms * rms * rms * gen_in_all[b, hid : hid + 1, :])
+        for s in range(4):
+            value = value + pk[b, pl.ds(4 * (states - 1) + s, 1), :] * gn[s, :, where]
+        hist_grad[states - 1, :, where] = value.astype(bf16)
+
+    prm[...] = jnp.zeros_like(prm)
+    for index in range(13):
+        prm[:, index : index + 1] = jnp.sum(accs[index], axis=1, keepdims=True)
+    vec[0:16, :] = prm[...].T[0:16]
+    for k in range(1, zn):
+        pltpu.make_async_remote_copy(
+            src_ref=vec, dst_ref=vec_z.at[zc], send_sem=ex_send.at[4, k], recv_sem=ex_recv.at[4, k],
+            device_id={"dp": (zc + k) % zn}, device_id_type=MESH,
+        ).start()
+    z_fold(11)
+    z_end(8)
+    vec_z[zc] = vec[...]
+    for k in range(1, zn):
+        place_z = vec_z.at[(zc + zn - k) % zn]
+        pltpu.make_async_remote_copy(
+            src_ref=place_z, dst_ref=place_z, send_sem=ex_send.at[4, k], recv_sem=ex_recv.at[4, k],
+            device_id={"dp": (zc + k) % zn}, device_id_type=MESH,
+        ).wait()
+    total = vec_z[0]
+    for k in range(1, zn):
+        total = total + vec_z[k]
+    vec_sum[...] = total
+    vec_all[me] = total
+    alls = Everyone(
+        at, lambda to: vec_sum, lambda k: vec_all.at[me], lambda k, origin: vec_all.at[origin],
+        ex_send.at[5], ex_recv.at[5],
+    )
+    alls.start()
+    z_fold(2)
+    z_fold(1)
+    z_end(9)
+    z_end(10)
+    for k in range(1, n):
+        alls.wait(k)
+    shared = vec_all[0, 56:104, :]
+    for k in range(1, n):
+        shared = shared + vec_all[k, 56:104, :]
+    prm[...] = jnp.zeros_like(prm)
+    prm[0:40, :] = shared[0:40]
+    count = shared[43:44, 0:1]
+    mean = shared[41:42] / count
+    prm[40:41, :] = shared[40:41]
+    prm[41:42, :] = mean
+    prm[42:43, :] = shared[42:43] / count - mean * mean
+    turned = prm[...].T
+    for j in range(states):
+        gout_tot[j] = turned[4 * j : 4 * j + 4, 0:hid]
+        gbias_tot[:, j : j + 1] = turned[4 * j : 4 * j + 4, 40:41]
+        mean_tot[:, j : j + 1] = turned[4 * j : 4 * j + 4, 41:42]
+        var_tot[:, j : j + 1] = turned[4 * j : 4 * j + 4, 42:43]
+    for k in range(n):
+        where = pl.ds(k * feats, feats)
+        bias_tot[:, where] = vec_all[k, 0:7, :]
+        ngain_tot[:, where] = vec_all[k, 7:9, :]
+        nbias_tot[:, where] = vec_all[k, 9:11, :]
+        gain_tot[:, where] = vec_all[k, 11:12, :]
+        outb_tot[:, where] = vec_all[k, 12:13, :]
+        gin_tot[:, where] = vec_all[k, 16 : 16 + hid, :]
+    z_fold(0)
+    z_end(11)
+    for c in (2, 1, 0):
+        z_end(c)
+    for c in range(12):
+        z_drain(c)
+    for i in range(5):
+        rs_drain(i)
+    for exchange in (turns, sums, mixes, owns, alls):
+        exchange.drain()
+    for copy in stages:
+        copy.wait()
+
+
+def back(n, zn, nbuf, cot_all, cols, pk, raw, scaled, st3, stat, history, gen_gain, gen_in, gen_out, norm_gain, in_bias, out_bias, w_in):
+    f32, bf16 = jnp.float32, jnp.bfloat16
+    states, feats, tokens = history.shape
+    block = tokens // n
+    width = n * feats
+    hid = gen_in.shape[1]
+    heads = feats // HEAD_DIM
+    vmem = pl.BlockSpec(memory_space=pltpu.VMEM)
+    anys = pl.BlockSpec(memory_space=pl.ANY)
+    shape = jax.ShapeDtypeStruct
+    dma = pltpu.SemaphoreType.DMA
+    return pl.pallas_call(
+        functools.partial(back_kernel, n, zn),
+        out_shape=(
+            shape((feats, tokens), bf16),
+            shape((states, feats, tokens), bf16),
+            shape((12, feats, width), bf16),
+            shape((7, width), f32),
+            shape((2, width), f32),
+            shape((2, width), f32),
+            shape((1, width), f32),
+            shape((1, width), f32),
+            shape((hid, width), f32),
+            shape((states, 4, hid), f32),
+            shape((4, states), f32),
+            shape((4, states), f32),
+            shape((4, states), f32),
+        ),
+        in_specs=[anys] * 5 + [vmem] * 11,
+        out_specs=(vmem, vmem, anys) + (vmem,) * 10,
+        scratch_shapes=[
+            pltpu.VMEM((4 * n, feats, tokens), bf16),
+            pltpu.VMEM((width, tokens), bf16),
+            pltpu.VMEM((width, 5 * feats), bf16),
+            pltpu.VMEM((feats, feats), f32),
+            pltpu.VMEM((feats, feats), f32),
+            pltpu.VMEM((3, feats, tokens), bf16),
+            pltpu.VMEM((5 * feats, tokens), bf16),
+            pltpu.VMEM((4, feats, tokens), f32),
+            pltpu.VMEM((n * heads, block, block), f32),
+            pltpu.VMEM((feats, tokens), bf16),
+            pltpu.VMEM((7 * feats, tokens), bf16),
+            pltpu.VMEM((5, width, feats), bf16),
+            pltpu.VMEM((24, tokens), f32),
+            pltpu.VMEM((13, feats, block), f32),
+            pltpu.VMEM((4, feats, tokens), f32),
+            pltpu.VMEM((5, width, tokens), bf16),
+            pltpu.VMEM((5, 4, feats, tokens), bf16),
+            pltpu.VMEM((5, 2, feats, tokens), bf16),
+            pltpu.VMEM((5, feats, tokens), bf16),
+            pltpu.VMEM((12, feats, width), bf16),
+            pltpu.VMEM((12, feats, width), bf16),
+            pltpu.VMEM((12, feats, width), bf16),
+            pltpu.VMEM((8, tokens), f32),
+            pltpu.VMEM((n, 8, tokens), f32),
+            pltpu.VMEM((n, 40, block), f32),
+            pltpu.VMEM((n, 40, block), f32),
+            pltpu.VMEM((8, tokens), f32),
+            pltpu.VMEM((hid + 8, block), f32),
+            pltpu.VMEM((n, hid + 8, block), f32),
+            pltpu.VMEM((104, feats), f32),
+            pltpu.VMEM((zn, 104, feats), f32),
+            pltpu.VMEM((104, feats), f32),
+            pltpu.VMEM((n, 104, feats), f32),
+            dma((9,)), dma((5, 7)), dma((5, 7)), dma((6, n)), dma((6, n)),
+            dma((12, 3)), dma((12, 2)), dma((12,)),
+        ],
+        compiler_params=pltpu.CompilerParams(
+            collective_id=2, has_side_effects=True, vmem_limit_bytes=67043328
+        ),
+        name="back",
+    )(
+        nbuf, cot_all, cols, history, scaled,
+        w_in.transpose(1, 0, 2), pk, raw, st3, stat, gen_gain.reshape(1, width), gen_in.T,
+        gen_out.transpose(2, 1, 0), norm_gain, in_bias, out_bias.reshape(1, width),
+    )
+
+
 def tp_device(
     history, cotangent, bucket_len, valid_len, gen_gain, gen_in, gen_out, gen_bias,
     norm_gain, norm_bias, w_in, in_bias, w_out, w_down, out_bias,
 ):
-    f32, bf16 = jnp.float32, jnp.bfloat16
-    n = lax.axis_size("seq")
-    me = lax.axis_index("seq")
-    states, feats, tokens = history.shape
-    width = n * feats
-    block = tokens // n
-    heads = feats // HEAD_DIM
-
-    def local(array, axis):
-        return lax.dynamic_slice_in_dim(array, me * feats, feats, axis)
-
-    def sum_feats(part):
-        return lax.psum(part, "seq")
-
-    normed, cot_all, cols, pk, own, scaled, stream3, stat = front(
+    n, zn = lax.axis_size("seq"), lax.axis_size("dp")
+    nbuf, cot_all, cols, pk, raw, scaled, st3, stat = front(
         n, history, cotangent, bucket_len, valid_len, gen_gain, gen_in, gen_out, gen_bias,
         norm_gain, norm_bias, w_out, w_down,
     )
-    cols = cols.reshape(width, 5, feats)
-    m = 4 * states
-    hid = gen_out.shape[0]
-    index = jnp.arange(block, dtype=jnp.int32)[None, :].astype(f32)
-    second = index >= pk[:, m + 1]
-    position = index - jnp.where(second, pk[:, m + 1], 0.0)
-    valid = position < jnp.where(second, pk[:, m + 3], pk[:, m + 2])
-    valid_float = valid.reshape(tokens).astype(f32)
-    grad_out = jnp.where(valid.reshape(1, tokens), cot_all, jnp.zeros_like(cot_all))
-    grad_out_local = jnp.where(valid.reshape(1, tokens), cotangent, jnp.zeros_like(cotangent))
-    last = history[states - 1].astype(f32)
-    gain_l = local(gen_gain, 0)[:, None]
-    gen_in_l = local(gen_in, 0)
-    mixing = jnp.swapaxes(pk[:, :m], 0, 1).reshape(m, tokens)
-    rms = pk[:, m].reshape(1, tokens)
-    raw = lax.all_gather(own[:hid], "seq", axis=1, tiled=True)
-    gen_pre = raw * rms
-    gen_hidden, gen_pull = jax.vjp(gelu_exact, gen_pre)
-    out_flat = gen_out.transpose(0, 2, 1).reshape(hid, m)
-    weighted = mixing * valid_float
-    stat_sums = jnp.sum(weighted, axis=1)
-    stat_squares = jnp.sum(weighted * mixing, axis=1)
-    stat_count = jnp.sum(valid_float)
-    mix = mixing.reshape(states, 4, 1, tokens).swapaxes(0, 1)
-    streams = [None, None, None, stream3]
-    inverse = stat[4:, None]
-    which = jnp.array([0, 0, 0, 1])
-    ng = local(norm_gain, 1)[which][:, :, None]
-    slot_stream = [0, 1, 2, 3, 3, 3, 3]
-    proj = jnp.stack(
-        [jnp.dot(w_in[:, s], normed[slot_stream[s]], preferred_element_type=f32) for s in range(7)]
-    ) + local(in_bias, 1)[:, :, None]
-    cosine, sine = rotary_tables(position.reshape(tokens))
-    cosine, sine = cosine.T, sine.T
-
-    def rot(value, sine):
-        value = value.reshape(heads, HEAD_DIM, tokens)
-        a, b, rest = value[:, :8], value[:, 8:16], value[:, 16:]
-        return jnp.concatenate([a * cosine - b * sine, b * cosine + a * sine, rest], axis=1)
-
-    scale = HEAD_DIM ** (-0.5)
-    shape = (heads, HEAD_DIM, n, block)
-    queries = (rot(proj[0], sine) * scale).astype(bf16).reshape(shape)
-    keys = rot(proj[1], sine).astype(bf16).reshape(shape)
-    values = proj[2].astype(bf16).reshape(shape)
-    ar = jnp.arange(block, dtype=jnp.int32)
-    allowed = (
-        (second[:, :, None] == second[:, None, :])
-        & (ar[:, None] <= ar[None, :])
-        & valid[:, :, None]
-    )
-    scores = jnp.einsum("hdbk,hdbq->hbkq", keys, queries, preferred_element_type=f32)
-    scores = jnp.where(allowed, scores, masked_score)
-    top = jnp.max(scores, axis=2, keepdims=True)
-    weights = jnp.exp(scores - top)
-    probs = jnp.where(allowed, weights / jnp.sum(weights, axis=2, keepdims=True), 0.0)
-    probs_low = probs.astype(bf16)
-    attended = jnp.einsum("hdbk,hbkq->hdbq", values, probs_low, preferred_element_type=f32)
-    attn_low = attended.astype(bf16).reshape(feats, tokens)
-    gelu_up, up_pull = jax.vjp(gelu_exact, proj[3:])
-    act = jnp.concatenate([attn_low[None], gelu_up.astype(bf16)], axis=0)
-    branch = jnp.einsum("njk,jkt->nt", cols, act, preferred_element_type=f32)
-    branch = lax.psum_scatter(branch.astype(bf16), "seq", scatter_dimension=0, tiled=True)
-    new_state = (streams[3] + branch.astype(f32) + local(out_bias, 0)[:, None]).astype(bf16)
-    back = jnp.einsum("njk,nt->jkt", cols, grad_out, preferred_element_type=f32)
-    col_grads = jnp.einsum("nt,jkt->njk", grad_out, act, preferred_element_type=f32).astype(bf16)
-    row_grads = lax.all_to_all(
-        col_grads.reshape(n, feats, 5, feats), "seq", split_axis=0, concat_axis=3, tiled=True
-    ).reshape(feats, 5 * width)
-    row_grads = lax.psum(row_grads, "dp").astype(f32)
-    grad_attn = back[0].astype(bf16).reshape(shape)
-    grad_values = jnp.einsum("hbkq,hdbq->hdbk", probs_low, grad_attn, preferred_element_type=f32)
-    dprob = jnp.einsum("hdbk,hdbq->hbkq", values, grad_attn, preferred_element_type=f32)
-    grad_scores = (probs * (dprob - jnp.sum(probs * dprob, axis=2, keepdims=True))).astype(bf16)
-    grad_queries = jnp.einsum("hdbk,hbkq->hdbq", keys, grad_scores, preferred_element_type=f32) * scale
-    grad_keys = jnp.einsum("hdbq,hbkq->hdbk", queries, grad_scores, preferred_element_type=f32)
-    flat = (feats, tokens)
-    grad_proj = jnp.concatenate(
-        [
-            rot(grad_queries.reshape(flat), -sine).reshape((1,) + flat),
-            rot(grad_keys.reshape(flat), -sine).reshape((1,) + flat),
-            grad_values.reshape((1,) + flat),
-            up_pull(back[1:])[0],
-        ],
-        axis=0,
-    )
-    in_bias_grad = jnp.sum(grad_proj, axis=2)
-    low = grad_proj.astype(bf16)
-    w_in_grad = jnp.stack(
-        [
-            jnp.einsum("nt,kt->nk", low[s], normed[slot_stream[s]], preferred_element_type=f32)
-            for s in range(7)
-        ],
-        axis=1,
-    )
-    w_in_grad = lax.psum(w_in_grad.astype(bf16), "dp").astype(f32)
-    grad_normed = jnp.concatenate(
-        [
-            jnp.einsum("nsk,snt->skt", w_in[:, :3], low[:3], preferred_element_type=f32),
-            jnp.einsum("njk,jnt->kt", w_in[:, 3:], low[3:], preferred_element_type=f32)[None],
-        ],
-        axis=0,
-    ).astype(bf16)
-    grad_normed = lax.psum_scatter(grad_normed, "seq", scatter_dimension=1, tiled=True).astype(f32)
-    gx = jnp.sum(grad_normed * scaled, axis=2)
-    gs = jnp.sum(grad_normed, axis=2)
-    norm_gain_grad = jnp.stack([gx[0] + gx[1] + gx[2], gx[3]])
-    norm_bias_grad = jnp.stack([gs[0] + gs[1] + gs[2], gs[3]])
-    g = grad_normed * ng
-    means = sum_feats(jnp.stack([jnp.sum(g, axis=1), jnp.sum(g * scaled, axis=1)])) / width
-    grad_streams = inverse * (g - means[0][:, None] - scaled * means[1][:, None])
-    grad_streams = grad_streams.at[3].add(grad_out_local.astype(f32))
-    grad_mixing = sum_feats(
-        jnp.stack(
-            [jnp.sum(grad_streams * history[j].astype(f32), axis=1) for j in range(states)], axis=0
-        ).reshape(4 * states, tokens)
-    )
-    gen_bias_grad = jnp.sum(grad_mixing, axis=1)
-    gen_out_grad = jnp.einsum("ht,mt->hm", gen_hidden, grad_mixing, precision=highest)
-    grad_hidden = jnp.einsum("hm,mt->ht", out_flat, grad_mixing, precision=highest)
-    grad_pre = gen_pull(grad_hidden)[0].astype(bf16)
-    gen_normed = (last * rms * gain_l).astype(bf16)
-    gen_in_grad = jnp.einsum("dt,ht->dh", gen_normed, grad_pre, preferred_element_type=f32)
-    grad_gen = jnp.einsum("dh,ht->dt", gen_in_l, grad_pre, preferred_element_type=f32)
-    gen_gain_grad = jnp.sum(grad_gen * last * rms, axis=1)
-    mz = jnp.sum(grad_pre.astype(f32) * raw, axis=0, keepdims=True) / width
-    hist_terms = []
-    for j in range(states):
-        term = jnp.sum(mix[:, j] * grad_streams, axis=0)
-        if j == states - 1:
-            term = term + rms * grad_gen * gain_l - last * (rms * rms * rms) * mz
-        hist_terms.append(term.astype(bf16))
-    history_grad = jnp.stack(hist_terms)
-    out_bias_grad = jnp.sum(grad_out_local.astype(f32), axis=1)
-    vec = jnp.concatenate(
-        [
-            in_bias_grad, norm_gain_grad, norm_bias_grad, gen_gain_grad[None],
-            out_bias_grad[None], gen_in_grad.T,
-        ],
-        axis=0,
-    )
-    vec = lax.all_gather(lax.psum(vec, "dp"), "seq", axis=1, tiled=True)
-    shared = lax.psum(
-        jnp.concatenate(
-            [gen_out_grad.reshape(-1), gen_bias_grad, stat_sums, stat_squares, stat_count[None]]
-        ),
-        "dp",
-    )
-    count = shared[-1]
-    mix_mean = shared[hid * m + m : hid * m + 2 * m] / count
-    mix_var = shared[hid * m + 2 * m : hid * m + 3 * m] / count - mix_mean * mix_mean
+    (
+        new_state, history_grad, totals, bias, ngain, nbias, gain, outb, gin, gout, gbias, mean, var,
+    ) = back(
+        n, zn, nbuf, cot_all, cols, pk, raw, scaled, st3, stat, history, gen_gain, gen_in, gen_out,
+        norm_gain, in_bias, out_bias, w_in,
+    )
+    totals = totals.astype(jnp.float32)
+    feats, width = totals.shape[1:]
     return (
-        new_state, history_grad,
-        mix_mean.reshape(states, 4).T, mix_var.reshape(states, 4).T,
-        vec[11], vec[13:].T, shared[: hid * m].reshape(hid, states, 4).swapaxes(1, 2),
-        shared[hid * m : hid * m + m].reshape(states, 4).T,
-        vec[7:9], vec[9:11], w_in_grad, vec[0:7],
-        row_grads[:, :width], row_grads[:, width:], vec[12],
+        new_state, history_grad, mean, var, gain.reshape(width), gin.T, gout.transpose(2, 1, 0),
+        gbias, ngain, nbias, totals[:7].transpose(1, 0, 2), bias, totals[7],
+        totals[8:].transpose(1, 0, 2).reshape(feats, 4 * width), outb.reshape(width),
     )
 
 
@@ -868,8 +1419,8 @@
         P("seq", None),
         P(),
     )
-    split_heads = HEADS % mesh.shape["seq"] == 0
-    body = tp_device if split_heads else per_device
+    by_feature = mesh.shape["seq"] == 8 and mesh.shape["dp"] in (1, 4)
+    body = tp_device if by_feature else per_device
     return jax.shard_map(
         body, mesh=mesh, in_specs=in_specs, out_specs=out_specs, check_vma=False
     )

time: 433 us -> 257 us (0.59)
  Pallas kernels: 79.8 us -> 237 us
  waiting for transfers between devices: 128 us -> 0 us
  blocking collectives: 63.4 us -> 0 us
  matrix products: 55.2 us -> 0 us
  other arithmetic: 42.1 us -> 2.64 us
  local copies, waits for them, and re-layouts: 43.2 us -> 16.3 us
  between operations: 16.5 us -> 0.75 us
    pallas_call x1 -> x2, Pallas kernels: 79.8 us -> 237 us  [the longest x1 158 us: back(): pl.pallas_call(functools.partial(back_kernel, n, zn), out_shape=(shape((f...]
    psum x2 -> x0, waiting for transfers between devices: 128 us -> none  [the longest x1 79.6 us: tp_device(): row_grads = lax.psum(row_grads, 'dp').astype(f32)]
    dot_general x28 -> x0, matrix products: 54.6 us -> none  [the longest x7 13.9 us: tp_device(): jnp.dot(w_in[:, s], normed[slot_stream[s]], preferred_element_type=f32)]
    psum x2 -> x0, blocking collectives: 43.1 us -> none  [the longest x1 23.8 us: sum_feats(): return lax.psum(part, 'seq')]
    all_gather x2 -> x0, blocking collectives: 20.3 us -> none  [the longest x1 10.5 us: tp_device(): vec = lax.all_gather(lax.psum(vec, 'dp'), 'seq', axis=1, tiled=True)]
    reduce_sum x8 -> x0, other arithmetic: 12.6 us -> none  [the longest x1 4.35 us: tp_device(): jnp.sum(grad_streams * history[j].astype(f32), axis=1)]
    concatenate x3 -> x0, other arithmetic: 6.88 us -> none  [the longest x1 6.74 us: tp_device(): jnp.concatenate([jnp.einsum('nsk,snt->skt', w_in[:, :3], low[:3], preferr...]
    slice x12 -> x0, local copies, waits for them, and re-layouts: 6.33 us -> none  [the longest x1 1.36 us: tp_device(): row_grads[:, width:]]
  transfers between devices with their start and end apart: 5 -> 0, of which waited for: 2 -> 0; matrix products, arithmetic and copies ran while one was open for 16% -> 0% of each run, Pallas kernels for 0% -> 0%
where the time goes in v3:
time: 257 us
  Pallas kernels  237 us (92%)
  local copies, waits for them, and re-layouts  16.3 us (6%)
  other arithmetic  2.64 us (1%)
    pallas_call x1, Pallas kernels, back(): pl.pallas_call(functools.partial(back_kernel, n, zn), out_shape=(shape((f...  158 us
    pallas_call x1, Pallas kernels, front(): pl.pallas_call(functools.partial(front_kernel, n), out_shape=(shape((4 *...  79.7 us
    unnamed x37, local copies, waits for them, and re-layouts  11.2 us

profile of v3, /device:TPU:0, one launch (start us, length us, event | category | flops | bytes accessed | tf_op | source)
XLA Modules:
  0.0 256.9 jit_solution(15752444253234945149)
XLA Ops:
  0.6 79.7 %front.1 = (bf16[32,128,1024]{2,1,0:T(8,128)(2,1)}, bf16[1024,1024]{1,0:T(8,128)(2,1)}, bf16[1024,640]{1,0:T(8,128)(2,1)}, f32[8,40,128]{2,1,0:T(8,128)}, f32[48...) custom-call(bf16[9,128,1024]{2,1,0:T(8,128)(2,1)} %history.1, ...), custom_call_target="tpu_custom_call" | custom-call | tf_op jit(solution)/shard_map/front/pallas_call | solution.py:614
  80.3 157.5 %back.1 = (bf16[128,1024]{1,0:T(8,128)(2,1)}, bf16[9,128,1024]{2,1,0:T(8,128)(2,1)}, bf16[12,128,1024]{2,1,0:T(8,128)(2,1)}, f32[7,1024]{1,0:T(8,128)}, f32[2,10...) custom-call(bf16[32,128,1024]{2,1,0:T(8,128)(2,1)} %get-tuple-elemen, ...), custom_call_target="tpu_custom_call" | custom-call | tf_op jit(solution)/shard_map/back/pallas_call | solution.py:1296
  237.9 2.6 %convert_element_type.3 = f32[12,128,1024]{2,1,0:T(8,128)S(1)} convert(bf16[12,128,1024]{2,1,0:T(8,128)(2,1)} %get-tuple-element.54) | non-fusion elementwise | flops 1572864 | bytes 9437184 | tf_op jit(solution)/shard_map/convert_element_type | solution.py:1378
  240.5 0.8 slice_bitcast_fusion.2
  241.4 0.1 slice_bitcast_fusion.1
  241.5 2.3 slice_bitcast_fusion
  243.8 1.8 copy.30
  245.6 3.0 %copy.31 = f32[128,4096]{1,0:T(8,128)} copy(f32[128,4096]{0,1:T(8,128)} %bitcast.16) | data formatting | bytes 4194304
  248.7 0.0 copy-done.1
  248.7 0.7 copy.44
  249.4 0.0 copy-done
  249.4 0.0 copy-start.2
  249.4 0.0 copy-start.4
  249.4 0.0 copy-start.9
  249.4 0.0 copy-start.6
  249.4 0.0 copy-start.5
  249.4 0.0 copy-start.3
  249.4 0.0 copy-start.7
  249.5 1.4 copy.45
  250.9 0.0 copy-done.11
  250.9 0.6 copy.46
  251.4 0.6 copy.47
  252.0 0.0 copy-done.8
  252.0 0.6 copy.48
  252.6 0.0 copy-done.2
  252.6 0.7 copy.49
  253.3 0.6 copy.50
  253.9 0.6 copy.51
  254.5 0.6 copy.52
  255.1 0.6 copy.53
  255.7 0.6 copy.54
  256.3 0.6 copy.55
  (12 shorter events, 0.0 us)
Async XLA Ops:
  245.6 3.0 %copy-start.1 = (bf16[128,1024]{1,0:T(8,128)(2,1)S(1)}, bf16[128,1024]{1,0:T(8,128)(2,1)}, u32[]{:S(2)}) copy-start(bf16[128,1024]{1,0:T(8,128)(2,1)} %get-tuple-element.87) | copy-start | bytes 786436
  245.6 3.7 %copy-start = (bf16[9,128,1024]{2,1,0:T(8,128)(2,1)S(1)}, bf16[9,128,1024]{2,1,0:T(8,128)(2,1)}, u32[]{:S(2)}) copy-start(bf16[9,128,1024]{2,1,0:T(8,128)(2,1)} %get-tuple-element.88) | copy-start | bytes 7077892
  249.4 1.5 copy-start.11
  249.4 2.1 copy-start.10
  249.4 2.6 %copy-start.8 = (f32[1,1024]{1,0:T(1,128)S(1)}, f32[1,1024]{1,0:T(1,128)}, u32[]{:S(2)}) copy-start(f32[1,1024]{1,0:T(1,128)} %get-tuple-element.48) | copy-start | bytes 12292
  249.4 3.2 %copy-start.2 = (f32[40,1024]{1,0:T(8,128)S(1)}, f32[40,1024]{1,0:T(8,128)}, u32[]{:S(2)}) copy-start(f32[40,1024]{1,0:T(8,128)} %get-tuple-element.49) | copy-start | bytes 491524
  249.4 3.9 %copy-start.4 = (f32[9,4,40]{2,1,0:T(4,128)S(1)}, f32[9,4,40]{2,1,0:T(4,128)}, u32[]{:S(2)}) copy-start(f32[9,4,40]{2,1,0:T(4,128)} %get-tuple-element.50) | copy-start | bytes 17284
  249.4 4.5 %copy-start.9 = (f32[4,9]{1,0:T(4,128)S(1)}, f32[4,9]{1,0:T(4,128)}, u32[]{:S(2)}) copy-start(f32[4,9]{1,0:T(4,128)} %get-tuple-element.94) | copy-start | bytes 436
  249.4 5.1 %copy-start.6 = (f32[2,1024]{1,0:T(2,128)S(1)}, f32[2,1024]{1,0:T(2,128)}, u32[]{:S(2)}) copy-start(f32[2,1024]{1,0:T(2,128)} %get-tuple-element.95) | copy-start | bytes 24580
  249.4 5.7 %copy-start.5 = (f32[2,1024]{1,0:T(2,128)S(1)}, f32[2,1024]{1,0:T(2,128)}, u32[]{:S(2)}) copy-start(f32[2,1024]{1,0:T(2,128)} %get-tuple-element.96) | copy-start | bytes 24580
  249.4 6.3 %copy-start.3 = (f32[7,1024]{1,0:T(8,128)S(1)}, f32[7,1024]{1,0:T(8,128)}, u32[]{:S(2)}) copy-start(f32[7,1024]{1,0:T(8,128)} %get-tuple-element.98) | copy-start | bytes 86020
  249.4 6.9 %copy-start.7 = (f32[1,1024]{1,0:T(1,128)S(1)}, f32[1,1024]{1,0:T(1,128)}, u32[]{:S(2)}) copy-start(f32[1,1024]{1,0:T(1,128)} %get-tuple-element.56) | copy-start | bytes 12292

commit v4 on v3

--- a/solution.py
+++ b/solution.py
@@ -339,14 +339,6 @@
         self.pb = self.a + flip
         self.pdg = self.dg + flip
 
-    def greet(self):
-        barrier = pltpu.get_barrier_semaphore()
-        for k in range(1, self.n):
-            pl.semaphore_signal(
-                barrier, inc=1, device_id={"seq": (self.me + k) % self.n}, device_id_type=MESH
-            )
-        pl.semaphore_wait(barrier, self.n - 1)
-
     def copy(self, src, dst, send, recv, to):
         return pltpu.make_async_remote_copy(
             src_ref=src, dst_ref=dst, send_sem=send, recv_sem=recv,
@@ -427,57 +419,90 @@
             at.copy(place, place, self.send.at[k], self.recv.at[k], at.p).wait_send()
 
 
-def front_kernel(
-    n,
-    hist, cot, lens, vals, gain, gin, gout, gbias, ng, nb, w_out, w_down,
-    nbuf, cot_all, cols, pk, raw_out, scaled, st3, stat_out,
-    prm, colp, part, part_in, stat, stat_in, streams, nown,
-    ex_send, ex_recv, ag_send, ag_recv, local_sem,
+COLS_EARLY = 2
+
+
+def layer_kernel(
+    n, zn,
+    history, cotangent, lens, vals, gain, gin, gout, gbias, ng, nb, w_in, in_bias, w_out, w_down, out_bias,
+    new_out, hist_out, totals,
+    bias_tot, ngain_tot, nbias_tot, gain_tot, outb_tot, gin_tot, gout_tot,
+    gbias_tot, mean_tot, var_tot,
+    hist, new_state, big, cot, cols, w_turn, prm, colp, qkv, act, deriv, probs, gattn, gp, gcol, rope, accs, gn,
+    scaled, st3, pk, raw, part, part_in, stat, stat_in, stat_out,
+    ybuf, abuf, from_a, from_b, zown, zin, zmid,
+    gsum, gsum_in, gmix, gmix_in, pre, genmsg, gen_in_all, vec, vec_z, vec_sum, vec_all,
+    load_sem, ag_send, ag_recv, rs_send, rs_recv, ex_send, ex_recv, z_send, z_recv, out_sem,
 ):
     f32, bf16 = jnp.float32, jnp.bfloat16
     states, feats, tokens = hist.shape
     block = tokens // n
     width = n * feats
     hid = gin.shape[0]
+    heads = feats // HEAD_DIM
+    scale = HEAD_DIM ** (-0.5)
+    m = 4 * states
+    wide = 2 * block
+    chunks = tokens // wide
+    quarter = width // 4
     at = Links(n)
     me = at.me
-    mine = pl.ds(pl.multiple_of(me * feats, feats), feats)
+    zc = lax.axis_index("dp")
 
     def rows(owner):
         return pl.ds(pl.multiple_of(owner * feats, feats), feats)
 
-    def lanes(owner):
-        return pl.ds(pl.multiple_of(owner * block, block), block)
+    def lanes(index, size=block):
+        return pl.ds(pl.multiple_of(index * size, size), size)
+
+    mine = rows(me)
+
+    load_last = pltpu.make_async_copy(history.at[states - 1], hist.at[states - 1], load_sem.at[0])
+    load_hist = pltpu.make_async_copy(
+        history.at[pl.ds(0, states - 1)], hist.at[pl.ds(0, states - 1)], load_sem.at[1]
+    )
+    load_cot = pltpu.make_async_copy(cotangent, cot.at[mine, :], load_sem.at[2])
+    for copy in (load_last, load_hist, load_cot):
+        copy.start()
+    barrier = pltpu.get_barrier_semaphore()
+    for k in range(1, n):
+        pl.semaphore_signal(
+            barrier, inc=1, device_id={"seq": (me + k) % n}, device_id_type=MESH
+        )
+    for k in range(1, zn):
+        pl.semaphore_signal(
+            barrier, inc=1, device_id={"dp": (zc + k) % zn}, device_id_type=MESH
+        )
 
     gathers = [
-        Gather(at, lambda owner, s=s: nbuf.at[s * n + owner], ag_send.at[s], ag_recv.at[s])
+        Gather(at, lambda owner, s=s: big.at[s * n + owner], ag_send.at[s], ag_recv.at[s])
         for s in range(4)
     ]
-    cots = Gather(at, lambda owner: cot_all.at[rows(owner), :], ag_send.at[4], ag_recv.at[4])
+    cots = Gather(at, lambda owner: cot.at[rows(owner), :], ag_send.at[4], ag_recv.at[4])
     parts = Everyone(
         at, lambda to: part.at[to], lambda k: part_in.at[k], lambda k, origin: part_in.at[k],
-        ex_send.at[0], ex_recv.at[0],
-    )
-    mixes = Everyone(
+        ex_send.at[6], ex_recv.at[6],
+    )
+    spread_mix = Everyone(
         at, lambda to: pk.at[me], lambda k: pk.at[me], lambda k, origin: pk.at[origin],
-        ex_send.at[1], ex_recv.at[1],
+        ex_send.at[7], ex_recv.at[7],
     )
     stats = Everyone(
         at, lambda to: stat, lambda k: stat_in.at[me], lambda k, origin: stat_in.at[origin],
-        ex_send.at[2], ex_recv.at[2],
-    )
-
-    at.greet()
-    cots.start(cot)
-    keep_cot = pltpu.make_async_copy(cot, cot_all.at[mine, :], local_sem.at[0])
-    keep_cot.start()
+        ex_send.at[8], ex_recv.at[8],
+    )
 
     prm[...] = jnp.zeros_like(prm)
     prm[0:1, :] = gain[:, mine]
     prm[1:3, :] = ng[:, mine]
     prm[3:5, :] = nb[:, mine]
+    prm[5:6, :] = out_bias[:, mine]
+    prm[8:15, :] = in_bias[:, mine]
     colp[...] = prm[...].T
+    accs[...] = jnp.zeros_like(accs)
+
     gin_mine = gin[:, mine]
+    load_last.wait()
     for b in range(n):
         last = hist[states - 1, :, b * block : (b + 1) * block].astype(f32)
         product = (last * colp[:, 0:1]).astype(bf16)
@@ -485,45 +510,51 @@
         part[b, hid : hid + 8, :] = jnp.broadcast_to(
             jnp.sum(last * last, axis=0, keepdims=True), (8, block)
         )
+    pl.semaphore_wait(barrier, n - 1 + zn - 1)
     parts.start()
+
+    @pl.loop(0, n)
+    def _(r):
+        for j in range(4):
+            ybuf[0, rows(r), j * feats : (j + 1) * feats] = w_in[3 + j, :, lanes(r, feats)].T
+
+    load_hist.wait()
     total = part[me]
     for k in range(1, n):
         parts.wait(k)
         total = total + part_in[k]
-    raw_out[...] = total
+    raw[...] = total
     rms = lax.rsqrt(total[hid : hid + 1] * (1.0 / width) + rms_eps)
     hidden, _ = gelu_pair(total[0:hid] * rms)
     table = jnp.concatenate([gout[j] for j in range(states)], axis=0)
     mixing = jnp.dot(table, hidden, precision=highest, preferred_element_type=f32)
     for j in range(states):
         pk[me, 4 * j : 4 * j + 4, :] = mixing[4 * j : 4 * j + 4] + gbias[:, j : j + 1]
-    row = 4 * states
-    pk[me, row : row + 1, :] = rms
+    pk[me, m : m + 1, :] = rms
     for offset, value in ((1, lens[0, 0, 0]), (2, vals[0, 0, 0]), (3, vals[0, 0, 1])):
-        pk[me, row + offset : row + offset + 1, :] = jnp.full((1, block), value.astype(f32))
-    mixes.start()
-
-    def column_copies(to, send, recv):
-        out = []
-        for j in range(5):
-            if j == 0:
-                src = w_out.at[:, rows(to)]
-            else:
-                src = w_down.at[:, pl.ds(pl.multiple_of((j - 1) * width + to * feats, feats), feats)]
-            out.append((src, cols.at[mine, pl.ds(j * feats, feats)]))
-        return out
-
-    for k in range(1, n):
-        to = (me + k) % n
-        for src, dst in column_copies(to, None, None):
-            at.copy(src, dst, ex_send.at[3, k], ex_recv.at[3, k], to).start()
+        pk[me, m + offset : m + offset + 1, :] = jnp.full((1, block), value.astype(f32))
+    spread_mix.start()
+
+    def column_copy(to, j):
+        if j == 0:
+            src = w_out.at[:, rows(to)]
+        else:
+            src = w_down.at[:, pl.ds(pl.multiple_of((j - 1) * width + to * feats, feats), feats)]
+        return src, cols.at[mine, pl.ds(j * feats, feats)]
+
+    def send_columns(which):
+        for j in which:
+            for k in range(1, n):
+                to = (me + k) % n
+                src, dst = column_copy(to, j)
+                at.copy(src, dst, ex_send.at[9, k], ex_recv.at[9, k], to).start()
+
     own_cols = [
-        pltpu.make_async_copy(src, dst, local_sem.at[1 + j])
-        for j, (src, dst) in enumerate(column_copies(me, None, None))
+        pltpu.make_async_copy(*column_copy(me, j), load_sem.at[3 + j]) for j in range(5)
     ]
     for copy in own_cols:
         copy.start()
-    cots.near()
+    send_columns(range(COLS_EARLY))
 
     def mix_block(owner):
         where = lanes(owner)
@@ -537,9 +568,9 @@
                     term = weight * value
                     sums[s] = term if sums[s] is None else sums[s] + term
             for s in range(4):
-                streams[s, part_rows, where] = sums[s]
+                scaled[s, part_rows, where] = sums[s]
         for s in range(4):
-            value = streams[s, :, where]
+            value = scaled[s, :, where]
             mean = jnp.sum(value, axis=0, keepdims=True) * (1.0 / feats)
             off = value - mean
             stat[pl.ds(s, 1), where] = mean
@@ -549,10 +580,38 @@
 
     @pl.loop(1, n)
     def _(k):
-        mix_block(mixes.wait(k))
+        mix_block(spread_mix.wait(k))
 
     stats.start()
-    cots.far()
+
+    spot = lax.broadcasted_iota(jnp.int32, (1, block), 1).astype(f32)
+    freq = jnp.exp(
+        lax.broadcasted_iota(jnp.int32, (8, block), 0).astype(f32)
+        * (-2.0 * math.log(10000.0) / ROT)
+    )
+
+    def place(owner, index):
+        cut = pk[owner, m + 1 : m + 2, :]
+        second = index >= cut
+        position = index - jnp.where(second, cut, 0.0)
+        limit = jnp.where(second, pk[owner, m + 3 : m + 4, :], pk[owner, m + 2 : m + 3, :])
+        return second, position, position < limit
+
+    load_cot.wait()
+    for b in range(n):
+        where = pl.ds(b * block, block)
+        _, position, valid = place(b, spot)
+        angle = freq * position
+        rope[0:8, where] = jnp.cos(angle)
+        rope[8:16, where] = jnp.sin(angle)
+        kept = jnp.where(valid, 1.0, 0.0)
+        cot[mine, where] = cot[mine, where] * kept.astype(bf16)
+
+    @pl.loop(0, n)
+    def _(r):
+        for s in range(3):
+            w_turn[rows(r), s * feats : (s + 1) * feats] = w_in[s, :, lanes(r, feats)].T
+
     for k in range(1, n):
         stats.wait(k)
     stat_in[me] = stat[...]
@@ -567,173 +626,22 @@
     stat_out[0:4, :] = means
     stat_out[4:8, :] = lax.rsqrt(spread * (1.0 / width) + ln_eps)
 
-    keeps = []
-    for s in range(4):
+    def normalise(s):
         which = 0 if s < 3 else 1
-        for b in range(n):
-            where = pl.ds(b * block, block)
-            xhat = (streams[s, :, where] - stat_out[s : s + 1, where]) * stat_out[4 + s : 5 + s, where]
+
+        @pl.loop(0, n)
+        def _(b):
+            where = lanes(b)
+            value = scaled[s, :, where]
+            if s == 3:
+                st3[:, where] = value
+            xhat = (value - stat_out[s : s + 1, where]) * stat_out[4 + s : 5 + s, where]
             scaled[s, :, where] = xhat
-            nown[s, :, where] = (
+            big[s * n + me, :, where] = (
                 xhat * colp[:, 1 + which : 2 + which] + colp[:, 3 + which : 4 + which]
             ).astype(bf16)
-        gathers[s].start(nown.at[s])
-        keep = pltpu.make_async_copy(nown.at[s], nbuf.at[s * n + me], local_sem.at[6 + s])
-        keep.start()
-        keeps.append(keep)
-    st3[...] = streams[3]
-    for s in range(4):
-        gathers[s].near()
-        if s >= 1:
-            gathers[s - 1].far()
-    gathers[3].far()
-    for g in [cots] + gathers:
-        g.other()
-    for k in range(1, n):
-        place = cols.at[rows((me + n - k) % n), :]
-        at.copy(place, place, ex_send.at[3, k], ex_recv.at[3, k], at.p).wait()
-    for g in [cots] + gathers:
-        g.drain()
-    for exchange in (parts, mixes, stats):
-        exchange.drain()
-    keep_cot.wait()
-    for copy in own_cols + keeps:
-        copy.wait()
-
-
-def front(n, history, cotangent, bucket_len, valid_len, gen_gain, gen_in, gen_out, gen_bias, norm_gain, norm_bias, w_out, w_down):
-    f32, bf16 = jnp.float32, jnp.bfloat16
-    states, feats, tokens = history.shape
-    block = tokens // n
-    width = n * feats
-    hid = gen_in.shape[1]
-    vmem = pl.BlockSpec(memory_space=pltpu.VMEM)
-    smem = pl.BlockSpec(memory_space=pltpu.SMEM)
-    anys = pl.BlockSpec(memory_space=pl.ANY)
-    shape = jax.ShapeDtypeStruct
-    return pl.pallas_call(
-        functools.partial(front_kernel, n),
-        out_shape=(
-            shape((4 * n, feats, tokens), bf16),
-            shape((width, tokens), bf16),
-            shape((width, 5 * feats), bf16),
-            shape((n, 40, block), f32),
-            shape((hid + 8, block), f32),
-            shape((4, feats, tokens), f32),
-            shape((feats, tokens), f32),
-            shape((8, tokens), f32),
-        ),
-        in_specs=[vmem, vmem, smem, smem] + [vmem] * 6 + [anys] * 2,
-        out_specs=(anys, anys, anys, vmem, vmem, vmem, vmem, vmem),
-        scratch_shapes=[
-            pltpu.VMEM((feats, feats), f32),
-            pltpu.VMEM((feats, feats), f32),
-            pltpu.VMEM((n, hid + 8, block), f32),
-            pltpu.VMEM((n, hid + 8, block), f32),
-            pltpu.VMEM((8, tokens), f32),
-            pltpu.VMEM((n, 8, tokens), f32),
-            pltpu.VMEM((4, feats, tokens), f32),
-            pltpu.VMEM((4, feats, tokens), bf16),
-            pltpu.SemaphoreType.DMA((4, n)),
-            pltpu.SemaphoreType.DMA((4, n)),
-            pltpu.SemaphoreType.DMA((5, 7)),
-            pltpu.SemaphoreType.DMA((5, 7)),
-            pltpu.SemaphoreType.DMA((10,)),
-        ],
-        compiler_params=pltpu.CompilerParams(
-            collective_id=1, has_side_effects=True, vmem_limit_bytes=60 * 2**20
-        ),
-        name="front",
-    )(
-        history, cotangent, bucket_len, valid_len, gen_gain.reshape(1, width), gen_in.T,
-        gen_out.transpose(2, 1, 0), gen_bias, norm_gain, norm_bias, w_out, w_down,
-    )
-
-
-def back_kernel(
-    n, zn,
-    nbuf, cot_all, cols_in, history, scaled_in,
-    w_in, pk, raw, st3, stat, gain, gin, gout, ng, in_bias, out_bias,
-    new_state, hist_grad, totals,
-    bias_tot, ngain_tot, nbias_tot, gain_tot, outb_tot, gin_tot, gout_tot,
-    gbias_tot, mean_tot, var_tot,
-    big, cot, cols, prm, colp, qkv, act, deriv, probs, gattn, gp, gcol, rope, accs, gn,
-    ybuf, abuf, from_a, from_b, zown, zin, zmid,
-    gsum, gsum_in, gmix, gmix_in, pre, genmsg, gen_in_all, vec, vec_z, vec_sum, vec_all,
-    load_sem, rs_send, rs_recv, ex_send, ex_recv, z_send, z_recv, out_sem,
-):
-    f32, bf16 = jnp.float32, jnp.bfloat16
-    states = history.shape[0]
-    feats, tokens = st3.shape
-    block = tokens // n
-    width = n * feats
-    hid = gin.shape[0]
-    heads = feats // HEAD_DIM
-    scale = HEAD_DIM ** (-0.5)
-    m = 4 * states
-    wide = 2 * block
-    chunks = tokens // wide
-    at = Links(n)
-    me = at.me
-    zc = lax.axis_index("dp")
-
-    def rows(owner):
-        return pl.ds(pl.multiple_of(owner * feats, feats), feats)
-
-    def lanes(index, size=block):
-        return pl.ds(pl.multiple_of(index * size, size), size)
-
-    loads = [
-        pltpu.make_async_copy(
-            nbuf.at[pl.ds(s * n, n)], big.at[pl.ds(s * n, n)], load_sem.at[s]
-        )
-        for s in range(4)
-    ]
-    loads.append(pltpu.make_async_copy(cot_all, cot, load_sem.at[4]))
-    loads.append(pltpu.make_async_copy(cols_in, cols, load_sem.at[5]))
-    for index in (0, 1, 2, 3, 5, 4):
-        loads[index].start()
-    load_scaled = pltpu.make_async_copy(scaled_in, deriv, load_sem.at[6])
-    load_hist = pltpu.make_async_copy(history, big.at[pl.ds(0, states)], load_sem.at[7])
-
-    barrier = pltpu.get_barrier_semaphore()
-    for k in range(1, n):
-        pl.semaphore_signal(
-            barrier, inc=1, device_id={"seq": (me + k) % n}, device_id_type=MESH
-        )
-    for k in range(1, zn):
-        pl.semaphore_signal(
-            barrier, inc=1, device_id={"dp": (zc + k) % zn}, device_id_type=MESH
-        )
-
-    prm[...] = jnp.zeros_like(prm)
-    prm[0:1, :] = gain[:, rows(me)]
-    prm[1:3, :] = ng[:, rows(me)]
-    prm[3:4, :] = out_bias[:, rows(me)]
-    prm[8:15, :] = in_bias[:, rows(me)]
-    colp[...] = prm[...].T
-    accs[...] = jnp.zeros_like(accs)
-
-    spot = lax.broadcasted_iota(jnp.int32, (1, block), 1).astype(f32)
-    freq = jnp.exp(
-        lax.broadcasted_iota(jnp.int32, (8, block), 0).astype(f32)
-        * (-2.0 * math.log(10000.0) / ROT)
-    )
-
-    def place(owner, index):
-        cut = pk[owner, m + 1 : m + 2, :]
-        second = index >= cut
-        position = index - jnp.where(second, cut, 0.0)
-        limit = jnp.where(second, pk[owner, m + 3 : m + 4, :], pk[owner, m + 2 : m + 3, :])
-        return second, position, position < limit
-
-    for b in range(n):
-        where = pl.ds(b * block, block)
-        _, position, valid = place(b, spot)
-        angle = freq * position
-        rope[0:8, where] = jnp.cos(angle)
-        rope[8:16, where] = jnp.sin(angle)
-        rope[16:17, where] = jnp.where(valid, 1.0, 0.0)
+
+        gathers[s].start(big.at[s * n + me])
 
     def rotated(value, where, sign):
         cosine, sine = rope[0:8, where], rope[8:16, where] * sign
@@ -751,11 +659,9 @@
     def stream(s, where):
         return big[pl.ds(s * n, n), :, where].reshape(width, -1)
 
-    for s in range(3):
-        loads[s].wait()
-
+    def project(s):
         @pl.loop(0, chunks)
-        def _(c, s=s):
+        def _(c):
             where = lanes(c, wide)
             value = jnp.dot(w_in[s], stream(s, where), preferred_element_type=f32)
             value = value + colp[:, 8 + s : 9 + s]
@@ -765,36 +671,70 @@
                 value = value * scale
             qkv[s, :, where] = value.astype(bf16)
 
-    loads[3].wait()
-    for j in range(4):
-
+    def project_up(pair):
         @pl.loop(0, chunks)
-        def _(c, j=j):
+        def _(c):
             where = lanes(c, wide)
-            value = jnp.dot(w_in[3 + j], stream(3, where), preferred_element_type=f32)
-            up, slope = gelu_pair(value + colp[:, 11 + j : 12 + j])
-            act[pl.ds((1 + j) * feats, feats), where] = up.astype(bf16)
-            deriv[j, :, where] = slope
+            weight = w_in[3 + 2 * pair : 5 + 2 * pair].reshape(2 * feats, width)
+            both = jnp.dot(weight, stream(3, where), preferred_element_type=f32)
+            for i in range(2):
+                j = 2 * pair + i
+                up, slope = gelu_pair(
+                    both[i * feats : (i + 1) * feats] + colp[:, 11 + j : 12 + j]
+                )
+                act[pl.ds((1 + j) * feats, feats), where] = up.astype(bf16)
+                deriv[j, :, where] = slope
+
+    normalise(3)
+    normalise(0)
+    gathers[3].near()
+    normalise(1)
+    gathers[0].near()
+    normalise(2)
+    gathers[3].far()
+    gathers[3].other()
+    project_up(0)
+    gathers[1].near()
+    gathers[0].far()
+    project_up(1)
+    gathers[2].near()
+    cots.start(cot.at[mine, :])
+    send_columns(range(COLS_EARLY, 5))
+    gathers[0].other()
+    project(0)
+    gathers[1].far()
+    gathers[1].other()
+    project(1)
+    gathers[2].far()
+    gathers[2].other()
+    project(2)
 
     key_at = lax.broadcasted_iota(jnp.int32, (block, block), 0).astype(f32)
     query_at = lax.broadcasted_iota(jnp.int32, (block, block), 1).astype(f32)
 
-    @pl.loop(0, n)
-    def _(b):
-        where = lanes(b)
-        cut = pk[b, m + 1 : m + 2, :]
-        _, _, valid = place(b, key_at)
-        same = jnp.where(key_at >= cut, 1.0, 0.0) == jnp.where(query_at >= cut, 1.0, 0.0)
-        allowed = same & (key_at <= query_at) & valid
-        for h in range(heads):
-            part = pl.ds(h * HEAD_DIM, HEAD_DIM)
-            scores = contract(qkv[1, part, where], qkv[0, part, where], 0, 0)
+    @pl.loop(0, n // 2)
+    def _(pair):
+        chains = []
+        for u in range(2):
+            b = 2 * pair + u
+            where = lanes(b)
+            cut = pk[b, m + 1 : m + 2, :]
+            _, _, valid = place(b, key_at)
+            same = jnp.where(key_at >= cut, 1.0, 0.0) == jnp.where(query_at >= cut, 1.0, 0.0)
+            allowed = same & (key_at <= query_at) & valid
+            for h in range(heads):
+                rows_h = pl.ds(h * HEAD_DIM, HEAD_DIM)
+                scores = contract(qkv[1, rows_h, where], qkv[0, rows_h, where], 0, 0)
+                chains.append((b, h, rows_h, where, allowed, scores))
+        softs = []
+        for b, h, rows_h, where, allowed, scores in chains:
             scores = jnp.where(allowed, scores, masked_score)
             weights = jnp.exp(scores - jnp.max(scores, axis=0, keepdims=True))
-            soft = weights * (1.0 / jnp.sum(weights, axis=0, keepdims=True))
+            softs.append(weights * (1.0 / jnp.sum(weights, axis=0, keepdims=True)))
+        for (b, h, rows_h, where, _, _), soft in zip(chains, softs):
             probs[b * heads + h] = soft
-            act[part, where] = jnp.dot(
-                qkv[2, part, where], soft.astype(bf16), preferred_element_type=f32
+            act[rows_h, where] = jnp.dot(
+                qkv[2, rows_h, where], soft.astype(bf16), preferred_element_type=f32
             ).astype(bf16)
 
     def rs_copy(i, src, dst, slot, to):
@@ -947,44 +887,87 @@
                 z_cross(c).wait_send()
                 z_down(c).wait_send()
 
-    loads[5].wait()
-    quarter = width // 4
+    z_order = (3, 4, 5, 6, 7, 8, 9, 10, 11, 0, 1, 2)
+    z_actions = []
+    for t in range(14):
+        if t < 12:
+            z_actions.append((z_fold, z_order[t]))
+        if t >= 2:
+            z_actions.append((z_end, z_order[t - 2]))
+    z_actions = iter(z_actions)
+
+    def z_step(count):
+        for _ in range(count):
+            step, c = next(z_actions)
+            step(c)
+
+
+    cots.near()
+    for k in range(1, n):
+        arrived = cols.at[rows((me + n - k) % n), :]
+        at.copy(arrived, arrived, ex_send.at[9, k], ex_recv.at[9, k], at.p).wait()
+    for copy in own_cols:
+        copy.wait()
 
     @pl.loop(0, chunks)
     def _(c):
         where = lanes(c, wide)
-        for r in range(4):
-            part = slice(r * quarter, (r + 1) * quarter)
-            ybuf[4, part, where] = jnp.dot(
-                cols[part, :], act[:, where], preferred_element_type=f32
+        for r in range(2):
+            half = slice(r * width // 2, (r + 1) * width // 2)
+            ybuf[4, half, where] = jnp.dot(
+                cols[half, :], act[:, where], preferred_element_type=f32
             ).astype(bf16)
 
-    pl.semaphore_wait(barrier, n - 1 + zn - 1)
     rs_start(4)
-
-    loads[4].wait()
+    cots.far()
 
     @pl.loop(0, n)
-    def _(b):
-        where = lanes(b)
-        mask = rope[16:17, where].astype(bf16)
-        cot[:, where] = cot[:, where] * mask
-
-    for j in range(5):
-        gn[0] = contract(cols[:, j * feats : (j + 1) * feats], cot[...], 0, 0)
-
+    def _(r):
+        for j in range(5):
+            zown[j, :, lanes(r, feats)] = cols[rows(r), j * feats : (j + 1) * feats].T
+
+    cots.other()
+
+    @pl.loop(0, chunks)
+    def _(c):
+        where = lanes(c, wide)
+        gattn[:, where] = jnp.dot(zown[0], cot[:, where], preferred_element_type=f32).astype(bf16)
+        for pair in range(2):
+            weight = zown[1 + 2 * pair : 3 + 2 * pair].reshape(2 * feats, width)
+            both = jnp.dot(weight, cot[:, where], preferred_element_type=f32)
+            for i in range(2):
+                j = 2 * pair + i
+                value = both[i * feats : (i + 1) * feats] * deriv[j, :, where]
+                accs[3 + j] = accs[3 + j] + (value[:, :block] + value[:, block:])
+                gp[pl.ds((3 + j) * feats, feats), where] = value.astype(bf16)
+
+    def normed_grad(i, source, first, count):
         @pl.loop(0, chunks)
-        def _(c, j=j):
+        def _(c):
             where = lanes(c, wide)
-            value = gn[0, :, where]
-            if j == 0:
-                gattn[:, where] = value.astype(bf16)
-            else:
-                value = value * deriv[j - 1, :, where]
-                accs[2 + j] = accs[2 + j] + (value[:, :block] + value[:, block:])
-                gp[pl.ds((2 + j) * feats, feats), where] = value.astype(bf16)
-
-    load_scaled.start()
+            for r in range(2):
+                half = slice(r * width // 2, (r + 1) * width // 2)
+                ybuf[i, half, where] = jnp.dot(
+                    source[half, :], gp[first * feats : (first + count) * feats, where],
+                    preferred_element_type=f32,
+                ).astype(bf16)
+
+        rs_start(i)
+
+    def weight_grad(first, count, source):
+        @pl.loop(0, 4)
+        def _(r):
+            part_in_rows = big[pl.ds(source * n + r * (n // 4), n // 4), :, :].reshape(quarter, tokens)
+            value = contract(gp[first * feats : (first + count) * feats, :], part_in_rows, 1, 1)
+            for s in range(count):
+                zown[first + s, :, lanes(r, quarter)] = value[s * feats : (s + 1) * feats].astype(bf16)
+
+        for s in range(first, first + count):
+            z_start(s)
+
+    rs_fold(4)
+    normed_grad(3, ybuf.at[0, :, 0 : 4 * feats], 3, 4)
+    weight_grad(3, 4, 3)
     for r in range(4):
         grads = contract(cot[r * quarter : (r + 1) * quarter, :], act[...], 1, 1).astype(bf16)
         for j in range(5):
@@ -993,100 +976,80 @@
     turns = Everyone(
         at,
         lambda to: gcol.at[:, rows(to), :],
-        lambda k: zown.at[pl.ds(7, 5), :, rows(me)],
+        lambda k: zown.at[pl.ds(7, 5), :, mine],
         lambda k, origin: zown.at[pl.ds(7, 5), :, rows(origin)],
         ex_send.at[0], ex_recv.at[0],
     )
     turns.start()
     keep = pltpu.make_async_copy(
-        gcol.at[:, rows(me), :], zown.at[pl.ds(7, 5), :, rows(me)], load_sem.at[8]
+        gcol.at[:, mine, :], zown.at[pl.ds(7, 5), :, mine], load_sem.at[8]
     )
     keep.start()
-
-    def normed_grad(i, first, count):
-        @pl.loop(0, n)
-        def _(r):
-            weight = jnp.concatenate(
-                [w_in[first + s, :, lanes(r, feats)] for s in range(count)], axis=0
-            )
-            ybuf[i, rows(r), :] = contract(
-                weight, gp[first * feats : (first + count) * feats, :], 0, 0
-            ).astype(bf16)
-
-        rs_start(i)
-
-    def weight_grad(s, source):
-        @pl.loop(0, 4)
-        def _(r):
-            part = big[pl.ds(source * n + r * (n // 4), n // 4), :, :].reshape(quarter, tokens)
-            zown[s, :, lanes(r, quarter)] = contract(
-                gp[s * feats : (s + 1) * feats, :], part, 1, 1
-            ).astype(bf16)
-
-        z_start(s)
-
-    normed_grad(3, 3, 4)
-    for s in range(3, 7):
-        weight_grad(s, 3)
-    rs_fold(4)
-
-    @pl.loop(0, n)
-    def _(b):
-        where = lanes(b)
-        grads = [[], [], []]
-        for h in range(heads):
-            part = pl.ds(h * HEAD_DIM, HEAD_DIM)
-            soft = probs[b * heads + h]
-            grad = gattn[part, where]
-            grads[2].append(contract(grad, soft.astype(bf16), 1, 1))
-            dprob = contract(qkv[2, part, where], grad, 0, 0)
+    rs_pass(4)
+    rs_fold(3)
+
+    @pl.loop(0, n // 2)
+    def _(pair):
+        first = []
+        for u in range(2):
+            b = 2 * pair + u
+            where = lanes(b)
+            for h in range(heads):
+                rows_h = pl.ds(h * HEAD_DIM, HEAD_DIM)
+                soft = probs[b * heads + h]
+                grad = gattn[rows_h, where]
+                dprob = contract(qkv[2, rows_h, where], grad, 0, 0)
+                values_grad = contract(grad, soft.astype(bf16), 1, 1)
+                first.append((rows_h, where, soft, dprob, values_grad))
+        lows = []
+        for rows_h, where, soft, dprob, values_grad in first:
             inner = jnp.sum(soft * dprob, axis=0, keepdims=True)
-            low = (soft * (dprob - inner)).astype(bf16)
-            grads[0].append(
-                jnp.dot(qkv[1, part, where], low, preferred_element_type=f32) * scale
-            )
-            grads[1].append(contract(qkv[0, part, where], low, 1, 1))
-        for s in range(3):
-            value = jnp.concatenate(grads[s], axis=0)
-            if s < 2:
-                value = rotated(value, where, -1.0)
-            accs[s] = accs[s] + value
-            gp[pl.ds(s * feats, feats), where] = value.astype(bf16)
-
-    rs_fold(3)
-    rs_pass(4)
+            lows.append((soft * (dprob - inner)).astype(bf16))
+        for u in range(2):
+            where = first[u * heads][1]
+            grads = [[], [], []]
+            for h in range(heads):
+                rows_h, _, _, _, values_grad = first[u * heads + h]
+                low = lows[u * heads + h]
+                grads[0].append(
+                    jnp.dot(qkv[1, rows_h, where], low, preferred_element_type=f32) * scale
+                )
+                grads[1].append(contract(qkv[0, rows_h, where], low, 1, 1))
+                grads[2].append(values_grad)
+            for s in range(3):
+                value = jnp.concatenate(grads[s], axis=0)
+                if s < 2:
+                    value = rotated(value, where, -1.0)
+                accs[s] = accs[s] + value
+                gp[pl.ds(s * feats, feats), where] = value.astype(bf16)
+
     for s in range(3):
-        normed_grad(s, s, 1)
-    z_fold(3)
+        normed_grad(s, w_turn.at[:, s * feats : (s + 1) * feats], s, 1)
+    rs_pass(3)
+    z_step(1)
+    rs_fold(0)
     for k in range(1, n):
         turns.wait(k)
     keep.wait()
     for c in range(7, 12):
         z_start(c)
     for s in range(3):
-        weight_grad(s, s)
-    load_hist.start()
-    rs_fold(0)
-    z_fold(4)
-    rs_pass(3)
+        weight_grad(s, 1, s)
+    z_step(2)
     rs_fold(1)
-    z_fold(5)
-    rs_pass(0)
-    rs_fold(2)
-    z_fold(6)
-    rs_pass(1)
-    z_end(3)
     rs_end(4)
 
     @pl.loop(0, n)
     def _(b):
         where = lanes(b)
-        new_state[:, where] = (st3[:, where] + rs_value(4, where) + colp[:, 3:4]).astype(bf16)
-
-    rs_pass(2)
-    z_fold(7)
-    z_end(4)
-    load_scaled.wait()
+        new_state[:, where] = (st3[:, where] + rs_value(4, where) + colp[:, 5:6]).astype(bf16)
+
+    keep_new = pltpu.make_async_copy(new_state, new_out, load_sem.at[9])
+    keep_new.start()
+    z_step(1)
+    rs_pass(0)
+    rs_fold(2)
+    z_step(2)
 
     def norm_sums(s):
         which = 0 if s < 3 else 1
@@ -1095,7 +1058,7 @@
         def _(b):
             where = lanes(b)
             value = rs_value(s, where)
-            xhat = deriv[s, :, where]
+            xhat = scaled[s, :, where]
             along = value * xhat
             accs[7 + which] = accs[7 + which] + along
             accs[9 + which] = accs[9 + which] + value
@@ -1104,17 +1067,24 @@
             gsum[s : s + 1, where] = jnp.sum(value * factor, axis=0, keepdims=True)
             gsum[4 + s : 5 + s, where] = jnp.sum(along * factor, axis=0, keepdims=True)
 
-    for s in (3, 0, 1, 2):
-        rs_end(s)
-        norm_sums(s)
+    rs_end(3)
+    norm_sums(3)
+    rs_pass(1)
+    z_step(1)
+    rs_end(0)
+    norm_sums(0)
+    rs_pass(2)
+    z_step(2)
+    rs_end(1)
+    norm_sums(1)
+    rs_end(2)
+    norm_sums(2)
     sums = Everyone(
         at, lambda to: gsum, lambda k: gsum_in.at[me], lambda k, origin: gsum_in.at[origin],
         ex_send.at[1], ex_recv.at[1],
     )
     sums.start()
-    z_fold(8)
-    z_end(5)
-    load_hist.wait()
+    z_step(2)
     for k in range(1, n):
         sums.wait(k)
     gsum_in[me] = gsum[...]
@@ -1127,17 +1097,17 @@
     def _(b):
         where = lanes(b)
         for s in range(4):
-            xhat = deriv[s, :, where]
-            value = stat[4 + s : 5 + s, where] * (
+            xhat = scaled[s, :, where]
+            value = stat_out[4 + s : 5 + s, where] * (
                 gn[s, :, where] - pre[s : s + 1, where] - xhat * pre[4 + s : 5 + s, where]
             )
             if s == 3:
-                direct = cot[rows(me), where].astype(f32)
+                direct = cot[mine, where].astype(f32)
                 accs[12] = accs[12] + direct
                 value = value + direct
             gn[s, :, where] = value
         for j in range(states):
-            past = big[j, :, where].astype(f32)
+            past = hist[j, :, where].astype(f32)
             for s in range(4):
                 gmix[b, 4 * j + s : 4 * j + s + 1, :] = jnp.sum(
                     gn[s, :, where] * past, axis=0, keepdims=True
@@ -1148,8 +1118,7 @@
         ex_send.at[2], ex_recv.at[2],
     )
     mixes.start()
-    z_fold(9)
-    z_end(6)
+    z_step(2)
 
     @pl.loop(0, n)
     def _(b):
@@ -1158,7 +1127,12 @@
             value = pk[b, pl.ds(4 * j, 1), :] * gn[0, :, where]
             for s in range(1, 4):
                 value = value + pk[b, pl.ds(4 * j + s, 1), :] * gn[s, :, where]
-            hist_grad[j, :, where] = value.astype(bf16)
+            hist[j, :, where] = value.astype(bf16)
+
+    keep_hist = pltpu.make_async_copy(
+        hist.at[pl.ds(0, states - 1)], hist_out.at[pl.ds(0, states - 1)], load_sem.at[10]
+    )
+    keep_hist.start()
 
     total = gmix[me]
     for k in range(1, n):
@@ -1178,8 +1152,7 @@
         ex_send.at[3], ex_recv.at[3],
     )
     owns.start()
-    z_fold(10)
-    z_end(7)
+    z_step(2)
     _, _, valid = place(me, spot)
     kept = jnp.where(valid, 1.0, 0.0)
     ones = jnp.ones((8, block), f32)
@@ -1199,7 +1172,7 @@
         where = lanes(b)
         low_b = gen_in_all[b, 0:hid, :].astype(bf16)
         rms = pk[b, m : m + 1, :]
-        last = big[states - 1, :, where].astype(f32)
+        last = hist[states - 1, :, where].astype(f32)
         grad_gen = contract(gin_mine, low_b, 0, 0)
         accs[11] = accs[11] + grad_gen * last * rms
         normed = (last * rms * colp[:, 0:1]).astype(bf16)
@@ -1208,7 +1181,10 @@
         value = value - last * (rms * rms * rms * gen_in_all[b, hid : hid + 1, :])
         for s in range(4):
             value = value + pk[b, pl.ds(4 * (states - 1) + s, 1), :] * gn[s, :, where]
-        hist_grad[states - 1, :, where] = value.astype(bf16)
+        hist[states - 1, :, where] = value.astype(bf16)
+
+    keep_last = pltpu.make_async_copy(hist.at[states - 1], hist_out.at[states - 1], load_sem.at[11])
+    keep_last.start()
 
     prm[...] = jnp.zeros_like(prm)
     for index in range(13):
@@ -1219,8 +1195,7 @@
             src_ref=vec, dst_ref=vec_z.at[zc], send_sem=ex_send.at[4, k], recv_sem=ex_recv.at[4, k],
             device_id={"dp": (zc + k) % zn}, device_id_type=MESH,
         ).start()
-    z_fold(11)
-    z_end(8)
+    z_step(2)
     vec_z[zc] = vec[...]
     for k in range(1, zn):
         place_z = vec_z.at[(zc + zn - k) % zn]
@@ -1238,10 +1213,7 @@
         ex_send.at[5], ex_recv.at[5],
     )
     alls.start()
-    z_fold(2)
-    z_fold(1)
-    z_end(9)
-    z_end(10)
+    z_step(2)
     for k in range(1, n):
         alls.wait(k)
     shared = vec_all[0, 56:104, :]
@@ -1268,21 +1240,21 @@
         gain_tot[:, where] = vec_all[k, 11:12, :]
         outb_tot[:, where] = vec_all[k, 12:13, :]
         gin_tot[:, where] = vec_all[k, 16 : 16 + hid, :]
-    z_fold(0)
-    z_end(11)
-    for c in (2, 1, 0):
-        z_end(c)
+    for step, c in z_actions:
+        step(c)
     for c in range(12):
         z_drain(c)
     for i in range(5):
         rs_drain(i)
-    for exchange in (turns, sums, mixes, owns, alls):
+    for g in [cots] + gathers:
+        g.drain()
+    for exchange in (parts, spread_mix, stats, turns, sums, mixes, owns, alls):
         exchange.drain()
-    for copy in stages:
+    for copy in stages + [keep_new, keep_hist, keep_last]:
         copy.wait()
 
 
-def back(n, zn, nbuf, cot_all, cols, pk, raw, scaled, st3, stat, history, gen_gain, gen_in, gen_out, norm_gain, in_bias, out_bias, w_in):
+def layer(n, zn, history, cotangent, bucket_len, valid_len, gen_gain, gen_in, gen_out, gen_bias, norm_gain, norm_bias, w_in, in_bias, w_out, w_down, out_bias):
     f32, bf16 = jnp.float32, jnp.bfloat16
     states, feats, tokens = history.shape
     block = tokens // n
@@ -1290,11 +1262,12 @@
     hid = gen_in.shape[1]
     heads = feats // HEAD_DIM
     vmem = pl.BlockSpec(memory_space=pltpu.VMEM)
+    smem = pl.BlockSpec(memory_space=pltpu.SMEM)
     anys = pl.BlockSpec(memory_space=pl.ANY)
     shape = jax.ShapeDtypeStruct
     dma = pltpu.SemaphoreType.DMA
     return pl.pallas_call(
-        functools.partial(back_kernel, n, zn),
+        functools.partial(layer_kernel, n, zn),
         out_shape=(
             shape((feats, tokens), bf16),
             shape((states, feats, tokens), bf16),
@@ -1310,12 +1283,15 @@
             shape((4, states), f32),
             shape((4, states), f32),
         ),
-        in_specs=[anys] * 5 + [vmem] * 11,
-        out_specs=(vmem, vmem, anys) + (vmem,) * 10,
+        in_specs=[anys] * 2 + [smem] * 2 + [vmem] * 8 + [anys] * 2 + [vmem],
+        out_specs=(anys,) * 3 + (vmem,) * 10,
         scratch_shapes=[
+            pltpu.VMEM((states, feats, tokens), bf16),
+            pltpu.VMEM((feats, tokens), bf16),
             pltpu.VMEM((4 * n, feats, tokens), bf16),
             pltpu.VMEM((width, tokens), bf16),
             pltpu.VMEM((width, 5 * feats), bf16),
+            pltpu.VMEM((width, 3 * feats), bf16),
             pltpu.VMEM((feats, feats), f32),
             pltpu.VMEM((feats, feats), f32),
             pltpu.VMEM((3, feats, tokens), bf16),
@@ -1325,9 +1301,18 @@
             pltpu.VMEM((feats, tokens), bf16),
             pltpu.VMEM((7 * feats, tokens), bf16),
             pltpu.VMEM((5, width, feats), bf16),
-            pltpu.VMEM((24, tokens), f32),
+            pltpu.VMEM((16, tokens), f32),
             pltpu.VMEM((13, feats, block), f32),
             pltpu.VMEM((4, feats, tokens), f32),
+            pltpu.VMEM((4, feats, tokens), f32),
+            pltpu.VMEM((feats, tokens), f32),
+            pltpu.VMEM((n, 40, block), f32),
+            pltpu.VMEM((hid + 8, block), f32),
+            pltpu.VMEM((n, hid + 8, block), f32),
+            pltpu.VMEM((n, hid + 8, block), f32),
+            pltpu.VMEM((8, tokens), f32),
+            pltpu.VMEM((n, 8, tokens), f32),
+            pltpu.VMEM((8, tokens), f32),
             pltpu.VMEM((5, width, tokens), bf16),
             pltpu.VMEM((5, 4, feats, tokens), bf16),
             pltpu.VMEM((5, 2, feats, tokens), bf16),
@@ -1346,18 +1331,82 @@
             pltpu.VMEM((zn, 104, feats), f32),
             pltpu.VMEM((104, feats), f32),
             pltpu.VMEM((n, 104, feats), f32),
-            dma((9,)), dma((5, 7)), dma((5, 7)), dma((6, n)), dma((6, n)),
+            dma((12,)), dma((5, 7)), dma((5, 7)), dma((5, 7)), dma((5, 7)), dma((10, n)), dma((10, n)),
             dma((12, 3)), dma((12, 2)), dma((12,)),
         ],
         compiler_params=pltpu.CompilerParams(
-            collective_id=2, has_side_effects=True, vmem_limit_bytes=67043328
+            collective_id=1, has_side_effects=True, vmem_limit_bytes=67043328
         ),
-        name="back",
+        name="layer",
     )(
-        nbuf, cot_all, cols, history, scaled,
-        w_in.transpose(1, 0, 2), pk, raw, st3, stat, gen_gain.reshape(1, width), gen_in.T,
-        gen_out.transpose(2, 1, 0), norm_gain, in_bias, out_bias.reshape(1, width),
-    )
+        history, cotangent, bucket_len, valid_len, gen_gain.reshape(1, width), gen_in.T,
+        gen_out.transpose(2, 1, 0), gen_bias, norm_gain, norm_bias, w_in.transpose(1, 0, 2), in_bias,
+        w_out, w_down, out_bias.reshape(1, width),
+    )
+
+
+def finish_kernel(new_in, hist_in, totals, *refs):
+    count = (len(refs) - 10) // 2
+    small_in = refs[:count]
+    new_out, hist_out, in_out, out_out, down_out = refs[count : count + 5]
+    small_out = refs[count + 5 : 2 * count + 5]
+    new_buf, hist_buf, low, full, sem_in = refs[2 * count + 5 :]
+    width = totals.shape[2]
+    states = hist_in.shape[0]
+    sources = [(new_in, new_buf)] + [(hist_in.at[j], hist_buf.at[j]) for j in range(states)]
+    sources += [(totals.at[c], low.at[c]) for c in range(12)]
+    targets = [(new_buf, new_out)] + [(hist_buf.at[j], hist_out.at[j]) for j in range(states)]
+    for c in range(12):
+        if c < 7:
+            targets.append((full.at[c], in_out.at[c]))
+        elif c == 7:
+            targets.append((full.at[c], out_out))
+        else:
+            targets.append((full.at[c], down_out.at[:, (c - 8) * width : (c - 7) * width]))
+    loads = [pltpu.make_async_copy(a, b, sem_in.at[0, i]) for i, (a, b) in enumerate(sources)]
+    stores = [pltpu.make_async_copy(a, b, sem_in.at[1, i]) for i, (a, b) in enumerate(targets)]
+    order = list(range(1 + states, 13 + states)) + list(range(1 + states))
+    for i in order:
+        loads[i].start()
+    for a, b in zip(small_in, small_out):
+        b[...] = a[...]
+    for i in order:
+        loads[i].wait()
+        if i > states:
+            c = i - 1 - states
+            full[c] = low[c].astype(jnp.float32)
+        stores[i].start()
+    for copy in stores:
+        copy.wait()
+
+
+def finish(new_state, history_grad, totals, smalls):
+    f32, bf16 = jnp.float32, jnp.bfloat16
+    feats, width = totals.shape[1:]
+    vmem = pl.BlockSpec(memory_space=pltpu.VMEM)
+    anys = pl.BlockSpec(memory_space=pl.ANY)
+    shape = jax.ShapeDtypeStruct
+    return pl.pallas_call(
+        finish_kernel,
+        out_shape=(
+            shape(new_state.shape, bf16),
+            shape(history_grad.shape, bf16),
+            shape((7, feats, width), f32),
+            shape((feats, width), f32),
+            shape((feats, 4 * width), f32),
+        ) + tuple(shape(x.shape, x.dtype) for x in smalls),
+        in_specs=[anys] * 3 + [vmem] * len(smalls),
+        out_specs=(anys,) * 5 + (vmem,) * len(smalls),
+        scratch_shapes=[
+            pltpu.VMEM(new_state.shape, bf16),
+            pltpu.VMEM(history_grad.shape, bf16),
+            pltpu.VMEM(totals.shape, bf16),
+            pltpu.VMEM(totals.shape, f32),
+            pltpu.SemaphoreType.DMA((2, 13 + history_grad.shape[0])),
+        ],
+        compiler_params=pltpu.CompilerParams(vmem_limit_bytes=40 * 2**20),
+        name="finish",
+    )(new_state, history_grad, totals, *smalls)
 
 
 def tp_device(
@@ -1365,22 +1414,18 @@
     norm_gain, norm_bias, w_in, in_bias, w_out, w_down, out_bias,
 ):
     n, zn = lax.axis_size("seq"), lax.axis_size("dp")
-    nbuf, cot_all, cols, pk, raw, scaled, st3, stat = front(
-        n, history, cotangent, bucket_len, valid_len, gen_gain, gen_in, gen_out, gen_bias,
-        norm_gain, norm_bias, w_out, w_down,
+    new_state, history_grad, totals, *smalls = layer(
+        n, zn, history, cotangent, bucket_len, valid_len, gen_gain, gen_in, gen_out, gen_bias,
+        norm_gain, norm_bias, w_in, in_bias, w_out, w_down, out_bias,
     )
     (
-        new_state, history_grad, totals, bias, ngain, nbias, gain, outb, gin, gout, gbias, mean, var,
-    ) = back(
-        n, zn, nbuf, cot_all, cols, pk, raw, scaled, st3, stat, history, gen_gain, gen_in, gen_out,
-        norm_gain, in_bias, out_bias, w_in,
-    )
-    totals = totals.astype(jnp.float32)
-    feats, width = totals.shape[1:]
+        new_state, history_grad, in_grad, out_grad, down_grad,
+        bias, ngain, nbias, gain, outb, gin, gout, gbias, mean, var,
+    ) = finish(new_state, history_grad, totals, smalls)
+    width = gen_gain.shape[0]
     return (
         new_state, history_grad, mean, var, gain.reshape(width), gin.T, gout.transpose(2, 1, 0),
-        gbias, ngain, nbias, totals[:7].transpose(1, 0, 2), bias, totals[7],
-        totals[8:].transpose(1, 0, 2).reshape(feats, 4 * width), outb.reshape(width),
+        gbias, ngain, nbias, in_grad.transpose(1, 0, 2), bias, out_grad, down_grad, outb.reshape(width),
     )
 
 

time: 257 us -> 228 us (0.89)
  Pallas kernels: 237 us -> 215 us
  local copies, waits for them, and re-layouts: 16.3 us -> 11.6 us
  other arithmetic: 2.64 us -> 0 us
    pallas_call x2, Pallas kernels: 237 us -> 215 us  [the longest x1 210 us: layer(): pl.pallas_call(functools.partial(layer_kernel, n, zn), out_shape=(shape((...]
    transpose x3 -> x0, local copies, waits for them, and re-layouts: 4.27 us -> none  [the longest x1 2.34 us: tp_device(): totals[:7].transpose(1, 0, 2)]
    convert_element_type x1 -> x0, other arithmetic: 2.64 us -> none  [tp_device(): totals = totals.astype(jnp.float32)]
    unnamed x37 -> x26, local copies, waits for them, and re-layouts: 11.2 us -> 11.6 us
where the time goes in v4:
time: 228 us; the launch traced here: 227 us
  Pallas kernels  215 us (94%)
  local copies, waits for them, and re-layouts  11.6 us (5%)
    pallas_call x1, Pallas kernels, layer(): pl.pallas_call(functools.partial(layer_kernel, n, zn), out_shape=(shape((...  210 us
    unnamed x26, local copies, waits for them, and re-layouts  11.6 us
    pallas_call x1, Pallas kernels, finish(): pl.pallas_call(finish_kernel, out_shape=(shape(new_state.shape, bf16), sh...  5.03 us

profile of v4, /device:TPU:0, one launch (start us, length us, event | category | flops | bytes accessed | tf_op | source)
XLA Modules:
  0.0 227.1 jit_solution(664791718426122818)
XLA Ops:
  0.7 209.7 %layer.1 = (bf16[128,1024]{1,0:T(8,128)(2,1)}, bf16[9,128,1024]{2,1,0:T(8,128)(2,1)}, bf16[12,128,1024]{2,1,0:T(8,128)(2,1)}, f32[7,1024]{1,0:T(8,128)}, f32[2,1...) custom-call(bf16[9,128,1024]{2,1,0:T(8,128)(2,1)} %history.1, ...), custom_call_target="tpu_custom_call" | custom-call | tf_op jit(solution)/shard_map/layer/pallas_call | solution.py:1269
  210.4 0.0 copy-start
  210.4 1.9 copy-done
  212.3 0.0 copy-start.1
  212.3 1.7 copy-done.1
  214.0 0.0 copy-start.2
  214.0 0.9 copy-done.2
  214.9 0.0 copy-start.3
  214.9 0.9 copy-done.3
  215.8 0.0 copy-start.4
  215.8 0.8 copy-done.4
  216.6 0.0 copy-start.5
  216.6 0.7 copy-done.5
  217.3 0.0 copy-start.6
  217.3 0.7 copy-done.6
  218.0 0.0 copy-start.7
  218.0 0.7 copy-done.7
  218.7 0.0 copy-start.8
  218.7 0.7 copy-done.8
  219.4 0.0 copy-start.9
  219.4 0.7 copy-done.9
  220.1 0.0 copy-start.10
  220.1 0.7 copy-done.10
  220.7 0.0 copy-start.11
  220.7 0.7 copy-done.11
  221.4 0.0 copy-start.12
  221.4 0.7 copy-done.12
  222.1 5.0 %finish.1 = (bf16[128,1024]{1,0:T(8,128)(2,1)}, bf16[9,128,1024]{2,1,0:T(8,128)(2,1)}, f32[7,128,1024]{2,1,0:T(8,128)}, f32[128,1024]{1,0:T(8,128)}, f32[128,409...) custom-call(bf16[128,1024]{1,0:T(8,128)(2,1)S(1)} %copy-done.2, ...), custom_call_target="tpu_custom_call" | custom-call | tf_op jit(solution)/shard_map/finish/pallas_call | solution.py:1389
Async XLA Ops:
  210.4 1.9 copy-start
  212.3 1.7 copy-start.1
  214.0 0.9 copy-start.2
  214.9 0.9 copy-start.3
  215.8 0.8 copy-start.4
  216.6 0.7 copy-start.5
  217.3 0.7 copy-start.6
  218.0 0.7 copy-start.7
  218.7 0.7 copy-start.8
  219.4 0.7 copy-start.9
  220.1 0.7 copy-start.10
  220.7 0.7 copy-start.11
  221.4 0.7 copy-start.12

commit v5 on v4

--- a/solution.py
+++ b/solution.py
@@ -419,19 +419,17 @@
             at.copy(place, place, self.send.at[k], self.recv.at[k], at.p).wait_send()
 
 
-COLS_EARLY = 2
-
-
 def layer_kernel(
     n, zn,
     history, cotangent, lens, vals, gain, gin, gout, gbias, ng, nb, w_in, in_bias, w_out, w_down, out_bias,
     new_out, hist_out, totals,
     bias_tot, ngain_tot, nbias_tot, gain_tot, outb_tot, gin_tot, gout_tot,
     gbias_tot, mean_tot, var_tot,
-    hist, new_state, big, cot, cols, w_turn, prm, colp, qkv, act, deriv, probs, gattn, gp, gcol, rope, accs, gn,
+    hist, new_state, big, cot, cols, w_turn, prm, colp, qkv, act, deriv, probs, gattn, gp, gcol, rope, masks, accs, gn,
     scaled, st3, pk, raw, part, part_in, stat, stat_in, stat_out,
     ybuf, abuf, from_a, from_b, zown, zin, zmid,
     gsum, gsum_in, gmix, gmix_in, pre, genmsg, gen_in_all, vec, vec_z, vec_sum, vec_all,
+    late, late_z, late_sum, late_all, gproj, gproj_in,
     load_sem, ag_send, ag_recv, rs_send, rs_recv, ex_send, ex_recv, z_send, z_recv, out_sem,
 ):
     f32, bf16 = jnp.float32, jnp.bfloat16
@@ -512,6 +510,8 @@
         )
     pl.semaphore_wait(barrier, n - 1 + zn - 1)
     parts.start()
+    load_cot.wait()
+    cots.start(cot.at[mine, :])
 
     @pl.loop(0, n)
     def _(r):
@@ -535,26 +535,49 @@
         pk[me, m + offset : m + offset + 1, :] = jnp.full((1, block), value.astype(f32))
     spread_mix.start()
 
+    share = feats // zn
+    shared_rows = pl.ds(pl.multiple_of(zc * share, share), share)
+
     def column_copy(to, j):
         if j == 0:
-            src = w_out.at[:, rows(to)]
+            src = w_out.at[shared_rows, rows(to)]
         else:
-            src = w_down.at[:, pl.ds(pl.multiple_of((j - 1) * width + to * feats, feats), feats)]
-        return src, cols.at[mine, pl.ds(j * feats, feats)]
-
-    def send_columns(which):
-        for j in which:
-            for k in range(1, n):
-                to = (me + k) % n
-                src, dst = column_copy(to, j)
-                at.copy(src, dst, ex_send.at[9, k], ex_recv.at[9, k], to).start()
-
+            src = w_down.at[
+                shared_rows, pl.ds(pl.multiple_of((j - 1) * width + to * feats, feats), feats)
+            ]
+        return src, cols.at[me, zc, :, pl.ds(j * feats, feats)]
+
+    for k in range(1, n):
+        to = (me + k) % n
+        for j in range(5):
+            src, dst = column_copy(to, j)
+            at.copy(src, dst, ex_send.at[9, k], ex_recv.at[9, k], to).start()
     own_cols = [
         pltpu.make_async_copy(*column_copy(me, j), load_sem.at[3 + j]) for j in range(5)
     ]
     for copy in own_cols:
         copy.start()
-    send_columns(range(COLS_EARLY))
+    cots.near()
+
+    def line_columns(k, owner):
+        part_cols = cols.at[:, owner]
+        return pltpu.make_async_remote_copy(
+            src_ref=part_cols, dst_ref=part_cols, send_sem=ex_send.at[10, k], recv_sem=ex_recv.at[10, k],
+            device_id={"dp": (zc + k) % zn}, device_id_type=MESH,
+        )
+
+    def share_columns():
+        for k in range(1, n):
+            arrived = cols.at[(me + n - k) % n, zc]
+            at.copy(arrived, arrived, ex_send.at[9, k], ex_recv.at[9, k], at.p).wait()
+        for copy in own_cols:
+            copy.wait()
+        for k in range(1, zn):
+            line_columns(k, zc).start()
+
+    def wait_columns():
+        for k in range(1, zn):
+            line_columns(k, (zc + zn - k) % zn).wait()
 
     def mix_block(owner):
         where = lanes(owner)
@@ -578,7 +601,13 @@
 
     mix_block(me)
 
-    @pl.loop(1, n)
+    @pl.loop(1, n // 2)
+    def _(k):
+        mix_block(spread_mix.wait(k))
+
+    share_columns()
+
+    @pl.loop(n // 2, n)
     def _(k):
         mix_block(spread_mix.wait(k))
 
@@ -597,15 +626,15 @@
         limit = jnp.where(second, pk[owner, m + 3 : m + 4, :], pk[owner, m + 2 : m + 3, :])
         return second, position, position < limit
 
-    load_cot.wait()
     for b in range(n):
         where = pl.ds(b * block, block)
         _, position, valid = place(b, spot)
         angle = freq * position
         rope[0:8, where] = jnp.cos(angle)
         rope[8:16, where] = jnp.sin(angle)
-        kept = jnp.where(valid, 1.0, 0.0)
-        cot[mine, where] = cot[mine, where] * kept.astype(bf16)
+        masks[0:1, where] = jnp.where(valid, 1.0, 0.0)
+
+    cots.far()
 
     @pl.loop(0, n)
     def _(r):
@@ -685,29 +714,341 @@
                 act[pl.ds((1 + j) * feats, feats), where] = up.astype(bf16)
                 deriv[j, :, where] = slope
 
+    def rs_copy(i, src, dst, slot, to):
+        return at.copy(src, dst, rs_send.at[i, slot], rs_recv.at[i, slot], to)
+
+    def rs_first(i):
+        return [
+            rs_copy(i, ybuf.at[i, rows(owner), :], abuf.at[i, q], q, at.p)
+            for q, owner in enumerate((at.p, at.pa, at.pb, at.pdg))
+        ]
+
+    def rs_second(i):
+        return [
+            rs_copy(i, ybuf.at[i, rows(at.a), :], from_a.at[i, 0], 4, at.a),
+            rs_copy(i, ybuf.at[i, rows(at.dg), :], from_a.at[i, 1], 5, at.a),
+        ]
+
+    def rs_third(i):
+        return [rs_copy(i, ybuf.at[i, rows(at.b), :], from_b.at[i], 6, at.b)]
+
+    def rs_start(i):
+        for copy in rs_first(i):
+            copy.start()
+
+    def rs_fold(i):
+        for copy in rs_first(i):
+            copy.wait_recv()
+
+        @pl.loop(0, chunks)
+        def _(c):
+            where = lanes(c, wide)
+            for q, owner in ((1, at.a), (3, at.dg)):
+                ybuf[i, rows(owner), where] = (
+                    ybuf[i, rows(owner), where].astype(f32) + abuf[i, q, :, where].astype(f32)
+                ).astype(bf16)
+
+        for copy in rs_second(i):
+            copy.start()
+
+    def rs_pass(i):
+        for copy in rs_second(i):
+            copy.wait_recv()
+
+        @pl.loop(0, chunks)
+        def _(c):
+            where = lanes(c, wide)
+            ybuf[i, rows(at.b), where] = (
+                ybuf[i, rows(at.b), where].astype(f32)
+                + abuf[i, 2, :, where].astype(f32)
+                + from_a[i, 1, :, where].astype(f32)
+            ).astype(bf16)
+
+        for copy in rs_third(i):
+            copy.start()
+
+    def rs_end(i):
+        for copy in rs_third(i):
+            copy.wait_recv()
+
+    def rs_value(i, where):
+        return (
+            ybuf[i, rows(me), where].astype(f32)
+            + abuf[i, 0, :, where].astype(f32)
+            + from_a[i, 0, :, where].astype(f32)
+            + from_b[i, :, where].astype(f32)
+        )
+
+    def rs_drain(i):
+        for copy in rs_first(i) + rs_second(i) + rs_third(i):
+            copy.wait_send()
+
+    outer = (zc == 0) | (zc == 3)
+    z_in = 1 + zc // 3
+    z_out = 3 * (zc - 1)
+    z_over = 3 - zc
+
+    def z_copy(c, src, dst, slot, recv_slot, to):
+        return pltpu.make_async_remote_copy(
+            src_ref=src, dst_ref=dst, send_sem=z_send.at[c, slot], recv_sem=z_recv.at[c, recv_slot],
+            device_id={"dp": to}, device_id_type=MESH,
+        )
+
+    def z_up(c):
+        return z_copy(c, zown.at[c], zin.at[c], 0, 0, z_in)
+
+    def z_cross(c):
+        return z_copy(c, zown.at[c], zmid.at[c], 1, 1, z_over)
+
+    def z_down(c):
+        return z_copy(c, zin.at[c], zin.at[c], 2, 0, z_out)
+
+    def z_start(c):
+        if zn > 1:
+
+            @pl.when(outer)
+            def _():
+                z_up(c).start()
+
+    def z_fold(c):
+        if zn > 1:
+
+            @pl.when(jnp.logical_not(outer))
+            def _():
+                z_up(c).wait_recv()
+
+                @pl.loop(0, chunks)
+                def _(k):
+                    where = lanes(k, wide)
+                    zown[c, :, where] = (
+                        zown[c, :, where].astype(f32) + zin[c, :, where].astype(f32)
+                    ).astype(bf16)
+
+                z_cross(c).start()
+
+    stages = []
+
+    def z_end(c):
+        if zn > 1:
+
+            @pl.when(jnp.logical_not(outer))
+            def _():
+                z_cross(c).wait_recv()
+
+                @pl.loop(0, chunks)
+                def _(k):
+                    where = lanes(k, wide)
+                    zin[c, :, where] = (
+                        zown[c, :, where].astype(f32) + zmid[c, :, where].astype(f32)
+                    ).astype(bf16)
+
+                z_down(c).start()
+
+            @pl.when(outer)
+            def _():
+                z_up(c).wait_recv()
+
+        source = zin if zn > 1 else zown
+        stages.append(pltpu.make_async_copy(source.at[c], totals.at[c], out_sem.at[c]))
+        stages[-1].start()
+
+    def z_drain(c):
+        if zn > 1:
+
+            @pl.when(outer)
+            def _():
+                z_up(c).wait_send()
+
+            @pl.when(jnp.logical_not(outer))
+            def _():
+                z_cross(c).wait_send()
+                z_down(c).wait_send()
+
+    z_order = (3, 4, 5, 6, 11, 10, 0, 1, 2, 9, 8, 7)
+    z_actions = []
+    for t in range(14):
+        if t < 12:
+            z_actions.append((z_fold, z_order[t]))
+        if t >= 2:
+            z_actions.append((z_end, z_order[t - 2]))
+    z_actions = iter(z_actions)
+
+    def z_step(count):
+        for _ in range(count):
+            step, c = next(z_actions)
+            step(c)
+
+
+    def turn_columns(which):
+        @pl.loop(0, n)
+        def _(r):
+            for j in which:
+                zown[j, :, lanes(r, feats)] = (
+                    cols[r, :, :, j * feats : (j + 1) * feats].reshape(feats, feats).T
+                )
+
+    def back_up(pair):
+        @pl.loop(0, chunks)
+        def _(c):
+            where = lanes(c, wide)
+            weight = zown[1 + 2 * pair : 3 + 2 * pair].reshape(2 * feats, width)
+            both = jnp.dot(weight, cot[:, where], preferred_element_type=f32)
+            for i in range(2):
+                j = 2 * pair + i
+                value = both[i * feats : (i + 1) * feats] * deriv[j, :, where]
+                accs[3 + j] = accs[3 + j] + (value[:, :block] + value[:, block:])
+                gp[pl.ds((3 + j) * feats, feats), where] = value.astype(bf16)
+
+    def out_grads(first, count):
+        for r in range(4):
+            grads = contract(
+                cot[r * quarter : (r + 1) * quarter, :],
+                act[first * feats : (first + count) * feats, :], 1, 1,
+            ).astype(bf16)
+            for j in range(count):
+                gcol[first + j, r * quarter : (r + 1) * quarter, :] = (
+                    grads[:, j * feats : (j + 1) * feats]
+                )
+
+    turns = [
+        Everyone(
+            at,
+            lambda to, j=j: gcol.at[j, rows(to), :],
+            lambda k, j=j: zown.at[7 + j, :, mine],
+            lambda k, origin, j=j: zown.at[7 + j, :, rows(origin)],
+            ex_send.at[(0, 11, 12, 13, 14)[j]], ex_recv.at[(0, 11, 12, 13, 14)[j]],
+        )
+        for j in range(5)
+    ]
+    keeps = [
+        pltpu.make_async_copy(gcol.at[j, mine, :], zown.at[7 + j, :, mine], load_sem.at[12 + j])
+        for j in range(5)
+    ]
+
+    def turn_start(j):
+        turns[j].start()
+        keeps[j].start()
+
+    def turn_end(j):
+        for k in range(1, n):
+            turns[j].wait(k)
+        keeps[j].wait()
+        z_start(7 + j)
+
+    def normed_grad(i, source, first, count):
+        @pl.loop(0, chunks)
+        def _(c):
+            where = lanes(c, wide)
+            for r in range(2):
+                half = slice(r * width // 2, (r + 1) * width // 2)
+                ybuf[i, half, where] = jnp.dot(
+                    source[half, :], gp[first * feats : (first + count) * feats, where],
+                    preferred_element_type=f32,
+                ).astype(bf16)
+
+        rs_start(i)
+
+    def weight_grad(first, count, source):
+        @pl.loop(0, 4)
+        def _(r):
+            part_in_rows = big[pl.ds(source * n + r * (n // 4), n // 4), :, :].reshape(quarter, tokens)
+            value = contract(gp[first * feats : (first + count) * feats, :], part_in_rows, 1, 1)
+            for s in range(count):
+                zown[first + s, :, lanes(r, quarter)] = value[s * feats : (s + 1) * feats].astype(bf16)
+
+        for s in range(first, first + count):
+            z_start(s)
+
+    def along_history():
+        @pl.loop(0, n)
+        def _(b):
+            where = lanes(b)
+            for j in range(states):
+                past = hist[j, :, where].astype(f32)
+                gproj[b, m + j : m + j + 1, :] = jnp.sum(past, axis=0, keepdims=True)
+                for s in range(4):
+                    gproj[b, 4 * j + s : 4 * j + s + 1, :] = jnp.sum(
+                        scaled[s, :, where] * past, axis=0, keepdims=True
+                    )
+
+    projs = Everyone(
+        at, lambda to: gproj.at[to], lambda k: gproj_in.at[k], lambda k, origin: gproj_in.at[k],
+        ex_send.at[15], ex_recv.at[15],
+    )
+
+    def norm_sums(s):
+        which = 0 if s < 3 else 1
+
+        @pl.loop(0, n)
+        def _(b):
+            where = lanes(b)
+            value = rs_value(s, where)
+            along = value * scaled[s, :, where]
+            accs[7 + which] = accs[7 + which] + along
+            accs[9 + which] = accs[9 + which] + value
+            factor = colp[:, 1 + which : 2 + which]
+            value = value * factor
+            gn[s, :, where] = value
+            gsum[s : s + 1, where] = jnp.sum(value, axis=0, keepdims=True)
+            gsum[4 + s : 5 + s, where] = jnp.sum(along * factor, axis=0, keepdims=True)
+            if s == 3:
+                direct = cot[mine, where].astype(f32)
+                accs[12] = accs[12] + direct
+                value = value + direct * (1.0 / stat_out[4 + s : 5 + s, where])
+            for j in range(states):
+                gmix[b, 4 * j + s : 4 * j + s + 1, :] = jnp.sum(
+                    value * hist[j, :, where].astype(f32), axis=0, keepdims=True
+                )
+
     normalise(3)
     normalise(0)
+    cots.other()
+    cots.drain()
+
+    @pl.loop(0, n)
+    def _(b):
+        where = lanes(b)
+        cot[:, where] = cot[:, where] * masks[0:1, where].astype(bf16)
+
     gathers[3].near()
     normalise(1)
     gathers[0].near()
     normalise(2)
+    along_history()
+    projs.start()
     gathers[3].far()
+    wait_columns()
+    turn_columns(range(5))
+
+    @pl.loop(0, chunks)
+    def _(c):
+        where = lanes(c, wide)
+        gattn[:, where] = jnp.dot(zown[0], cot[:, where], preferred_element_type=f32).astype(bf16)
+
     gathers[3].other()
     project_up(0)
-    gathers[1].near()
     gathers[0].far()
     project_up(1)
+    gathers[1].near()
+    back_up(0)
+    back_up(1)
     gathers[2].near()
-    cots.start(cot.at[mine, :])
-    send_columns(range(COLS_EARLY, 5))
+    normed_grad(3, ybuf.at[0, :, 0 : 4 * feats], 3, 4)
+    weight_grad(3, 4, 3)
+    gathers[1].far()
+    rs_fold(3)
+    out_grads(1, 4)
+    for j in (4, 3, 2, 1):
+        turn_start(j)
     gathers[0].other()
     project(0)
-    gathers[1].far()
     gathers[1].other()
     project(1)
+    z_step(1)
     gathers[2].far()
     gathers[2].other()
     project(2)
+    rs_pass(3)
 
     key_at = lax.broadcasted_iota(jnp.int32, (block, block), 0).astype(f32)
     query_at = lax.broadcasted_iota(jnp.int32, (block, block), 1).astype(f32)
@@ -737,177 +1078,6 @@
                 qkv[2, rows_h, where], soft.astype(bf16), preferred_element_type=f32
             ).astype(bf16)
 
-    def rs_copy(i, src, dst, slot, to):
-        return at.copy(src, dst, rs_send.at[i, slot], rs_recv.at[i, slot], to)
-
-    def rs_first(i):
-        return [
-            rs_copy(i, ybuf.at[i, rows(owner), :], abuf.at[i, q], q, at.p)
-            for q, owner in enumerate((at.p, at.pa, at.pb, at.pdg))
-        ]
-
-    def rs_second(i):
-        return [
-            rs_copy(i, ybuf.at[i, rows(at.a), :], from_a.at[i, 0], 4, at.a),
-            rs_copy(i, ybuf.at[i, rows(at.dg), :], from_a.at[i, 1], 5, at.a),
-        ]
-
-    def rs_third(i):
-        return [rs_copy(i, ybuf.at[i, rows(at.b), :], from_b.at[i], 6, at.b)]
-
-    def rs_start(i):
-        for copy in rs_first(i):
-            copy.start()
-
-    def rs_fold(i):
-        for copy in rs_first(i):
-            copy.wait_recv()
-
-        @pl.loop(0, chunks)
-        def _(c):
-            where = lanes(c, wide)
-            for q, owner in ((1, at.a), (3, at.dg)):
-                ybuf[i, rows(owner), where] = (
-                    ybuf[i, rows(owner), where].astype(f32) + abuf[i, q, :, where].astype(f32)
-                ).astype(bf16)
-
-        for copy in rs_second(i):
-            copy.start()
-
-    def rs_pass(i):
-        for copy in rs_second(i):
-            copy.wait_recv()
-
-        @pl.loop(0, chunks)
-        def _(c):
-            where = lanes(c, wide)
-            ybuf[i, rows(at.b), where] = (
-                ybuf[i, rows(at.b), where].astype(f32)
-                + abuf[i, 2, :, where].astype(f32)
-                + from_a[i, 1, :, where].astype(f32)
-            ).astype(bf16)
-
-        for copy in rs_third(i):
-            copy.start()
-
-    def rs_end(i):
-        for copy in rs_third(i):
-            copy.wait_recv()
-
-    def rs_value(i, where):
-        return (
-            ybuf[i, rows(me), where].astype(f32)
-            + abuf[i, 0, :, where].astype(f32)
-            + from_a[i, 0, :, where].astype(f32)
-            + from_b[i, :, where].astype(f32)
-        )
-
-    def rs_drain(i):
-        for copy in rs_first(i) + rs_second(i) + rs_third(i):
-            copy.wait_send()
-
-    outer = (zc == 0) | (zc == 3)
-    z_in = 1 + zc // 3
-    z_out = 3 * (zc - 1)
-    z_over = 3 - zc
-
-    def z_copy(c, src, dst, slot, recv_slot, to):
-        return pltpu.make_async_remote_copy(
-            src_ref=src, dst_ref=dst, send_sem=z_send.at[c, slot], recv_sem=z_recv.at[c, recv_slot],
-            device_id={"dp": to}, device_id_type=MESH,
-        )
-
-    def z_up(c):
-        return z_copy(c, zown.at[c], zin.at[c], 0, 0, z_in)
-
-    def z_cross(c):
-        return z_copy(c, zown.at[c], zmid.at[c], 1, 1, z_over)
-
-    def z_down(c):
-        return z_copy(c, zin.at[c], zin.at[c], 2, 0, z_out)
-
-    def z_start(c):
-        if zn > 1:
-
-            @pl.when(outer)
-            def _():
-                z_up(c).start()
-
-    def z_fold(c):
-        if zn > 1:
-
-            @pl.when(jnp.logical_not(outer))
-            def _():
-                z_up(c).wait_recv()
-
-                @pl.loop(0, chunks)
-                def _(k):
-                    where = lanes(k, wide)
-                    zown[c, :, where] = (
-                        zown[c, :, where].astype(f32) + zin[c, :, where].astype(f32)
-                    ).astype(bf16)
-
-                z_cross(c).start()
-
-    stages = []
-
-    def z_end(c):
-        if zn > 1:
-
-            @pl.when(jnp.logical_not(outer))
-            def _():
-                z_cross(c).wait_recv()
-
-                @pl.loop(0, chunks)
-                def _(k):
-                    where = lanes(k, wide)
-                    zin[c, :, where] = (
-                        zown[c, :, where].astype(f32) + zmid[c, :, where].astype(f32)
-                    ).astype(bf16)
-
-                z_down(c).start()
-
-            @pl.when(outer)
-            def _():
-                z_up(c).wait_recv()
-
-        source = zin if zn > 1 else zown
-        stages.append(pltpu.make_async_copy(source.at[c], totals.at[c], out_sem.at[c]))
-        stages[-1].start()
-
-    def z_drain(c):
-        if zn > 1:
-
-            @pl.when(outer)
-            def _():
-                z_up(c).wait_send()
-
-            @pl.when(jnp.logical_not(outer))
-            def _():
-                z_cross(c).wait_send()
-                z_down(c).wait_send()
-
-    z_order = (3, 4, 5, 6, 7, 8, 9, 10, 11, 0, 1, 2)
-    z_actions = []
-    for t in range(14):
-        if t < 12:
-            z_actions.append((z_fold, z_order[t]))
-        if t >= 2:
-            z_actions.append((z_end, z_order[t - 2]))
-    z_actions = iter(z_actions)
-
-    def z_step(count):
-        for _ in range(count):
-            step, c = next(z_actions)
-            step(c)
-
-
-    cots.near()
-    for k in range(1, n):
-        arrived = cols.at[rows((me + n - k) % n), :]
-        at.copy(arrived, arrived, ex_send.at[9, k], ex_recv.at[9, k], at.p).wait()
-    for copy in own_cols:
-        copy.wait()
 
     @pl.loop(0, chunks)
     def _(c):
@@ -915,78 +1085,15 @@
         for r in range(2):
             half = slice(r * width // 2, (r + 1) * width // 2)
             ybuf[4, half, where] = jnp.dot(
-                cols[half, :], act[:, where], preferred_element_type=f32
+                cols[r * n // 2 : (r + 1) * n // 2].reshape(width // 2, 5 * feats), act[:, where],
+                preferred_element_type=f32,
             ).astype(bf16)
 
     rs_start(4)
-    cots.far()
-
-    @pl.loop(0, n)
-    def _(r):
-        for j in range(5):
-            zown[j, :, lanes(r, feats)] = cols[rows(r), j * feats : (j + 1) * feats].T
-
-    cots.other()
-
-    @pl.loop(0, chunks)
-    def _(c):
-        where = lanes(c, wide)
-        gattn[:, where] = jnp.dot(zown[0], cot[:, where], preferred_element_type=f32).astype(bf16)
-        for pair in range(2):
-            weight = zown[1 + 2 * pair : 3 + 2 * pair].reshape(2 * feats, width)
-            both = jnp.dot(weight, cot[:, where], preferred_element_type=f32)
-            for i in range(2):
-                j = 2 * pair + i
-                value = both[i * feats : (i + 1) * feats] * deriv[j, :, where]
-                accs[3 + j] = accs[3 + j] + (value[:, :block] + value[:, block:])
-                gp[pl.ds((3 + j) * feats, feats), where] = value.astype(bf16)
-
-    def normed_grad(i, source, first, count):
-        @pl.loop(0, chunks)
-        def _(c):
-            where = lanes(c, wide)
-            for r in range(2):
-                half = slice(r * width // 2, (r + 1) * width // 2)
-                ybuf[i, half, where] = jnp.dot(
-                    source[half, :], gp[first * feats : (first + count) * feats, where],
-                    preferred_element_type=f32,
-                ).astype(bf16)
-
-        rs_start(i)
-
-    def weight_grad(first, count, source):
-        @pl.loop(0, 4)
-        def _(r):
-            part_in_rows = big[pl.ds(source * n + r * (n // 4), n // 4), :, :].reshape(quarter, tokens)
-            value = contract(gp[first * feats : (first + count) * feats, :], part_in_rows, 1, 1)
-            for s in range(count):
-                zown[first + s, :, lanes(r, quarter)] = value[s * feats : (s + 1) * feats].astype(bf16)
-
-        for s in range(first, first + count):
-            z_start(s)
-
+    z_step(1)
+    out_grads(0, 1)
     rs_fold(4)
-    normed_grad(3, ybuf.at[0, :, 0 : 4 * feats], 3, 4)
-    weight_grad(3, 4, 3)
-    for r in range(4):
-        grads = contract(cot[r * quarter : (r + 1) * quarter, :], act[...], 1, 1).astype(bf16)
-        for j in range(5):
-            gcol[j, r * quarter : (r + 1) * quarter, :] = grads[:, j * feats : (j + 1) * feats]
-
-    turns = Everyone(
-        at,
-        lambda to: gcol.at[:, rows(to), :],
-        lambda k: zown.at[pl.ds(7, 5), :, mine],
-        lambda k, origin: zown.at[pl.ds(7, 5), :, rows(origin)],
-        ex_send.at[0], ex_recv.at[0],
-    )
-    turns.start()
-    keep = pltpu.make_async_copy(
-        gcol.at[:, mine, :], zown.at[pl.ds(7, 5), :, mine], load_sem.at[8]
-    )
-    keep.start()
-    rs_pass(4)
-    rs_fold(3)
+    turn_start(0)
 
     @pl.loop(0, n // 2)
     def _(pair):
@@ -1023,20 +1130,25 @@
                 accs[s] = accs[s] + value
                 gp[pl.ds(s * feats, feats), where] = value.astype(bf16)
 
-    for s in range(3):
-        normed_grad(s, w_turn.at[:, s * feats : (s + 1) * feats], s, 1)
-    rs_pass(3)
-    z_step(1)
+    turn_end(4)
+    z_step(2)
+    normed_grad(0, w_turn.at[:, 0:feats], 0, 1)
+    normed_grad(1, w_turn.at[:, feats : 2 * feats], 1, 1)
     rs_fold(0)
-    for k in range(1, n):
-        turns.wait(k)
-    keep.wait()
-    for c in range(7, 12):
-        z_start(c)
+    normed_grad(2, w_turn.at[:, 2 * feats : 3 * feats], 2, 1)
+    rs_pass(4)
+    rs_fold(1)
+    turn_end(3)
     for s in range(3):
         weight_grad(s, 1, s)
+    rs_fold(2)
     z_step(2)
-    rs_fold(1)
+    turn_end(2)
+    rs_end(3)
+    norm_sums(3)
+    z_step(2)
+    rs_pass(0)
+    turn_end(1)
     rs_end(4)
 
     @pl.loop(0, n)
@@ -1046,44 +1158,28 @@
 
     keep_new = pltpu.make_async_copy(new_state, new_out, load_sem.at[9])
     keep_new.start()
-    z_step(1)
-    rs_pass(0)
-    rs_fold(2)
     z_step(2)
-
-    def norm_sums(s):
-        which = 0 if s < 3 else 1
-
-        @pl.loop(0, n)
-        def _(b):
-            where = lanes(b)
-            value = rs_value(s, where)
-            xhat = scaled[s, :, where]
-            along = value * xhat
-            accs[7 + which] = accs[7 + which] + along
-            accs[9 + which] = accs[9 + which] + value
-            factor = colp[:, 1 + which : 2 + which]
-            gn[s, :, where] = value * factor
-            gsum[s : s + 1, where] = jnp.sum(value * factor, axis=0, keepdims=True)
-            gsum[4 + s : 5 + s, where] = jnp.sum(along * factor, axis=0, keepdims=True)
-
-    rs_end(3)
-    norm_sums(3)
     rs_pass(1)
-    z_step(1)
+    turn_end(0)
     rs_end(0)
     norm_sums(0)
+    z_step(2)
     rs_pass(2)
-    z_step(2)
     rs_end(1)
     norm_sums(1)
+    z_step(2)
     rs_end(2)
     norm_sums(2)
     sums = Everyone(
         at, lambda to: gsum, lambda k: gsum_in.at[me], lambda k, origin: gsum_in.at[origin],
         ex_send.at[1], ex_recv.at[1],
     )
+    mixes = Everyone(
+        at, lambda to: gmix.at[to], lambda k: gmix_in.at[k], lambda k, origin: gmix_in.at[k],
+        ex_send.at[2], ex_recv.at[2],
+    )
     sums.start()
+    mixes.start()
     z_step(2)
     for k in range(1, n):
         sums.wait(k)
@@ -1093,52 +1189,42 @@
         total = total + gsum_in[k]
     pre[0:8, :] = total * (1.0 / width)
 
-    @pl.loop(0, n)
-    def _(b):
+    def stream_block(b):
         where = lanes(b)
         for s in range(4):
-            xhat = scaled[s, :, where]
             value = stat_out[4 + s : 5 + s, where] * (
-                gn[s, :, where] - pre[s : s + 1, where] - xhat * pre[4 + s : 5 + s, where]
+                gn[s, :, where] - pre[s : s + 1, where] - scaled[s, :, where] * pre[4 + s : 5 + s, where]
             )
             if s == 3:
-                direct = cot[mine, where].astype(f32)
-                accs[12] = accs[12] + direct
-                value = value + direct
+                value = value + cot[mine, where].astype(f32)
             gn[s, :, where] = value
-        for j in range(states):
-            past = hist[j, :, where].astype(f32)
-            for s in range(4):
-                gmix[b, 4 * j + s : 4 * j + s + 1, :] = jnp.sum(
-                    gn[s, :, where] * past, axis=0, keepdims=True
-                )
-
-    mixes = Everyone(
-        at, lambda to: gmix.at[to], lambda k: gmix_in.at[k], lambda k, origin: gmix_in.at[k],
-        ex_send.at[2], ex_recv.at[2],
-    )
-    mixes.start()
-    z_step(2)
-
-    @pl.loop(0, n)
-    def _(b):
-        where = lanes(b)
         for j in range(states - 1):
             value = pk[b, pl.ds(4 * j, 1), :] * gn[0, :, where]
             for s in range(1, 4):
                 value = value + pk[b, pl.ds(4 * j + s, 1), :] * gn[s, :, where]
             hist[j, :, where] = value.astype(bf16)
 
-    keep_hist = pltpu.make_async_copy(
-        hist.at[pl.ds(0, states - 1)], hist_out.at[pl.ds(0, states - 1)], load_sem.at[10]
-    )
-    keep_hist.start()
+    pl.loop(0, n // 2)(stream_block)
 
     total = gmix[me]
     for k in range(1, n):
         mixes.wait(k)
         total = total + gmix_in[k]
-    grad_mix = total[0:m]
+    fixed = gproj[me]
+    for k in range(1, n):
+        projs.wait(k)
+        fixed = fixed + gproj_in[k]
+    own = lanes(me)
+
+    def each_state(value):
+        return jnp.concatenate([value] * states, axis=0)
+
+    history_sum = jnp.concatenate(
+        [jnp.broadcast_to(fixed[m + j : m + j + 1], (4, block)) for j in range(states)], axis=0
+    )
+    grad_mix = each_state(stat_out[4:8, own]) * (
+        total[0:m] - each_state(pre[0:4, own]) * history_sum - each_state(pre[4:8, own]) * fixed[0:m]
+    )
     table = jnp.concatenate([gout[j] for j in range(states)], axis=0)
     hidden, slope = gelu_pair(raw[0:hid, :] * pk[me, m : m + 1, :])
     grad_hidden = contract(table, grad_mix, 0, 0, precision=highest)
@@ -1158,14 +1244,53 @@
     ones = jnp.ones((8, block), f32)
     mixing = pk[me, 0:m, :]
     vec[...] = jnp.zeros_like(vec)
-    vec[56 : 56 + hid, 0:m] = contract(hidden, grad_mix, 1, 1, precision=highest)
+    vec[16 : 16 + hid, 0:m] = contract(hidden, grad_mix, 1, 1, precision=highest)
     for index, value in enumerate((grad_mix, mixing * kept, mixing * mixing * kept)):
-        vec[96 + index : 97 + index, 0:m] = contract(ones, value, 1, 1, precision=highest)[0:1]
-    vec[99:100, :] = jnp.broadcast_to(jnp.sum(kept, axis=1, keepdims=True), (1, block))
+        vec[56 + index : 57 + index, 0:m] = contract(ones, value, 1, 1, precision=highest)[0:1]
+    vec[59:60, :] = jnp.broadcast_to(jnp.sum(kept, axis=1, keepdims=True), (1, block))
+    prm[...] = jnp.zeros_like(prm)
+    for index in range(13):
+        prm[:, index : index + 1] = jnp.sum(accs[index], axis=1, keepdims=True)
+    vec[0:16, :] = prm[...].T[0:16]
+
+    def line(ref, landing, row, k, owner):
+        return pltpu.make_async_remote_copy(
+            src_ref=ref, dst_ref=landing.at[owner], send_sem=ex_send.at[row, k], recv_sem=ex_recv.at[row, k],
+            device_id={"dp": (zc + k) % zn}, device_id_type=MESH,
+        )
+
+    def line_start(ref, landing, row):
+        for k in range(1, zn):
+            line(ref, landing, row, k, zc).start()
+
+    def line_total(ref, landing, row):
+        landing[zc] = ref[...]
+        for k in range(1, zn):
+            line(ref, landing, row, k, (zc + zn - k) % zn).wait()
+        value = landing[0]
+        for k in range(1, zn):
+            value = value + landing[k]
+        return value
+
+    line_start(vec, vec_z, 4)
+    pl.loop(n // 2, n)(stream_block)
+    keep_hist = pltpu.make_async_copy(
+        hist.at[pl.ds(0, states - 1)], hist_out.at[pl.ds(0, states - 1)], load_sem.at[10]
+    )
+    keep_hist.start()
+    alls = Everyone(
+        at, lambda to: vec_sum, lambda k: vec_all.at[me], lambda k, origin: vec_all.at[origin],
+        ex_send.at[5], ex_recv.at[5],
+    )
+    total = line_total(vec, vec_z, 4)
+    vec_sum[...] = total
+    vec_all[me] = total
+    alls.start()
     gen_in_all[me] = genmsg[...]
     for k in range(1, n):
         owns.wait(k)
     gin_mine = gin[:, rows(me)]
+    late[...] = jnp.zeros_like(late)
 
     @pl.loop(0, n)
     def _(b):
@@ -1176,7 +1301,7 @@
         grad_gen = contract(gin_mine, low_b, 0, 0)
         accs[11] = accs[11] + grad_gen * last * rms
         normed = (last * rms * colp[:, 0:1]).astype(bf16)
-        vec[16 : 16 + hid, :] = vec[16 : 16 + hid, :] + contract(low_b, normed, 1, 1)
+        late[0:hid, :] = late[0:hid, :] + contract(low_b, normed, 1, 1)
         value = rms * grad_gen * colp[:, 0:1]
         value = value - last * (rms * rms * rms * gen_in_all[b, hid : hid + 1, :])
         for s in range(4):
@@ -1186,39 +1311,23 @@
     keep_last = pltpu.make_async_copy(hist.at[states - 1], hist_out.at[states - 1], load_sem.at[11])
     keep_last.start()
 
-    prm[...] = jnp.zeros_like(prm)
-    for index in range(13):
-        prm[:, index : index + 1] = jnp.sum(accs[index], axis=1, keepdims=True)
-    vec[0:16, :] = prm[...].T[0:16]
-    for k in range(1, zn):
-        pltpu.make_async_remote_copy(
-            src_ref=vec, dst_ref=vec_z.at[zc], send_sem=ex_send.at[4, k], recv_sem=ex_recv.at[4, k],
-            device_id={"dp": (zc + k) % zn}, device_id_type=MESH,
-        ).start()
+    prm[:, 0:1] = jnp.sum(accs[11], axis=1, keepdims=True)
+    late[hid : hid + 8, :] = prm[...].T[0:8]
+    line_start(late, late_z, 16)
     z_step(2)
-    vec_z[zc] = vec[...]
-    for k in range(1, zn):
-        place_z = vec_z.at[(zc + zn - k) % zn]
-        pltpu.make_async_remote_copy(
-            src_ref=place_z, dst_ref=place_z, send_sem=ex_send.at[4, k], recv_sem=ex_recv.at[4, k],
-            device_id={"dp": (zc + k) % zn}, device_id_type=MESH,
-        ).wait()
-    total = vec_z[0]
-    for k in range(1, zn):
-        total = total + vec_z[k]
-    vec_sum[...] = total
-    vec_all[me] = total
-    alls = Everyone(
-        at, lambda to: vec_sum, lambda k: vec_all.at[me], lambda k, origin: vec_all.at[origin],
-        ex_send.at[5], ex_recv.at[5],
-    )
-    alls.start()
-    z_step(2)
+    lates = Everyone(
+        at, lambda to: late_sum, lambda k: late_all.at[me], lambda k, origin: late_all.at[origin],
+        ex_send.at[17], ex_recv.at[17],
+    )
+    total = line_total(late, late_z, 16)
+    late_sum[...] = total
+    late_all[me] = total
+    lates.start()
     for k in range(1, n):
         alls.wait(k)
-    shared = vec_all[0, 56:104, :]
+    shared = vec_all[0, 16:64, :]
     for k in range(1, n):
-        shared = shared + vec_all[k, 56:104, :]
+        shared = shared + vec_all[k, 16:64, :]
     prm[...] = jnp.zeros_like(prm)
     prm[0:40, :] = shared[0:40]
     count = shared[43:44, 0:1]
@@ -1232,23 +1341,26 @@
         gbias_tot[:, j : j + 1] = turned[4 * j : 4 * j + 4, 40:41]
         mean_tot[:, j : j + 1] = turned[4 * j : 4 * j + 4, 41:42]
         var_tot[:, j : j + 1] = turned[4 * j : 4 * j + 4, 42:43]
+    z_step(1)
+    for k in range(1, n):
+        lates.wait(k)
     for k in range(n):
         where = pl.ds(k * feats, feats)
         bias_tot[:, where] = vec_all[k, 0:7, :]
         ngain_tot[:, where] = vec_all[k, 7:9, :]
         nbias_tot[:, where] = vec_all[k, 9:11, :]
-        gain_tot[:, where] = vec_all[k, 11:12, :]
         outb_tot[:, where] = vec_all[k, 12:13, :]
-        gin_tot[:, where] = vec_all[k, 16 : 16 + hid, :]
+        gain_tot[:, where] = late_all[k, hid : hid + 1, :]
+        gin_tot[:, where] = late_all[k, 0:hid, :]
     for step, c in z_actions:
         step(c)
     for c in range(12):
         z_drain(c)
     for i in range(5):
         rs_drain(i)
-    for g in [cots] + gathers:
+    for g in gathers:
         g.drain()
-    for exchange in (parts, spread_mix, stats, turns, sums, mixes, owns, alls):
+    for exchange in [parts, spread_mix, stats, projs, sums, mixes, owns, alls, lates] + turns:
         exchange.drain()
     for copy in stages + [keep_new, keep_hist, keep_last]:
         copy.wait()
@@ -1290,7 +1402,7 @@
             pltpu.VMEM((feats, tokens), bf16),
             pltpu.VMEM((4 * n, feats, tokens), bf16),
             pltpu.VMEM((width, tokens), bf16),
-            pltpu.VMEM((width, 5 * feats), bf16),
+            pltpu.VMEM((n, zn, feats // zn, 5 * feats), bf16),
             pltpu.VMEM((width, 3 * feats), bf16),
             pltpu.VMEM((feats, feats), f32),
             pltpu.VMEM((feats, feats), f32),
@@ -1302,6 +1414,7 @@
             pltpu.VMEM((7 * feats, tokens), bf16),
             pltpu.VMEM((5, width, feats), bf16),
             pltpu.VMEM((16, tokens), f32),
+            pltpu.VMEM((8, tokens), f32),
             pltpu.VMEM((13, feats, block), f32),
             pltpu.VMEM((4, feats, tokens), f32),
             pltpu.VMEM((4, feats, tokens), f32),
@@ -1327,11 +1440,17 @@
             pltpu.VMEM((8, tokens), f32),
             pltpu.VMEM((hid + 8, block), f32),
             pltpu.VMEM((n, hid + 8, block), f32),
-            pltpu.VMEM((104, feats), f32),
-            pltpu.VMEM((zn, 104, feats), f32),
-            pltpu.VMEM((104, feats), f32),
-            pltpu.VMEM((n, 104, feats), f32),
-            dma((12,)), dma((5, 7)), dma((5, 7)), dma((5, 7)), dma((5, 7)), dma((10, n)), dma((10, n)),
+            pltpu.VMEM((64, feats), f32),
+            pltpu.VMEM((zn, 64, feats), f32),
+            pltpu.VMEM((64, feats), f32),
+            pltpu.VMEM((n, 64, feats), f32),
+            pltpu.VMEM((hid + 8, feats), f32),
+            pltpu.VMEM((zn, hid + 8, feats), f32),
+            pltpu.VMEM((hid + 8, feats), f32),
+            pltpu.VMEM((n, hid + 8, feats), f32),
+            pltpu.VMEM((n, 48, block), f32),
+            pltpu.VMEM((n, 48, block), f32),
+            dma((17,)), dma((5, 7)), dma((5, 7)), dma((5, 7)), dma((5, 7)), dma((18, n)), dma((18, n)),
             dma((12, 3)), dma((12, 2)), dma((12,)),
         ],
         compiler_params=pltpu.CompilerParams(
@@ -1404,7 +1523,7 @@
             pltpu.VMEM(totals.shape, f32),
             pltpu.SemaphoreType.DMA((2, 13 + history_grad.shape[0])),
         ],
-        compiler_params=pltpu.CompilerParams(vmem_limit_bytes=40 * 2**20),
+        compiler_params=pltpu.CompilerParams(vmem_limit_bytes=67043328),
         name="finish",
     )(new_state, history_grad, totals, *smalls)
 

time: 228 us -> 194 us (0.85)
  Pallas kernels: 215 us -> 193 us
  local copies, waits for them, and re-layouts: 11.6 us -> 0 us
    pallas_call x1, Pallas kernels: 210 us -> 186 us  [layer(): pl.pallas_call(functools.partial(layer_kernel, n, zn), out_shape=(shape((...]
    unnamed x26 -> x0, local copies, waits for them, and re-layouts: 11.6 us -> none
where the time goes in v5:
time: 194 us
  Pallas kernels  193 us (99%)
    pallas_call x1, Pallas kernels, layer(): pl.pallas_call(functools.partial(layer_kernel, n, zn), out_shape=(shape((...  186 us
    pallas_call x1, Pallas kernels, finish(): pl.pallas_call(finish_kernel, out_shape=(shape(new_state.shape, bf16), sh...  7.16 us

profile of v5, /device:TPU:0, one launch (start us, length us, event | category | flops | bytes accessed | tf_op | source)
XLA Modules:
  0.0 193.9 jit_solution(5692760836432933377)
XLA Ops:
  0.7 185.9 %layer.1 = (bf16[128,1024]{1,0:T(8,128)(2,1)}, bf16[9,128,1024]{2,1,0:T(8,128)(2,1)}, bf16[12,128,1024]{2,1,0:T(8,128)(2,1)}, f32[7,1024]{1,0:T(8,128)}, f32[2,1...) custom-call(bf16[9,128,1024]{2,1,0:T(8,128)(2,1)} %history.1, ...), custom_call_target="tpu_custom_call" | custom-call | tf_op jit(solution)/shard_map/layer/pallas_call | solution.py:1381
  186.6 7.2 %finish.1 = (bf16[128,1024]{1,0:T(8,128)(2,1)}, bf16[9,128,1024]{2,1,0:T(8,128)(2,1)}, f32[7,128,1024]{2,1,0:T(8,128)}, f32[128,1024]{1,0:T(8,128)}, f32[128,409...) custom-call(bf16[128,1024]{1,0:T(8,128)(2,1)} %get-tuple-element.43., ...), custom_call_target="tpu_custom_call" | custom-call | tf_op jit(solution)/shard_map/finish/pallas_call | solution.py:1508

commit v6 on v5

--- a/solution.py
+++ b/solution.py
@@ -1092,7 +1092,6 @@
     rs_start(4)
     z_step(1)
     out_grads(0, 1)
-    rs_fold(4)
     turn_start(0)
 
     @pl.loop(0, n // 2)
@@ -1136,38 +1135,30 @@
     normed_grad(1, w_turn.at[:, feats : 2 * feats], 1, 1)
     rs_fold(0)
     normed_grad(2, w_turn.at[:, 2 * feats : 3 * feats], 2, 1)
-    rs_pass(4)
     rs_fold(1)
     turn_end(3)
     for s in range(3):
         weight_grad(s, 1, s)
     rs_fold(2)
+    rs_fold(4)
     z_step(2)
     turn_end(2)
     rs_end(3)
     norm_sums(3)
-    z_step(2)
+    z_step(3)
     rs_pass(0)
     turn_end(1)
-    rs_end(4)
-
-    @pl.loop(0, n)
-    def _(b):
-        where = lanes(b)
-        new_state[:, where] = (st3[:, where] + rs_value(4, where) + colp[:, 5:6]).astype(bf16)
-
-    keep_new = pltpu.make_async_copy(new_state, new_out, load_sem.at[9])
-    keep_new.start()
-    z_step(2)
+    z_step(3)
     rs_pass(1)
     turn_end(0)
     rs_end(0)
     norm_sums(0)
-    z_step(2)
+    z_step(3)
     rs_pass(2)
+    rs_pass(4)
     rs_end(1)
     norm_sums(1)
-    z_step(2)
+    z_step(3)
     rs_end(2)
     norm_sums(2)
     sums = Everyone(
@@ -1180,6 +1171,15 @@
     )
     sums.start()
     mixes.start()
+    rs_end(4)
+
+    @pl.loop(0, n)
+    def _(b):
+        where = lanes(b)
+        new_state[:, where] = (st3[:, where] + rs_value(4, where) + colp[:, 5:6]).astype(bf16)
+
+    keep_new = pltpu.make_async_copy(new_state, new_out, load_sem.at[9])
+    keep_new.start()
     z_step(2)
     for k in range(1, n):
         sums.wait(k)
@@ -1314,7 +1314,7 @@
     prm[:, 0:1] = jnp.sum(accs[11], axis=1, keepdims=True)
     late[hid : hid + 8, :] = prm[...].T[0:8]
     line_start(late, late_z, 16)
-    z_step(2)
+    z_step(1)
     lates = Everyone(
         at, lambda to: late_sum, lambda k: late_all.at[me], lambda k, origin: late_all.at[origin],
         ex_send.at[17], ex_recv.at[17],

time: 194 us -> 187 us (0.964)
  Pallas kernels: 193 us -> 186 us
    pallas_call x1, Pallas kernels: 186 us -> 179 us  [layer(): pl.pallas_call(functools.partial(layer_kernel, n, zn), out_shape=(shape((...]
where the time goes in v6:
time: 187 us
  Pallas kernels  186 us (99%)
    pallas_call x1, Pallas kernels, layer(): pl.pallas_call(functools.partial(layer_kernel, n, zn), out_shape=(shape((...  179 us
    pallas_call x1, Pallas kernels, finish(): pl.pallas_call(finish_kernel, out_shape=(shape(new_state.shape, bf16), sh...  7.16 us

profile of v6, /device:TPU:0, one launch (start us, length us, event | category | flops | bytes accessed | tf_op | source)
XLA Modules:
  0.0 186.7 jit_solution(3179217281996260507)
XLA Ops:
  0.7 178.7 %layer.1 = (bf16[128,1024]{1,0:T(8,128)(2,1)}, bf16[9,128,1024]{2,1,0:T(8,128)(2,1)}, bf16[12,128,1024]{2,1,0:T(8,128)(2,1)}, f32[7,1024]{1,0:T(8,128)}, f32[2,1...) custom-call(bf16[9,128,1024]{2,1,0:T(8,128)(2,1)} %history.1, ...), custom_call_target="tpu_custom_call" | custom-call | tf_op jit(solution)/shard_map/layer/pallas_call | solution.py:1381
  179.3 7.2 %finish.1 = (bf16[128,1024]{1,0:T(8,128)(2,1)}, bf16[9,128,1024]{2,1,0:T(8,128)(2,1)}, f32[7,128,1024]{2,1,0:T(8,128)}, f32[128,1024]{1,0:T(8,128)}, f32[128,409...) custom-call(bf16[128,1024]{1,0:T(8,128)(2,1)} %get-tuple-element.43., ...), custom_call_target="tpu_custom_call" | custom-call | tf_op jit(solution)/shard_map/finish/pallas_call | solution.py:1508

commit v7 on v6

--- a/solution.py
+++ b/solution.py
@@ -421,11 +421,11 @@
 
 def layer_kernel(
     n, zn,
-    history, cotangent, lens, vals, gain, gin, gout, gbias, ng, nb, w_in, in_bias, w_out, w_down, out_bias,
+    history, cotangent, lens, vals, gain, gin, gout, gbias, ng, nb, w_all, in_bias, w_out, w_down, out_bias,
     new_out, hist_out, totals,
     bias_tot, ngain_tot, nbias_tot, gain_tot, outb_tot, gin_tot, gout_tot,
     gbias_tot, mean_tot, var_tot,
-    hist, new_state, big, cot, cols, w_turn, prm, colp, qkv, act, deriv, probs, gattn, gp, gcol, rope, masks, accs, gn,
+    w_in, hist, new_state, big, cot, cols, w_turn, prm, colp, qkv, act, deriv, probs, gattn, gp, gcol, rope, masks, accs, gn,
     scaled, st3, pk, raw, part, part_in, stat, stat_in, stat_out,
     ybuf, abuf, from_a, from_b, zown, zin, zmid,
     gsum, gsum_in, gmix, gmix_in, pre, genmsg, gen_in_all, vec, vec_z, vec_sum, vec_all,
@@ -460,7 +460,8 @@
         history.at[pl.ds(0, states - 1)], hist.at[pl.ds(0, states - 1)], load_sem.at[1]
     )
     load_cot = pltpu.make_async_copy(cotangent, cot.at[mine, :], load_sem.at[2])
-    for copy in (load_last, load_hist, load_cot):
+    load_w = pltpu.make_async_copy(w_all, w_in, load_sem.at[17])
+    for copy in (load_last, load_cot, load_hist, load_w):
         copy.start()
     barrier = pltpu.get_barrier_semaphore()
     for k in range(1, n):
@@ -512,6 +513,7 @@
     parts.start()
     load_cot.wait()
     cots.start(cot.at[mine, :])
+    load_w.wait()
 
     @pl.loop(0, n)
     def _(r):
@@ -1129,14 +1131,14 @@
                 accs[s] = accs[s] + value
                 gp[pl.ds(s * feats, feats), where] = value.astype(bf16)
 
-    turn_end(4)
-    z_step(2)
     normed_grad(0, w_turn.at[:, 0:feats], 0, 1)
     normed_grad(1, w_turn.at[:, feats : 2 * feats], 1, 1)
     rs_fold(0)
     normed_grad(2, w_turn.at[:, 2 * feats : 3 * feats], 2, 1)
     rs_fold(1)
+    turn_end(4)
     turn_end(3)
+    z_step(2)
     for s in range(3):
         weight_grad(s, 1, s)
     rs_fold(2)
@@ -1395,9 +1397,10 @@
             shape((4, states), f32),
             shape((4, states), f32),
         ),
-        in_specs=[anys] * 2 + [smem] * 2 + [vmem] * 8 + [anys] * 2 + [vmem],
+        in_specs=[anys] * 2 + [smem] * 2 + [vmem] * 6 + [anys, vmem] + [anys] * 2 + [vmem],
         out_specs=(anys,) * 3 + (vmem,) * 10,
         scratch_shapes=[
+            pltpu.VMEM((7, feats, width), bf16),
             pltpu.VMEM((states, feats, tokens), bf16),
             pltpu.VMEM((feats, tokens), bf16),
             pltpu.VMEM((4 * n, feats, tokens), bf16),
@@ -1450,7 +1453,7 @@
             pltpu.VMEM((n, hid + 8, feats), f32),
             pltpu.VMEM((n, 48, block), f32),
             pltpu.VMEM((n, 48, block), f32),
-            dma((17,)), dma((5, 7)), dma((5, 7)), dma((5, 7)), dma((5, 7)), dma((18, n)), dma((18, n)),
+            dma((18,)), dma((5, 7)), dma((5, 7)), dma((5, 7)), dma((5, 7)), dma((18, n)), dma((18, n)),
             dma((12, 3)), dma((12, 2)), dma((12,)),
         ],
         compiler_params=pltpu.CompilerParams(
@@ -1465,11 +1468,12 @@
 
 
 def finish_kernel(new_in, hist_in, totals, *refs):
-    count = (len(refs) - 10) // 2
+    count = (len(refs) - 10) // 3
     small_in = refs[:count]
     new_out, hist_out, in_out, out_out, down_out = refs[count : count + 5]
     small_out = refs[count + 5 : 2 * count + 5]
-    new_buf, hist_buf, low, full, sem_in = refs[2 * count + 5 :]
+    small_buf = refs[2 * count + 5 : 3 * count + 5]
+    new_buf, hist_buf, low, full, sem_in = refs[3 * count + 5 :]
     width = totals.shape[2]
     states = hist_in.shape[0]
     sources = [(new_in, new_buf)] + [(hist_in.at[j], hist_buf.at[j]) for j in range(states)]
@@ -1482,16 +1486,17 @@
             targets.append((full.at[c], out_out))
         else:
             targets.append((full.at[c], down_out.at[:, (c - 8) * width : (c - 7) * width]))
+    sources += list(zip(small_in, small_buf))
+    targets += list(zip(small_buf, small_out))
     loads = [pltpu.make_async_copy(a, b, sem_in.at[0, i]) for i, (a, b) in enumerate(sources)]
     stores = [pltpu.make_async_copy(a, b, sem_in.at[1, i]) for i, (a, b) in enumerate(targets)]
     order = list(range(1 + states, 13 + states)) + list(range(1 + states))
+    order += list(range(13 + states, len(sources)))
     for i in order:
         loads[i].start()
-    for a, b in zip(small_in, small_out):
-        b[...] = a[...]
     for i in order:
         loads[i].wait()
-        if i > states:
+        if states < i < 13 + states:
             c = i - 1 - states
             full[c] = low[c].astype(jnp.float32)
         stores[i].start()
@@ -1502,7 +1507,6 @@
 def finish(new_state, history_grad, totals, smalls):
     f32, bf16 = jnp.float32, jnp.bfloat16
     feats, width = totals.shape[1:]
-    vmem = pl.BlockSpec(memory_space=pltpu.VMEM)
     anys = pl.BlockSpec(memory_space=pl.ANY)
     shape = jax.ShapeDtypeStruct
     return pl.pallas_call(
@@ -1514,14 +1518,14 @@
             shape((feats, width), f32),
             shape((feats, 4 * width), f32),
         ) + tuple(shape(x.shape, x.dtype) for x in smalls),
-        in_specs=[anys] * 3 + [vmem] * len(smalls),
-        out_specs=(anys,) * 5 + (vmem,) * len(smalls),
-        scratch_shapes=[
+        in_specs=[anys] * (3 + len(smalls)),
+        out_specs=(anys,) * (5 + len(smalls)),
+        scratch_shapes=[pltpu.VMEM(x.shape, x.dtype) for x in smalls] + [
             pltpu.VMEM(new_state.shape, bf16),
             pltpu.VMEM(history_grad.shape, bf16),
             pltpu.VMEM(totals.shape, bf16),
             pltpu.VMEM(totals.shape, f32),
-            pltpu.SemaphoreType.DMA((2, 13 + history_grad.shape[0])),
+            pltpu.SemaphoreType.DMA((2, 13 + history_grad.shape[0] + len(smalls))),
         ],
         compiler_params=pltpu.CompilerParams(vmem_limit_bytes=67043328),
         name="finish",

time: 187 us -> 183 us (0.979)
  Pallas kernels: 186 us -> 182 us
    pallas_call x1, Pallas kernels: 179 us -> 176 us  [layer(): pl.pallas_call(functools.partial(layer_kernel, n, zn), out_shape=(shape((...]
where the time goes in v7:
time: 183 us
  Pallas kernels  182 us (99%)
    pallas_call x1, Pallas kernels, layer(): pl.pallas_call(functools.partial(layer_kernel, n, zn), out_shape=(shape((...  176 us
    pallas_call x1, Pallas kernels, finish(): pl.pallas_call(finish_kernel, out_shape=(shape(new_state.shape, bf16), sh...  5.88 us

profile of v7, /device:TPU:0, one launch (start us, length us, event | category | flops | bytes accessed | tf_op | source)
XLA Modules:
  0.0 183.1 jit_solution(1272165724305145693)
XLA Ops:
  0.7 176.4 %layer.1 = (bf16[128,1024]{1,0:T(8,128)(2,1)}, bf16[9,128,1024]{2,1,0:T(8,128)(2,1)}, bf16[12,128,1024]{2,1,0:T(8,128)(2,1)}, f32[7,1024]{1,0:T(8,128)}, f32[2,1...) custom-call(bf16[9,128,1024]{2,1,0:T(8,128)(2,1)} %history.1, ...), custom_call_target="tpu_custom_call" | custom-call | tf_op jit(solution)/shard_map/layer/pallas_call | solution.py:1383
  177.1 5.9 %finish.1 = (bf16[128,1024]{1,0:T(8,128)(2,1)}, bf16[9,128,1024]{2,1,0:T(8,128)(2,1)}, f32[7,128,1024]{2,1,0:T(8,128)}, f32[128,1024]{1,0:T(8,128)}, f32[128,409...) custom-call(bf16[128,1024]{1,0:T(8,128)(2,1)} %get-tuple-element.43., ...), custom_call_target="tpu_custom_call" | custom-call | tf_op jit(solution)/shard_map/finish/pallas_call | solution.py:1512
